TPU v7x, 128 devices: a whole 4x4x4 slice. The times are simulated.
128 devices in a mesh: mp: 2 (over core), gx: 8 (over z, y_hi), gy: 8 (over y_lo, x).
Axes of the slice: x: 4, y: 4 (y_hi: 2, y_lo: 2; y = y_hi * 2 + y_lo), z: 4, core: 2. Of those that a mesh axis runs over, the one named last changes fastest.
Arguments:
- states: float32 [2, 64, 1024, 1024], P('mp', None, 'gx', 'gy'), may hold values from -6 to 6
- surface: float32 [2, 8, 1024, 1024], P('mp', None, 'gx', 'gy'), may hold values from -6 to 6
- land_mask: int32 [1024, 1024], P('gx', 'gy'), may hold values 0 or 1
- tile_weights: bfloat16 [2, 8, 8, 256, 128, 128], P('mp', 'gx', 'gy'), may hold values from -0.5 to 0.5
- tile_source: int32 [2, 8, 8, 256], P('mp', 'gx', 'gy'), may hold values from 0 to 127
- tile_target: int32 [2, 8, 8, 256, 1], P('mp', 'gx', 'gy'), may hold values from 0 to 63; in each aligned block of 256 rows (0 to 255, 256 to 511, ..., all dimensions but the last counted through in order) at most 8 rows name the same one
- tile_row: int32 [2, 8, 8, 256], P('mp', 'gx', 'gy'), may hold values from 0 to 127
Outputs:
- new_states: float32 [2, 64, 1024, 1024], P('mp', None, 'gx', 'gy')
- remapped: float32 [2, 8, 1024, 1024], P('mp', None, 'gx', 'gy')
Inputs may be any that keep to these rules, and one draw needn't show every extreme that they name: `tile_target`: among the tiles of one device, no destination device is named by more than 8 tiles, and some device is named by exactly 8.
All inputs are finite; a program needn't handle non-finite values. No bound on the sum of `land_mask` on one device may be relied on, other than what follows from the above.
Results may differ from a plain program's by a relative error of at most 0.0029.
Values sent between devices are 32-bit elements; how exact they have to be, the bound alone decides.
A program may use at most 192 MiB of HBM per device.

v0:
```python
import jax
import jax.numpy as jnp
from jax import lax
from jax.sharding import PartitionSpec as P

CY = 128
KF = 8
CAP = 8


force_gain = 0.5


def with_halo(shard, sides, width):
    for axis, dim in sides:
        devices, length = (lax.axis_size(axis), shard.shape[dim])
        up = [(i, (i + 1) % devices) for i in range(devices - 1)]
        down = [(j, i) for i, j in up]
        last = lax.slice_in_dim(shard, length - width, length, axis=dim)
        first = lax.slice_in_dim(shard, 0, width, axis=dim)
        before = lax.ppermute(last, axis, up)
        after = lax.ppermute(first, axis, down)
        shard = jnp.concatenate([before, shard, after], axis=dim)
    return shard


def vertical_part(state):
    column = jnp.pad(state, ((1, 1), (0, 0), (0, 0)))
    return column[2:] + column[:-2] - 2.0 * state


def stencil(state, wet, horiz, vert):
    weighted = state * wet
    padded = with_halo(weighted, (("gx", 1), ("gy", 2)), 1)
    lateral = (
        padded[:, 2:, 1:-1]
        + padded[:, :-2, 1:-1]
        + padded[:, 1:-1, 2:]
        + padded[:, 1:-1, :-2]
        - 4.0 * weighted
    )
    return wet * (state + horiz * lateral + vert * vertical_part(state))


def two_steps(state, wet, horiz, vert):
    first = stencil(state, wet, horiz, vert)
    return stencil(first, wet, horiz, vert)


def local(states, surface, land_mask, tile_weights, tile_source, tile_target, tile_row):
    group = lax.axis_index("mp")
    ndev = lax.axis_size("gx") * lax.axis_size("gy")
    state = states[0]
    rows_here = state.shape[1]
    wet = jnp.where(
        group == 0, jnp.ones(land_mask.shape, jnp.float32), land_mask.astype(jnp.float32)
    )
    horiz = jnp.where(group == 0, 0.15, 0.12)
    vert = jnp.where(group == 0, 0.1, 0.15)
    src = (surface[0] * wet).astype(jnp.bfloat16)
    source = tile_source[0, 0, 0]
    target = tile_target[0, 0, 0, :, 0]
    dest_row = tile_row[0, 0, 0]
    picked = jnp.take(src, source, axis=1)
    contrib = jnp.einsum(
        "tji,kti->tkj", tile_weights[0, 0, 0], picked, preferred_element_type=jnp.float32
    )
    onehot = (target[:, None] == jnp.arange(ndev, dtype=jnp.int32)[None, :]).astype(jnp.int32)
    earlier = jnp.cumsum(onehot, axis=0) - onehot
    rank = jnp.sum(earlier * onehot, axis=1)
    slot = target * CAP + rank
    buckets = (
        jnp.zeros((ndev * CAP, KF, CY), jnp.float32)
        .at[slot]
        .set(contrib)
        .reshape(ndev, CAP, KF, CY)
    )
    labels = jnp.zeros((ndev * CAP,), jnp.int32).at[slot].set(dest_row + 1).reshape(ndev, CAP)
    empty = jnp.zeros_like(buckets)
    empty_rows = jnp.zeros_like(labels)
    wide = jnp.where(
        group == 0, jnp.concatenate([empty, buckets], 0), jnp.concatenate([buckets, empty], 0)
    )
    wide_rows = jnp.where(
        group == 0,
        jnp.concatenate([empty_rows, labels], 0),
        jnp.concatenate([labels, empty_rows], 0),
    )
    arrived, arrived_rows = (
        lax.all_to_all(wide, ("mp", "gx", "gy"), split_axis=0, concat_axis=0, tiled=True),
        lax.all_to_all(wide_rows, ("mp", "gx", "gy"), split_axis=0, concat_axis=0, tiled=True),
    )
    start = (1 - group) * ndev
    got = lax.dynamic_slice_in_dim(arrived, start, ndev, 0)
    got_rows = lax.dynamic_slice_in_dim(arrived_rows, start, ndev, 0)
    select = (
        got_rows[:, :, None] == jnp.arange(1, rows_here + 1, dtype=jnp.int32)[None, None, :]
    ).astype(jnp.float32)
    received = jnp.einsum("scr,sckj->krj", select, got, precision=lax.Precision.HIGHEST)
    second = two_steps(state, wet, horiz, vert)
    second = second.at[0].add(force_gain * wet * received[0])
    return (second[None], received[None])


def solution(mesh):
    return jax.shard_map(
        local,
        mesh=mesh,
        in_specs=(
            P("mp", None, "gx", "gy"),
            P("mp", None, "gx", "gy"),
            P("gx", "gy"),
            P("mp", "gx", "gy", None, None, None),
            P("mp", "gx", "gy", None),
            P("mp", "gx", "gy", None, None),
            P("mp", "gx", "gy", None),
        ),
        out_specs=(P("mp", None, "gx", "gy"), P("mp", None, "gx", "gy")),
        check_vma=False,
    )
```

profile of v0, /device:TPU:72, one launch (start us, length us, event | category | flops | bytes accessed | tf_op | source)
XLA Modules:
  0.0 233.6 jit_solution(4570673680974329697)
XLA Ops:
  6.5 10.0 %all-to-all-start.1 = ((s32[128,1,8]{2,1,0:T(1,128)}), s32[128,1,8]{2,1,0:T(1,128)S(1)}, u32[]{:S(2)}, u32[]{:S(2)}) async-start(s32[128,1,8]{2,1,0:T(1,128)} %bitcast.17), calls=%async_computation.1 | async-start | bytes 131072 | tf_op jit(solution)/shard_map/all_to_all | solution.py:91
  20.4 6.8 %fusion = f32[256,8,128]{2,1,0:T(8,128)S(1)} fusion(bf16[1,1,1,256,128,128]{5,4,3,2,1,0:T(8,128)(2,1)} %param.12, bf16[256,8,128]{2,1,0:T(8,128)(2,1)S(1)} %gather_fusion, pred[256]{0:T(512)(128)(4,1)S(1)} %compare_and_fusion), kind=kOutput, calls=%fused_computation.3 | convolution fusion | flops 67371008 | bytes 9961728 | tf_op jit(solution)/shard_map/tji,kti->tkj/dot_general | solution.py:65
  27.4 6.9 %scatter_fusion = f32[512,8,128]{2,1,0:T(8,128)S(1)} fusion(f32[512,8,128]{2,1,0:T(8,128)S(1)} %broadcast_in_dim.41, s32[256]{0:T(256)S(1)} %bitcast.92, f32[256,8,128]{2,1,0:T(8,128)S(1)} %fusion), kind=kCustom, calls=%fused_computation.1 | custom fusion | bytes 3146752 | tf_op jit(solution)/shard_map/scatter | solution.py:75
  36.9 5.6 %copy.35 = f32[1,64,128,128]{2,3,1,0:T(8,128)} copy(f32[1,64,128,128]{3,2,1,0:T(8,128)} %param.9) | data formatting | bytes 8388608 | tf_op args[0]
  42.4 5.1 %copy.51 = f32[128,8,8,128]{3,1,2,0:T(8,128)} copy(f32[128,8,8,128]{3,2,1,0:T(8,128)} %pad_select_fusion) | data formatting | bytes 8388608 | tf_op jit(solution)/shard_map/jit(_where)/select_n | solution.py:81
  47.6 10.2 %all-to-all-start = ((f32[128,8,8,128]{3,1,2,0:T(8,128)}), f32[128,8,8,128]{3,1,2,0:T(8,128)}, u32[]{:S(2)}, u32[]{:S(2)}) async-start(f32[128,8,8,128]{3,1,2,0:T(8,128)} %copy.51), calls=%async_computation | async-start | bytes 8388608 | tf_op jit(solution)/shard_map/all_to_all | solution.py:90
  60.3 4.7 %fusion.43 = (f32[64,1,128]{1,2,0:T(8,128)}, f32[64,1,128]{1,2,0:T(8,128)}) fusion(f32[64,128,128]{1,2,0:T(8,128)S(1)} %broadcast_multiply_fusion.1), kind=kLoop, calls=%fused_computation.89 | loop fusion | bytes 131072 | tf_op jit(solution)/shard_map/slice | solution.py:19
  65.1 2.8 %copy.36 = f32[64,1,128]{2,0,1:T(8,128)S(1)} copy(f32[64,1,128]{1,2,0:T(8,128)} %get-tuple-element.31) | data formatting | bytes 65536 | tf_op jit(solution)/shard_map/slice | solution.py:20
  67.9 3.8 %collective-permute-start = (f32[64,1,128]{2,0,1:T(8,128)S(1)}, f32[64,1,128]{2,0,1:T(8,128)S(1)}, u32[]{:S(2)}, u32[]{:S(2)}) collective-permute-start(f32[64,1,128]{2,0,1:T(8,128)S(1)} %copy.36), channel_id=1, source_target_pairs={{8,0},{16,8},{24,16},{32,24},{40,32},{48,40},{56,48},{9,1},{17,9},... | collective-permute-start | bytes 98312 | tf_op jit(solution)/shard_map/ppermute | solution.py:22
  71.8 2.8 %copy.38 = f32[64,1,128]{2,0,1:T(8,128)S(1)} copy(f32[64,1,128]{1,2,0:T(8,128)} %get-tuple-element.30) | data formatting | bytes 65536 | tf_op jit(solution)/shard_map/slice | solution.py:19
  74.6 3.5 %collective-permute-start.1 = (f32[64,1,128]{2,0,1:T(8,128)S(1)}, f32[64,1,128]{2,0,1:T(8,128)S(1)}, u32[]{:S(2)}, u32[]{:S(2)}) collective-permute-start(f32[64,1,128]{2,0,1:T(8,128)S(1)} %copy.38), channel_id=1, source_target_pairs={{0,8},{8,16},{16,24},{24,32},{32,40},{40,48},{48,56},{1,9},{9,17},... | collective-permute-start | bytes 98312 | tf_op jit(solution)/shard_map/ppermute | solution.py:21
  78.1 32.0 %collective-permute-done = f32[64,1,128]{2,0,1:T(8,128)S(1)} collective-permute-done((f32[64,1,128]{2,0,1:T(8,128)S(1)}, f32[64,1,128]{2,0,1:T(8,128)S(1)}, u32[]{:S(2)}, u32[]{:S(2)}) %collective-permute-start) | collective-permute-done | bytes 32800 | tf_op jit(solution)/shard_map/ppermute | solution.py:22
  117.2 5.0 %collective-permute-start.2 = (f32[64,130,1]{1,2,0:T(1,128)S(1)}, f32[64,130,1]{1,2,0:T(1,128)S(1)}, u32[]{:S(2)}, u32[]{:S(2)}) collective-permute-start(f32[64,130,1]{1,2,0:T(1,128)S(1)} %get-tuple-element.26), channel_id=1, source_target_pairs={{1,0},{2,1},{3,2},{4,3},{5,4},{6,5},{7,6},{9,8},{10,9},{11,10},{12... | collective-permute-start | bytes 99848 | tf_op jit(solution)/shard_map/ppermute | solution.py:22
  125.0 5.4 %collective-permute-done.3 = f32[64,130,1]{1,2,0:T(1,128)S(1)} collective-permute-done((f32[64,130,1]{1,2,0:T(1,128)S(1)}, f32[64,130,1]{1,2,0:T(1,128)S(1)}, u32[]{:S(2)}, u32[]{:S(2)}) %collective-permute-start.3) | collective-permute-done | bytes 33312 | tf_op jit(solution)/shard_map/ppermute | solution.py:21
  130.5 24.4 %broadcast_multiply_fusion = (f32[64,128,128]{1,2,0:T(8,128)S(1)}, f32[64,128,128]{1,2,0:T(8,128)}) fusion(f32[128,128]{0,1:T(8,128)S(1)} %convert_select_fusion, f32[64,128,128]{1,2,0:T(8,128)} %bitcast.83, f32[]{:T(128)S(6)} %select_n.69, f32[64,128,128]{1,2,0:T(8,128)} %copy-done.1, f32[64,1,128]{1,2,0:T(8,128)} %copy.37, f32[64,1,128]{1,2,0:T(8,128)} %copy.39, ...), kind=kLoop, calls=%fused_computation.40 | loop fusion | flops 23068672 | bytes 16974856 | tf_op jit(solution)/shard_map/mul | solution.py:33
  154.9 4.9 %fusion.42 = (f32[64,1,128]{1,2,0:T(8,128)}, f32[64,1,128]{1,2,0:T(8,128)}) fusion(f32[64,128,128]{1,2,0:T(8,128)S(1)} %get-tuple-element.22), kind=kLoop, calls=%fused_computation.88 | loop fusion | bytes 131072 | tf_op jit(solution)/shard_map/slice | solution.py:19
  159.8 2.8 %copy.42 = f32[64,1,128]{2,0,1:T(8,128)S(1)} copy(f32[64,1,128]{1,2,0:T(8,128)} %get-tuple-element.29) | data formatting | bytes 65536 | tf_op jit(solution)/shard_map/slice | solution.py:20
  162.6 6.2 %collective-permute-start.4 = (f32[64,1,128]{2,0,1:T(8,128)S(1)}, f32[64,1,128]{2,0,1:T(8,128)S(1)}, u32[]{:S(2)}, u32[]{:S(2)}) collective-permute-start(f32[64,1,128]{2,0,1:T(8,128)S(1)} %copy.42), channel_id=1, source_target_pairs={{8,0},{16,8},{24,16},{32,24},{40,32},{48,40},{56,48},{9,1},{17,9},... | collective-permute-start | bytes 98312 | tf_op jit(solution)/shard_map/ppermute | solution.py:22
  168.8 2.8 %copy.44 = f32[64,1,128]{2,0,1:T(8,128)S(1)} copy(f32[64,1,128]{1,2,0:T(8,128)} %get-tuple-element.28) | data formatting | bytes 65536 | tf_op jit(solution)/shard_map/slice | solution.py:19
  176.3 3.6 %collective-permute-done.5 = f32[64,1,128]{2,0,1:T(8,128)S(1)} collective-permute-done((f32[64,1,128]{2,0,1:T(8,128)S(1)}, f32[64,1,128]{2,0,1:T(8,128)S(1)}, u32[]{:S(2)}, u32[]{:S(2)}) %collective-permute-start.5) | collective-permute-done | bytes 32800 | tf_op jit(solution)/shard_map/ppermute | solution.py:21
  186.5 3.7 %collective-permute-start.7 = (f32[64,130,1]{1,2,0:T(1,128)S(1)}, f32[64,130,1]{1,2,0:T(1,128)S(1)}, u32[]{:S(2)}, u32[]{:S(2)}) collective-permute-start(f32[64,130,1]{1,2,0:T(1,128)S(1)} %get-tuple-element.25), channel_id=1, source_target_pairs={{0,1},{1,2},{2,3},{3,4},{4,5},{5,6},{6,7},{8,9},{9,10},{10,11},{11... | collective-permute-start | bytes 99848 | tf_op jit(solution)/shard_map/ppermute | solution.py:21
  190.4 4.3 %collective-permute-done.7 = f32[64,130,1]{1,2,0:T(1,128)S(1)} collective-permute-done((f32[64,130,1]{1,2,0:T(1,128)S(1)}, f32[64,130,1]{1,2,0:T(1,128)S(1)}, u32[]{:S(2)}, u32[]{:S(2)}) %collective-permute-start.7) | collective-permute-done | bytes 33312 | tf_op jit(solution)/shard_map/ppermute | solution.py:21
  194.7 22.4 %fusion.7 = f32[64,128,128]{1,2,0:T(8,128)S(1)} fusion(f32[64,128,128]{1,2,0:T(8,128)} %get-tuple-element.23, f32[64,130,1]{1,2,0:T(1,128)S(1)} %collective-permute-done.7, f32[64,1,128]{1,2,0:T(8,128)} %copy.43, f32[64,128,128]{1,2,0:T(8,128)} %copy-done, f32[64,1,128]{1,2,0:T(8,128)} %copy.45, f32[64,130,1]{1,2,0:T(1,128)S(1)} %collective-permute-done.6, ...), kind=kLoop, calls=%fused_computation.11 | loop fusion | flops 22020096 | bytes 12780552 | tf_op jit(solution)/shard_map/mul | solution.py:42
  227.0 5.6 %copy.55 = f32[1,64,128,128]{3,2,1,0:T(8,128)} copy(f32[1,64,128,128]{2,3,1,0:T(8,128)} %fusion.36) | data formatting | bytes 8388608
  (50 shorter events, 47.2 us)
Async XLA Ops:
  6.5 41.1 %all-to-all-start.1 = ((s32[128,1,8]{2,1,0:T(1,128)}), s32[128,1,8]{2,1,0:T(1,128)S(1)}, u32[]{:S(2)}, u32[]{:S(2)}) async-start(s32[128,1,8]{2,1,0:T(1,128)} %bitcast.17), calls=%async_computation.1 | async-start | bytes 131072 | tf_op jit(solution)/shard_map/all_to_all | solution.py:91
  47.6 173.6 %all-to-all-start = ((f32[128,8,8,128]{3,1,2,0:T(8,128)}), f32[128,8,8,128]{3,1,2,0:T(8,128)}, u32[]{:S(2)}, u32[]{:S(2)}) async-start(f32[128,8,8,128]{3,1,2,0:T(8,128)} %copy.51), calls=%async_computation | async-start | bytes 8388608 | tf_op jit(solution)/shard_map/all_to_all | solution.py:90
  60.3 4.8 %copy-start.1 = (f32[64,128,128]{1,2,0:T(8,128)}, f32[64,128,128]{1,2,0:T(8,128)S(1)}, u32[]{:S(2)}) copy-start(f32[64,128,128]{1,2,0:T(8,128)S(1)} %broadcast_multiply_fusion.1) | copy-start | bytes 12582916
  67.9 42.2 %collective-permute-start = (f32[64,1,128]{2,0,1:T(8,128)S(1)}, f32[64,1,128]{2,0,1:T(8,128)S(1)}, u32[]{:S(2)}, u32[]{:S(2)}) collective-permute-start(f32[64,1,128]{2,0,1:T(8,128)S(1)} %copy.36), channel_id=1, source_target_pairs={{8,0},{16,8},{24,16},{32,24},{40,32},{48,40},{56,48},{9,1},{17,9},... | collective-permute-start | bytes 98312 | tf_op jit(solution)/shard_map/ppermute | solution.py:22
  74.6 38.1 %collective-permute-start.1 = (f32[64,1,128]{2,0,1:T(8,128)S(1)}, f32[64,1,128]{2,0,1:T(8,128)S(1)}, u32[]{:S(2)}, u32[]{:S(2)}) collective-permute-start(f32[64,1,128]{2,0,1:T(8,128)S(1)} %copy.38), channel_id=1, source_target_pairs={{0,8},{8,16},{16,24},{24,32},{32,40},{40,48},{48,56},{1,9},{9,17},... | collective-permute-start | bytes 98312 | tf_op jit(solution)/shard_map/ppermute | solution.py:21
  117.2 7.8 %collective-permute-start.2 = (f32[64,130,1]{1,2,0:T(1,128)S(1)}, f32[64,130,1]{1,2,0:T(1,128)S(1)}, u32[]{:S(2)}, u32[]{:S(2)}) collective-permute-start(f32[64,130,1]{1,2,0:T(1,128)S(1)} %get-tuple-element.26), channel_id=1, source_target_pairs={{1,0},{2,1},{3,2},{4,3},{5,4},{6,5},{7,6},{9,8},{10,9},{11,10},{12... | collective-permute-start | bytes 99848 | tf_op jit(solution)/shard_map/ppermute | solution.py:22
  122.2 8.3 %collective-permute-start.3 = (f32[64,130,1]{1,2,0:T(1,128)S(1)}, f32[64,130,1]{1,2,0:T(1,128)S(1)}, u32[]{:S(2)}, u32[]{:S(2)}) collective-permute-start(f32[64,130,1]{1,2,0:T(1,128)S(1)} %get-tuple-element.27), channel_id=1, source_target_pairs={{0,1},{1,2},{2,3},{3,4},{4,5},{5,6},{6,7},{8,9},{9,10},{10,11},{11... | collective-permute-start | bytes 99848 | tf_op jit(solution)/shard_map/ppermute | solution.py:21
  154.9 4.9 %copy-start = (f32[64,128,128]{1,2,0:T(8,128)}, f32[64,128,128]{1,2,0:T(8,128)S(1)}, u32[]{:S(2)}) copy-start(f32[64,128,128]{1,2,0:T(8,128)S(1)} %get-tuple-element.22) | copy-start | bytes 12582916
  162.6 11.0 %collective-permute-start.4 = (f32[64,1,128]{2,0,1:T(8,128)S(1)}, f32[64,1,128]{2,0,1:T(8,128)S(1)}, u32[]{:S(2)}, u32[]{:S(2)}) collective-permute-start(f32[64,1,128]{2,0,1:T(8,128)S(1)} %copy.42), channel_id=1, source_target_pairs={{8,0},{16,8},{24,16},{32,24},{40,32},{48,40},{56,48},{9,1},{17,9},... | collective-permute-start | bytes 98312 | tf_op jit(solution)/shard_map/ppermute | solution.py:22
  171.6 8.2 %collective-permute-start.5 = (f32[64,1,128]{2,0,1:T(8,128)S(1)}, f32[64,1,128]{2,0,1:T(8,128)S(1)}, u32[]{:S(2)}, u32[]{:S(2)}) collective-permute-start(f32[64,1,128]{2,0,1:T(8,128)S(1)} %copy.44), channel_id=1, source_target_pairs={{0,8},{8,16},{16,24},{24,32},{32,40},{40,48},{48,56},{1,9},{9,17},... | collective-permute-start | bytes 98312 | tf_op jit(solution)/shard_map/ppermute | solution.py:21
  184.3 6.2 %collective-permute-start.6 = (f32[64,130,1]{1,2,0:T(1,128)S(1)}, f32[64,130,1]{1,2,0:T(1,128)S(1)}, u32[]{:S(2)}, u32[]{:S(2)}) collective-permute-start(f32[64,130,1]{1,2,0:T(1,128)S(1)} %get-tuple-element.24), channel_id=1, source_target_pairs={{1,0},{2,1},{3,2},{4,3},{5,4},{6,5},{7,6},{9,8},{10,9},{11,10},{12... | collective-permute-start | bytes 99848 | tf_op jit(solution)/shard_map/ppermute | solution.py:22
  186.5 8.3 %collective-permute-start.7 = (f32[64,130,1]{1,2,0:T(1,128)S(1)}, f32[64,130,1]{1,2,0:T(1,128)S(1)}, u32[]{:S(2)}, u32[]{:S(2)}) collective-permute-start(f32[64,130,1]{1,2,0:T(1,128)S(1)} %get-tuple-element.25), channel_id=1, source_target_pairs={{0,1},{1,2},{2,3},{3,4},{4,5},{5,6},{6,7},{8,9},{9,10},{10,11},{11... | collective-permute-start | bytes 99848 | tf_op jit(solution)/shard_map/ppermute | solution.py:21
  217.2 2.0 copy-start.2
where the time goes:
time: 235 us; the launch traced here: 234 us
  local copies, waits for them, and re-layouts  65.2 us (28%)
  other arithmetic  63.2 us (27%)
  starting transfers between devices  49.2 us (21%)
  waiting for transfers between devices  45.6 us (19%)
  matrix products  9.5 us (4%)
    ppermute x4, waiting for transfers between devices, with_halo(): after = lax.ppermute(first, axis, down)  32.3 us
    mul x2, other arithmetic, stencil(): weighted = state * wet  26.9 us
    mul x1, other arithmetic, stencil(): return wet * (state + horiz * lateral + vert * vertical_part(state))  22.4 us
    ppermute x4, starting transfers between devices, with_halo(): after = lax.ppermute(first, axis, down)  17.2 us
    unnamed x12, local copies, waits for them, and re-layouts  17.1 us
    slice x4, local copies, waits for them, and re-layouts, with_halo(): last = lax.slice_in_dim(shard, length - width, length, axis=dim)  15.3 us
    ppermute x4, waiting for transfers between devices, with_halo(): before = lax.ppermute(last, axis, up)  13.3 us
    ppermute x4, starting transfers between devices, with_halo(): before = lax.ppermute(last, axis, up)  11.8 us
  transfers between devices with their start and end apart: 10, of which 6 were waited for; matrix products, arithmetic and copies ran while one was open for 50% of the time, Pallas kernels for 0%

commit v1 on v0

v1 whole, which is shorter than its diff:
```python
import functools

import jax
import jax.numpy as jnp
from jax import lax
from jax.experimental import pallas as pl
from jax.experimental.pallas import tpu as pltpu
from jax.sharding import PartitionSpec as P

CY = 128
KF = 8
CAP = 8
LB = 8

force_gain = 0.5


def shift_pairs(devices, forward):
    up = [(i, i + 1) for i in range(devices - 1)]
    return up if forward else [(j, i) for i, j in up]


def stencil_kernel(with_edges, with_force, coef_ref, wet_ref, u_ref, above_ref, below_ref,
                   hn_ref, hs_ref, hw_ref, he_ref, *rest):
    if with_force:
        force_ref, rest = rest[0], rest[1:]
    out_ref = rest[0]
    i = pl.program_id(0)
    nblk = pl.num_programs(0)
    horiz = coef_ref[0]
    vert = coef_ref[1]
    wet = wet_ref[...]
    rows, cols = wet.shape
    row = lax.broadcasted_iota(jnp.int32, (rows, cols), 0)
    col = lax.broadcasted_iota(jnp.int32, (rows, cols), 1)
    hw_t = jnp.transpose(hw_ref[...])
    he_t = jnp.transpose(he_ref[...])
    above = above_ref[0] * jnp.where(i > 0, 1.0, 0.0)
    below = below_ref[0] * jnp.where(i < nblk - 1, 1.0, 0.0)
    if with_edges:
        en_ref, es_ref, ew_ref, ee_ref, qw_ref, qe_ref = rest[1:]

        @pl.when(i == 0)
        def _():
            qw_ref[...] = jnp.zeros_like(qw_ref)
            qe_ref[...] = jnp.zeros_like(qe_ref)

    for l in range(LB):
        u = u_ref[l]
        prev = u_ref[l - 1] if l > 0 else above
        nxt = u_ref[l + 1] if l < LB - 1 else below
        w = wet * u
        north = jnp.where(row == 0, hn_ref[l:l + 1, :], pltpu.roll(w, 1, 0))
        south = jnp.where(row == rows - 1, hs_ref[l:l + 1, :], pltpu.roll(w, rows - 1, 0))
        west = jnp.where(col == 0, hw_t[:, l:l + 1], pltpu.roll(w, 1, 1))
        east = jnp.where(col == cols - 1, he_t[:, l:l + 1], pltpu.roll(w, cols - 1, 1))
        lateral = north + south + west + east - 4.0 * w
        vertical = prev + nxt - 2.0 * u
        res = wet * (u + horiz * lateral + vert * vertical)
        if with_force and l == 0:
            res = res + jnp.where(i == 0, 1.0, 0.0) * (force_gain * wet * force_ref[...])
        out_ref[l] = res
        if with_edges:
            fw = wet * res
            en_ref[l:l + 1, :] = fw[0:1, :]
            es_ref[l:l + 1, :] = fw[rows - 1:rows, :]
            lane = lax.broadcasted_iota(jnp.int32, qw_ref.shape, 1)
            hit = lane == i * LB + l
            qw_ref[...] = jnp.where(hit, fw[:, 0:1], qw_ref[...])
            qe_ref[...] = jnp.where(hit, fw[:, cols - 1:cols], qe_ref[...])

    if with_edges:
        @pl.when(i == nblk - 1)
        def _():
            lev = ew_ref.shape[0]
            ew_ref[...] = jnp.transpose(qw_ref[...])[0:lev, :]
            ee_ref[...] = jnp.transpose(qe_ref[...])[0:lev, :]


def stencil_step(coef, wet, u, halos, force=None, with_edges=False):
    lev, rows, cols = u.shape
    nblk = lev // LB
    full2 = lambda shape: pl.BlockSpec(shape, lambda i: (0, 0))
    lvl2 = pl.BlockSpec((LB, cols), lambda i: (i, 0))
    in_specs = [
        pl.BlockSpec(memory_space=pltpu.SMEM),
        full2((rows, cols)),
        pl.BlockSpec((LB, rows, cols), lambda i: (i, 0, 0)),
        pl.BlockSpec((1, rows, cols), lambda i: (jnp.maximum(i * LB - 1, 0), 0, 0)),
        pl.BlockSpec((1, rows, cols), lambda i: (jnp.minimum(i * LB + LB, lev - 1), 0, 0)),
        lvl2, lvl2, lvl2, lvl2,
    ]
    args = [coef, wet, u, u, u] + list(halos)
    if force is not None:
        in_specs.append(full2((rows, cols)))
        args.append(force)
    out_shape = [jax.ShapeDtypeStruct((lev, rows, cols), jnp.float32)]
    out_specs = [pl.BlockSpec((LB, rows, cols), lambda i: (i, 0, 0))]
    scratch = []
    if with_edges:
        out_shape += [jax.ShapeDtypeStruct((lev, cols), jnp.float32)] * 2
        out_shape += [jax.ShapeDtypeStruct((lev, rows), jnp.float32)] * 2
        out_specs += [lvl2, lvl2, full2((lev, rows)), full2((lev, rows))]
        scratch = [pltpu.VMEM((rows, 128), jnp.float32)] * 2
    return pl.pallas_call(
        functools.partial(stencil_kernel, with_edges, force is not None),
        grid=(nblk,),
        in_specs=in_specs,
        out_specs=out_specs,
        out_shape=out_shape,
        scratch_shapes=scratch,
        compiler_params=pltpu.CompilerParams(dimension_semantics=("arbitrary",)),
    )(*args)


def exchange(en, es, ew, ee):
    ngx, ngy = lax.axis_size("gx"), lax.axis_size("gy")
    hn = lax.ppermute(es, "gx", shift_pairs(ngx, True))
    hs = lax.ppermute(en, "gx", shift_pairs(ngx, False))
    hw = lax.ppermute(ee, "gy", shift_pairs(ngy, True))
    he = lax.ppermute(ew, "gy", shift_pairs(ngy, False))
    return hn, hs, hw, he


def bucket_kernel(inv_ref, lab_ref, contrib_ref, out_ref):
    ndest = out_ref.shape[0]
    ntiles = contrib_ref.shape[0]
    sub = lax.broadcasted_iota(jnp.int32, (KF, CY), 0)

    def body(d, carry):
        labv = jnp.zeros((KF, CY), jnp.float32)
        for c in range(CAP):
            t = inv_ref[d * CAP + c]
            val = contrib_ref[jnp.minimum(t, ntiles - 1)]
            out_ref[d, c] = jnp.where(t < ntiles, val, 0.0)
            labv = jnp.where(sub == c, lab_ref[d * CAP + c].astype(jnp.float32), labv)
        out_ref[d, CAP] = labv
        return carry

    lax.fori_loop(0, ndest, body, 0)


def recv_kernel(rows_ref, got_ref, acc_ref):
    acc_ref[...] = jnp.zeros_like(acc_ref)
    nslots = got_ref.shape[0] * CAP

    def body(s, carry):
        r = rows_ref[s]
        acc_ref[r] = acc_ref[r] + got_ref[s // CAP, s % CAP]
        return carry

    lax.fori_loop(0, nslots, body, 0)


def local(states, surface, land_mask, tile_weights, tile_source, tile_target, tile_row):
    group = lax.axis_index("mp")
    ndev = lax.axis_size("gx") * lax.axis_size("gy")
    state = states[0]
    lev, rows_here, cols_here = state.shape
    wet = jnp.where(
        group == 0, jnp.ones(land_mask.shape, jnp.float32), land_mask.astype(jnp.float32)
    )
    coef = jnp.stack([jnp.where(group == 0, 0.15, 0.12), jnp.where(group == 0, 0.1, 0.15)]).astype(
        jnp.float32
    )

    src = (surface[0] * wet).astype(jnp.bfloat16)
    source = tile_source[0, 0, 0]
    target = tile_target[0, 0, 0, :, 0]
    dest_row = tile_row[0, 0, 0]
    ntiles = source.shape[0]
    picked = jnp.take(src, source, axis=1)
    contrib = jnp.einsum(
        "tji,kti->tkj", tile_weights[0, 0, 0], picked, preferred_element_type=jnp.float32
    )
    onehot = (target[:, None] == jnp.arange(ndev, dtype=jnp.int32)[None, :]).astype(jnp.int32)
    earlier = jnp.cumsum(onehot, axis=0) - onehot
    rank = jnp.sum(earlier * onehot, axis=1)
    slot = target * CAP + rank
    inv = jnp.full((ndev * CAP,), ntiles, jnp.int32).at[slot].set(jnp.arange(ntiles, dtype=jnp.int32))
    labels = jnp.zeros((ndev * CAP,), jnp.int32).at[slot].set(dest_row)
    buckets = pl.pallas_call(
        bucket_kernel,
        in_specs=[
            pl.BlockSpec(memory_space=pltpu.SMEM),
            pl.BlockSpec(memory_space=pltpu.SMEM),
            pl.BlockSpec(memory_space=pltpu.VMEM),
        ],
        out_specs=pl.BlockSpec(memory_space=pltpu.VMEM),
        out_shape=jax.ShapeDtypeStruct((ndev, CAP + 1, KF, CY), jnp.float32),
    )(inv, labels, contrib)
    arrived = lax.all_to_all(buckets, ("gx", "gy"), split_axis=0, concat_axis=0, tiled=True)
    got_rows = jnp.clip(arrived[:, CAP, :, 0].astype(jnp.int32), 0, rows_here - 1).reshape(-1)
    acc = pl.pallas_call(
        recv_kernel,
        in_specs=[pl.BlockSpec(memory_space=pltpu.SMEM), pl.BlockSpec(memory_space=pltpu.VMEM)],
        out_specs=pl.BlockSpec(memory_space=pltpu.VMEM),
        out_shape=jax.ShapeDtypeStruct((rows_here, KF, CY), jnp.float32),
    )(got_rows, arrived)
    sent = jnp.transpose(acc, (1, 0, 2))
    received = lax.ppermute(sent, "mp", [(0, 1), (1, 0)])

    w0 = state * wet[None]
    halos0 = exchange(
        w0[:, 0, :], w0[:, rows_here - 1, :], w0[:, :, 0], w0[:, :, cols_here - 1]
    )
    first, en, es, ew, ee = stencil_step(coef, wet, state, halos0, with_edges=True)
    halos1 = exchange(en, es, ew, ee)
    (second,) = stencil_step(coef, wet, first, halos1, force=received[0])
    return (second[None], received[None])


def solution(mesh):
    return jax.shard_map(
        local,
        mesh=mesh,
        in_specs=(
            P("mp", None, "gx", "gy"),
            P("mp", None, "gx", "gy"),
            P("gx", "gy"),
            P("mp", "gx", "gy", None, None, None),
            P("mp", "gx", "gy", None),
            P("mp", "gx", "gy", None, None),
            P("mp", "gx", "gy", None),
        ),
        out_specs=(P("mp", None, "gx", "gy"), P("mp", None, "gx", "gy")),
        check_vma=False,
    )
```

time: 235 us -> 160 us (0.68)
  the two profiles are of different devices: /device:TPU:72 before, /device:TPU:38 now
where the time goes in v1:
time: 160 us; the launch traced here: 159 us
  starting transfers between devices  39.7 us (25%)
  Pallas kernels  38.7 us (24%)
  local copies, waits for them, and re-layouts  31.2 us (20%)
  waiting for transfers between devices  26.6 us (17%)
  other arithmetic  13.4 us (8%)
  matrix products  8.82 us (6%)
    pallas_call x2, Pallas kernels, stencil_step(): pl.pallas_call(functools.partial(stencil_kernel, with_edges, force is not...  25.8 us
    all_to_all x1, waiting for transfers between devices, local(): lax.all_to_all(buckets, ('gx', 'gy'), split_axis=0, concat_axis=0, tiled=...  18.2 us
    slice x2, local copies, waits for them, and re-layouts, local(): w0[:, 0, :]  11.7 us
    all_to_all x1, starting transfers between devices, local(): lax.all_to_all(buckets, ('gx', 'gy'), split_axis=0, concat_axis=0, tiled=...  11 us
    dot_general x1, matrix products, local(): jnp.einsum('tji,kti->tkj', tile_weights[0, 0, 0], picked, preferred_eleme...  8.82 us
    ppermute x2, starting transfers between devices, exchange(): hn = lax.ppermute(es, 'gx', shift_pairs(ngx, True))  8.49 us
    pallas_call x1, Pallas kernels, local(): pl.pallas_call(recv_kernel, in_specs=[pl.BlockSpec(memory_space=pltpu.SME...  8.43 us
    ppermute x2, waiting for transfers between devices, exchange(): he = lax.ppermute(ew, 'gy', shift_pairs(ngy, False))  8.38 us
  transfers between devices with their start and end apart: 10, of which 3 were waited for; matrix products, arithmetic and copies ran while one was open for 18% of the time, Pallas kernels for 10%

profile of v1, /device:TPU:38, one launch (start us, length us, event | category | flops | bytes accessed | tf_op | source)
XLA Modules:
  0.0 159.3 jit_solution(8024635189647841092)
XLA Ops:
  8.1 2.1 %scatter_custom_fusion.1.lab_ref = s32[512]{0:T(512)} fusion(s32[256]{0:T(256)S(1)} %bitcast.74, s32[256]{0:T(256)} %bitcast.77, s32[]{:T(128)} %constant.15.clone.1), kind=kCustom, calls=%fused_computation.35 | custom fusion | bytes 2560 | tf_op jit(solution)/shard_map/scatter | solution.py:181
  10.2 2.0 %scatter_custom_fusion.inv_ref = s32[512]{0:T(512)} fusion(s32[256]{0:T(256)S(1)} %bitcast.75, s32[256]{0:T(256)S(1)} %iota.11, s32[]{:T(128)} %constant.12.clone.1), kind=kCustom, calls=%fused_computation.37 | custom fusion | bytes 2052 | tf_op jit(solution)/shard_map/scatter | solution.py:180
  12.2 8.8 %fusion.contrib_ref = f32[256,8,128]{2,1,0:T(8,128)} fusion(bf16[1,1,1,256,128,128]{5,4,3,2,1,0:T(8,128)(2,1)} %param.10, bf16[256,8,128]{2,1,0:T(8,128)(2,1)S(1)} %gather_fusion, pred[256]{0:T(512)(128)(4,1)S(1)} %compare_and_fusion), kind=kOutput, calls=%fused_computation.3 | convolution fusion | flops 67371008 | bytes 9961728 | tf_op jit(solution)/shard_map/tji,kti->tkj/dot_general | solution.py:173
  21.0 4.5 %shard_map.87 = f32[64,9,8,128]{3,2,1,0:T(8,128)} custom-call(s32[512]{0:T(512)} %scatter_custom_fusion.inv_ref, s32[512]{0:T(512)} %scatter_custom_fusion.1.lab_ref, f32[256,8,128]{2,1,0:T(8,128)} %fusion.contrib_ref), custom_call_target="tpu_custom_call" | custom-call | tf_op jit(solution)/shard_map/pallas_call | solution.py:182
  25.5 11.0 %all-to-all-start = ((f32[64,9,8,128]{3,2,1,0:T(8,128)}), f32[64,9,8,128]{3,2,1,0:T(8,128)S(1)}, u32[]{:S(2)}, u32[]{:S(2)}) async-start(f32[64,9,8,128]{3,2,1,0:T(8,128)} %shard_map.87), calls=%async_computation | async-start | bytes 4718592 | tf_op jit(solution)/shard_map/all_to_all | solution.py:192
  36.6 5.3 %copy.18 = f32[1,64,128,128]{2,1,3,0:T(8,128)} copy(f32[1,64,128,128]{3,2,1,0:T(8,128)} %param.7) | data formatting | bytes 8388608 | tf_op args[0]
  42.0 5.2 %bitcast_multiply_fusion = f32[64,128,128]{1,0,2:T(8,128)} fusion(f32[1,64,128,128]{2,1,3,0:T(8,128)} %copy.18, f32[128,128]{0,1:T(8,128)S(1)} %copy.19), kind=kLoop, calls=%fused_computation.5 | loop fusion | flops 1048576 | bytes 8454144 | tf_op jit(solution)/shard_map/mul | solution.py:203
  47.2 18.2 %all-to-all-done.got_ref = f32[64,9,8,128]{3,2,1,0:T(8,128)S(1)} async-done(((f32[64,9,8,128]{3,2,1,0:T(8,128)}), f32[64,9,8,128]{3,2,1,0:T(8,128)S(1)}, u32[]{:S(2)}, u32[]{:S(2)}) %all-to-all-start) | async-done | bytes 2359328 | tf_op jit(solution)/shard_map/all_to_all | solution.py:192
  67.2 8.4 %shard_map.88 = f32[128,8,128]{2,1,0:T(8,128)} custom-call(s32[512]{0:T(512)} %min.12.rows_ref, f32[64,9,8,128]{3,2,1,0:T(8,128)} %copy-done), custom_call_target="tpu_custom_call" | custom-call | tf_op jit(solution)/shard_map/pallas_call | solution.py:194
  76.9 7.9 %fusion.18 = (f32[64,1,128]{1,0,2:T(8,128)}, f32[64,1,128]{1,0,2:T(8,128)}) fusion(f32[64,128,128]{1,0,2:T(8,128)} %bitcast_multiply_fusion), kind=kLoop, calls=%fused_computation.41 | loop fusion | bytes 131072 | tf_op jit(solution)/shard_map/slice | solution.py:205
  84.8 3.7 %copy.20 = f32[64,1,128]{2,0,1:T(8,128)S(1)} copy(f32[64,1,128]{1,0,2:T(8,128)} %get-tuple-element.15) | data formatting | bytes 65536 | tf_op jit(solution)/shard_map/slice | solution.py:205
  88.6 5.0 %collective-permute-start = (f32[64,128]{1,0:T(8,128)S(1)}, f32[64,128]{1,0:T(8,128)S(1)}, u32[]{:S(2)}, u32[]{:S(2)}) collective-permute-start(f32[64,128]{1,0:T(8,128)S(1)} %bitcast.68), channel_id=1, source_target_pairs={{0,8},{8,16},{16,24},{24,32},{32,40},{40,48},{48,56},{1,9},{9,17},... | collective-permute-start | bytes 98312 | tf_op jit(solution)/shard_map/ppermute | solution.py:118
  93.6 3.7 %copy.21 = f32[64,1,128]{2,0,1:T(8,128)S(1)} copy(f32[64,1,128]{1,0,2:T(8,128)} %get-tuple-element.14) | data formatting | bytes 65536 | tf_op jit(solution)/shard_map/slice | solution.py:205
  97.4 3.2 %collective-permute-start.1 = (f32[64,128]{1,0:T(8,128)S(1)}, f32[64,128]{1,0:T(8,128)S(1)}, u32[]{:S(2)}, u32[]{:S(2)}) collective-permute-start(f32[64,128]{1,0:T(8,128)S(1)} %bitcast.69), channel_id=1, source_target_pairs={{8,0},{16,8},{24,16},{32,24},{40,32},{48,40},{56,48},{9,1},{17,9},... | collective-permute-start | bytes 98312 | tf_op jit(solution)/shard_map/ppermute | solution.py:119
  101.4 4.0 %collective-permute-start.2 = (f32[64,128]{1,0:T(8,128)S(1)}, f32[64,128]{1,0:T(8,128)S(1)}, u32[]{:S(2)}, u32[]{:S(2)}) collective-permute-start(f32[64,128]{1,0:T(8,128)S(1)} %get-tuple-element.13), channel_id=1, source_target_pairs={{0,1},{1,2},{2,3},{3,4},{4,5},{5,6},{6,7},{8,9},{9,10},{10,11},{11... | collective-permute-start | bytes 98312 | tf_op jit(solution)/shard_map/ppermute | solution.py:120
  105.3 2.4 %collective-permute-start.3 = (f32[64,128]{1,0:T(8,128)S(1)}, f32[64,128]{1,0:T(8,128)S(1)}, u32[]{:S(2)}, u32[]{:S(2)}) collective-permute-start(f32[64,128]{1,0:T(8,128)S(1)} %get-tuple-element.12), channel_id=1, source_target_pairs={{1,0},{2,1},{3,2},{4,3},{5,4},{6,5},{7,6},{9,8},{10,9},{11,10},{12... | collective-permute-start | bytes 98312 | tf_op jit(solution)/shard_map/ppermute | solution.py:121
  108.4 4.9 %collective-permute-done.3.he_ref = f32[64,128]{1,0:T(8,128)S(1)} collective-permute-done((f32[64,128]{1,0:T(8,128)S(1)}, f32[64,128]{1,0:T(8,128)S(1)}, u32[]{:S(2)}, u32[]{:S(2)}) %collective-permute-start.3) | collective-permute-done | bytes 32800 | tf_op jit(solution)/shard_map/ppermute | solution.py:121
  113.9 15.9 %shard_map.86 = (f32[64,128,128]{2,1,0:T(8,128)}, f32[64,128]{1,0:T(8,128)}, f32[64,128]{1,0:T(8,128)}, f32[64,128]{1,0:T(8,128)}, f32[64,128]{1,0:T(8,128)}) custom-call(f32[2]{0:T(128)} %pad_maximum_fusion.coef_ref, f32[128,128]{1,0:T(8,128)} %copy-done.1, f32[64,128,128]{2,1,0:T(8,128)} %bitcast.62, f32[64,128,128]{2,1,0:T(8,128)} %bitcast.63, ...), custom_call_target="tpu_custom_call" | custom-call | tf_op jit(solution)/shard_map/pallas_call | solution.py:105
  129.8 3.4 %collective-permute-start.4 = (f32[64,128]{1,0:T(8,128)}, f32[64,128]{1,0:T(8,128)S(1)}, u32[]{:S(2)}, u32[]{:S(2)}) collective-permute-start(f32[64,128]{1,0:T(8,128)} %get-tuple-element.8), channel_id=1, source_target_pairs={{0,8},{8,16},{16,24},{24,32},{32,40},{40,48},{48,56},{1,9},{9,17},... | collective-permute-start | bytes 98312 | tf_op jit(solution)/shard_map/ppermute | solution.py:118
  133.3 4.8 %collective-permute-start.5 = (f32[64,128]{1,0:T(8,128)}, f32[64,128]{1,0:T(8,128)S(1)}, u32[]{:S(2)}, u32[]{:S(2)}) collective-permute-start(f32[64,128]{1,0:T(8,128)} %get-tuple-element.9), channel_id=1, source_target_pairs={{8,0},{16,8},{24,16},{32,24},{40,32},{48,40},{56,48},{9,1},{17,9},... | collective-permute-start | bytes 98312 | tf_op jit(solution)/shard_map/ppermute | solution.py:119
  138.1 1.9 %collective-permute-start.6 = (f32[64,128]{1,0:T(8,128)}, f32[64,128]{1,0:T(8,128)S(1)}, u32[]{:S(2)}, u32[]{:S(2)}) collective-permute-start(f32[64,128]{1,0:T(8,128)} %get-tuple-element.10), channel_id=1, source_target_pairs={{0,1},{1,2},{2,3},{3,4},{4,5},{5,6},{6,7},{8,9},{9,10},{10,11},{11... | collective-permute-start | bytes 98312 | tf_op jit(solution)/shard_map/ppermute | solution.py:120
  140.0 3.9 %collective-permute-start.7 = (f32[64,128]{1,0:T(8,128)}, f32[64,128]{1,0:T(8,128)S(1)}, u32[]{:S(2)}, u32[]{:S(2)}) collective-permute-start(f32[64,128]{1,0:T(8,128)} %get-tuple-element.11), channel_id=1, source_target_pairs={{1,0},{2,1},{3,2},{4,3},{5,4},{6,5},{7,6},{9,8},{10,9},{11,10},{12... | collective-permute-start | bytes 98312 | tf_op jit(solution)/shard_map/ppermute | solution.py:121
  144.6 3.5 %collective-permute-done.7.he_ref = f32[64,128]{1,0:T(8,128)S(1)} collective-permute-done((f32[64,128]{1,0:T(8,128)}, f32[64,128]{1,0:T(8,128)S(1)}, u32[]{:S(2)}, u32[]{:S(2)}) %collective-permute-start.7) | collective-permute-done | bytes 32800 | tf_op jit(solution)/shard_map/ppermute | solution.py:121
  148.7 9.8 %shard_map.89 = f32[64,128,128]{2,1,0:T(8,128)} custom-call(f32[2]{0:T(128)} %pad_maximum_fusion.coef_ref, f32[128,128]{1,0:T(8,128)} %copy-done.1, f32[64,128,128]{2,1,0:T(8,128)} %get-tuple-element.7.u_ref.above_ref.below_ref, f32[64,128,128]{2,1,0:T(8,128)} %get-tuple-element.7.u_ref.above_ref.below_ref, ...), custom_call_target="tpu_custom_call" | custom-call | tf_op jit(solution)/shard_map/pallas_call | solution.py:105
  (50 shorter events, 14.6 us)
Async XLA Ops:
  5.9 30.7 %copy-start.1 = (f32[128,128]{1,0:T(8,128)}, f32[128,128]{1,0:T(8,128)S(1)}, u32[]{:S(2)}) copy-start(f32[128,128]{1,0:T(8,128)S(1)} %convert_select_fusion.wet_ref) | copy-start | bytes 196612
  25.5 39.9 %all-to-all-start = ((f32[64,9,8,128]{3,2,1,0:T(8,128)}), f32[64,9,8,128]{3,2,1,0:T(8,128)S(1)}, u32[]{:S(2)}, u32[]{:S(2)}) async-start(f32[64,9,8,128]{3,2,1,0:T(8,128)} %shard_map.87), calls=%async_computation | async-start | bytes 4718592 | tf_op jit(solution)/shard_map/all_to_all | solution.py:192
  65.4 1.8 %copy-start = (f32[64,9,8,128]{3,2,1,0:T(8,128)}, f32[64,9,8,128]{3,2,1,0:T(8,128)S(1)}, u32[]{:S(2)}) copy-start(f32[64,9,8,128]{3,2,1,0:T(8,128)S(1)} %all-to-all-done.got_ref) | copy-start | bytes 7077892
  76.8 67.1 %collective-permute-start.8 = (f32[8,128,128]{2,1,0:T(8,128)S(1)}, f32[8,128,128]{2,1,0:T(8,128)S(1)}, u32[]{:S(2)}, u32[]{:S(2)}) collective-permute-start(f32[8,128,128]{2,1,0:T(8,128)S(1)} %bitcast.67), channel_id=1, source_target_pairs={{0,64},{64,0},{1,65},{65,1},{2,66},{66,2},{3,67},{67,3},{4,68},{68... | collective-permute-start | bytes 1572872 | tf_op jit(solution)/shard_map/ppermute | solution.py:201
  88.6 19.8 %collective-permute-start = (f32[64,128]{1,0:T(8,128)S(1)}, f32[64,128]{1,0:T(8,128)S(1)}, u32[]{:S(2)}, u32[]{:S(2)}) collective-permute-start(f32[64,128]{1,0:T(8,128)S(1)} %bitcast.68), channel_id=1, source_target_pairs={{0,8},{8,16},{16,24},{24,32},{32,40},{40,48},{48,56},{1,9},{9,17},... | collective-permute-start | bytes 98312 | tf_op jit(solution)/shard_map/ppermute | solution.py:118
  97.4 11.0 %collective-permute-start.1 = (f32[64,128]{1,0:T(8,128)S(1)}, f32[64,128]{1,0:T(8,128)S(1)}, u32[]{:S(2)}, u32[]{:S(2)}) collective-permute-start(f32[64,128]{1,0:T(8,128)S(1)} %bitcast.69), channel_id=1, source_target_pairs={{8,0},{16,8},{24,16},{32,24},{40,32},{48,40},{56,48},{9,1},{17,9},... | collective-permute-start | bytes 98312 | tf_op jit(solution)/shard_map/ppermute | solution.py:119
  101.4 7.0 %collective-permute-start.2 = (f32[64,128]{1,0:T(8,128)S(1)}, f32[64,128]{1,0:T(8,128)S(1)}, u32[]{:S(2)}, u32[]{:S(2)}) collective-permute-start(f32[64,128]{1,0:T(8,128)S(1)} %get-tuple-element.13), channel_id=1, source_target_pairs={{0,1},{1,2},{2,3},{3,4},{4,5},{5,6},{6,7},{8,9},{9,10},{10,11},{11... | collective-permute-start | bytes 98312 | tf_op jit(solution)/shard_map/ppermute | solution.py:120
  105.3 7.9 %collective-permute-start.3 = (f32[64,128]{1,0:T(8,128)S(1)}, f32[64,128]{1,0:T(8,128)S(1)}, u32[]{:S(2)}, u32[]{:S(2)}) collective-permute-start(f32[64,128]{1,0:T(8,128)S(1)} %get-tuple-element.12), channel_id=1, source_target_pairs={{1,0},{2,1},{3,2},{4,3},{5,4},{6,5},{7,6},{9,8},{10,9},{11,10},{12... | collective-permute-start | bytes 98312 | tf_op jit(solution)/shard_map/ppermute | solution.py:121
  108.3 4.9 %copy-start.2 = (f32[64,128]{1,0:T(8,128)}, f32[64,128]{1,0:T(8,128)S(1)}, u32[]{:S(2)}) copy-start(f32[64,128]{1,0:T(8,128)S(1)} %collective-permute-done.hn_ref) | copy-start | bytes 98308
  108.3 4.9 %copy-start.3 = (f32[64,128]{1,0:T(8,128)}, f32[64,128]{1,0:T(8,128)S(1)}, u32[]{:S(2)}) copy-start(f32[64,128]{1,0:T(8,128)S(1)} %collective-permute-done.1.hs_ref) | copy-start | bytes 98308
  108.4 4.9 %copy-start.4 = (f32[64,128]{1,0:T(8,128)}, f32[64,128]{1,0:T(8,128)S(1)}, u32[]{:S(2)}) copy-start(f32[64,128]{1,0:T(8,128)S(1)} %collective-permute-done.2.hw_ref) | copy-start | bytes 98308
  113.3 0.6 copy-start.7
  129.8 14.8 %collective-permute-start.4 = (f32[64,128]{1,0:T(8,128)}, f32[64,128]{1,0:T(8,128)S(1)}, u32[]{:S(2)}, u32[]{:S(2)}) collective-permute-start(f32[64,128]{1,0:T(8,128)} %get-tuple-element.8), channel_id=1, source_target_pairs={{0,8},{8,16},{16,24},{24,32},{32,40},{40,48},{48,56},{1,9},{9,17},... | collective-permute-start | bytes 98312 | tf_op jit(solution)/shard_map/ppermute | solution.py:118
  133.3 11.3 %collective-permute-start.5 = (f32[64,128]{1,0:T(8,128)}, f32[64,128]{1,0:T(8,128)S(1)}, u32[]{:S(2)}, u32[]{:S(2)}) collective-permute-start(f32[64,128]{1,0:T(8,128)} %get-tuple-element.9), channel_id=1, source_target_pairs={{8,0},{16,8},{24,16},{32,24},{40,32},{48,40},{56,48},{9,1},{17,9},... | collective-permute-start | bytes 98312 | tf_op jit(solution)/shard_map/ppermute | solution.py:119
  138.1 6.5 %collective-permute-start.6 = (f32[64,128]{1,0:T(8,128)}, f32[64,128]{1,0:T(8,128)S(1)}, u32[]{:S(2)}, u32[]{:S(2)}) collective-permute-start(f32[64,128]{1,0:T(8,128)} %get-tuple-element.10), channel_id=1, source_target_pairs={{0,1},{1,2},{2,3},{3,4},{4,5},{5,6},{6,7},{8,9},{9,10},{10,11},{11... | collective-permute-start | bytes 98312 | tf_op jit(solution)/shard_map/ppermute | solution.py:120
  140.0 8.1 %collective-permute-start.7 = (f32[64,128]{1,0:T(8,128)}, f32[64,128]{1,0:T(8,128)S(1)}, u32[]{:S(2)}, u32[]{:S(2)}) collective-permute-start(f32[64,128]{1,0:T(8,128)} %get-tuple-element.11), channel_id=1, source_target_pairs={{1,0},{2,1},{3,2},{4,3},{5,4},{6,5},{7,6},{9,8},{10,9},{11,10},{12... | collective-permute-start | bytes 98312 | tf_op jit(solution)/shard_map/ppermute | solution.py:121
  144.6 3.6 %copy-start.5 = (f32[64,128]{1,0:T(8,128)}, f32[64,128]{1,0:T(8,128)S(1)}, u32[]{:S(2)}) copy-start(f32[64,128]{1,0:T(8,128)S(1)} %collective-permute-done.4.hn_ref) | copy-start | bytes 98308
  144.6 3.5 %copy-start.6 = (f32[64,128]{1,0:T(8,128)}, f32[64,128]{1,0:T(8,128)S(1)}, u32[]{:S(2)}) copy-start(f32[64,128]{1,0:T(8,128)S(1)} %collective-permute-done.5.hs_ref) | copy-start | bytes 98308
  144.6 3.5 %copy-start.8 = (f32[64,128]{1,0:T(8,128)}, f32[64,128]{1,0:T(8,128)S(1)}, u32[]{:S(2)}) copy-start(f32[64,128]{1,0:T(8,128)S(1)} %collective-permute-done.6.hw_ref) | copy-start | bytes 98308
  148.1 0.6 copy-start.9

commit v2 on v1

--- a/solution.py
+++ b/solution.py
@@ -45,6 +45,10 @@
             qw_ref[...] = jnp.zeros_like(qw_ref)
             qe_ref[...] = jnp.zeros_like(qe_ref)
 
+    if with_edges:
+        lane = lax.broadcasted_iota(jnp.int32, qw_ref.shape, 1)
+        qw = qw_ref[...]
+        qe = qe_ref[...]
     for l in range(LB):
         u = u_ref[l]
         prev = u_ref[l - 1] if l > 0 else above
@@ -64,17 +68,85 @@
             fw = wet * res
             en_ref[l:l + 1, :] = fw[0:1, :]
             es_ref[l:l + 1, :] = fw[rows - 1:rows, :]
-            lane = lax.broadcasted_iota(jnp.int32, qw_ref.shape, 1)
             hit = lane == i * LB + l
-            qw_ref[...] = jnp.where(hit, fw[:, 0:1], qw_ref[...])
-            qe_ref[...] = jnp.where(hit, fw[:, cols - 1:cols], qe_ref[...])
-
-    if with_edges:
+            qw = jnp.where(hit, fw[:, 0:1], qw)
+            qe = jnp.where(hit, fw[:, cols - 1:cols], qe)
+
+    if with_edges:
+        qw_ref[...] = qw
+        qe_ref[...] = qe
+
         @pl.when(i == nblk - 1)
         def _():
             lev = ew_ref.shape[0]
             ew_ref[...] = jnp.transpose(qw_ref[...])[0:lev, :]
             ee_ref[...] = jnp.transpose(qe_ref[...])[0:lev, :]
+
+
+def edges_kernel(wet_ref, u_ref, en_ref, es_ref, ew_ref, ee_ref, qw_ref, qe_ref):
+    i = pl.program_id(0)
+    nblk = pl.num_programs(0)
+    wet = wet_ref[...]
+    rows, cols = wet.shape
+
+    @pl.when(i == 0)
+    def _():
+        qw_ref[...] = jnp.zeros_like(qw_ref)
+        qe_ref[...] = jnp.zeros_like(qe_ref)
+
+    lane = lax.broadcasted_iota(jnp.int32, qw_ref.shape, 1)
+    qw = qw_ref[...]
+    qe = qe_ref[...]
+    for l in range(LB):
+        fw = wet * u_ref[l]
+        en_ref[l:l + 1, :] = fw[0:1, :]
+        es_ref[l:l + 1, :] = fw[rows - 1:rows, :]
+        hit = lane == i * LB + l
+        qw = jnp.where(hit, fw[:, 0:1], qw)
+        qe = jnp.where(hit, fw[:, cols - 1:cols], qe)
+    qw_ref[...] = qw
+    qe_ref[...] = qe
+
+    @pl.when(i == nblk - 1)
+    def _():
+        lev = ew_ref.shape[0]
+        ew_ref[...] = jnp.transpose(qw_ref[...])[0:lev, :]
+        ee_ref[...] = jnp.transpose(qe_ref[...])[0:lev, :]
+
+
+def masked_edges(wet, u):
+    lev, rows, cols = u.shape
+    lvl2 = pl.BlockSpec((LB, cols), lambda i: (i, 0))
+    full2 = lambda shape: pl.BlockSpec(shape, lambda i: (0, 0))
+    return pl.pallas_call(
+        edges_kernel,
+        grid=(lev // LB,),
+        in_specs=[full2((rows, cols)), pl.BlockSpec((LB, rows, cols), lambda i: (i, 0, 0))],
+        out_specs=[lvl2, lvl2, full2((lev, rows)), full2((lev, rows))],
+        out_shape=[jax.ShapeDtypeStruct((lev, cols), jnp.float32)] * 2
+        + [jax.ShapeDtypeStruct((lev, rows), jnp.float32)] * 2,
+        scratch_shapes=[pltpu.VMEM((rows, 128), jnp.float32)] * 2,
+        compiler_params=pltpu.CompilerParams(dimension_semantics=("arbitrary",)),
+        cost_estimate=pl.CostEstimate(flops=2 * u.size, bytes_accessed=4 * u.size, transcendentals=0),
+    )(wet, u)
+
+
+def force_kernel(x_ref, wet_ref, f_ref, out_ref):
+    out_ref[0] = x_ref[0] + force_gain * wet_ref[...] * f_ref[...]
+
+
+def add_force(x, wet, f):
+    lev, rows, cols = x.shape
+    plane = pl.BlockSpec((rows, cols), lambda i: (0, 0))
+    level0 = pl.BlockSpec((1, rows, cols), lambda i: (0, 0, 0))
+    return pl.pallas_call(
+        force_kernel,
+        grid=(1,),
+        in_specs=[level0, plane, plane],
+        out_specs=level0,
+        out_shape=jax.ShapeDtypeStruct(x.shape, x.dtype),
+        input_output_aliases={0: 0},
+    )(x, wet, f)
 
 
 def stencil_step(coef, wet, u, halos, force=None, with_edges=False):
@@ -110,6 +182,7 @@
         out_shape=out_shape,
         scratch_shapes=scratch,
         compiler_params=pltpu.CompilerParams(dimension_semantics=("arbitrary",)),
+        cost_estimate=pl.CostEstimate(flops=30 * u.size, bytes_accessed=12 * u.size, transcendentals=0),
     )(*args)
 
 
@@ -138,18 +211,6 @@
         return carry
 
     lax.fori_loop(0, ndest, body, 0)
-
-
-def recv_kernel(rows_ref, got_ref, acc_ref):
-    acc_ref[...] = jnp.zeros_like(acc_ref)
-    nslots = got_ref.shape[0] * CAP
-
-    def body(s, carry):
-        r = rows_ref[s]
-        acc_ref[r] = acc_ref[r] + got_ref[s // CAP, s % CAP]
-        return carry
-
-    lax.fori_loop(0, nslots, body, 0)
 
 
 def local(states, surface, land_mask, tile_weights, tile_source, tile_target, tile_row):
@@ -190,23 +251,20 @@
         out_shape=jax.ShapeDtypeStruct((ndev, CAP + 1, KF, CY), jnp.float32),
     )(inv, labels, contrib)
     arrived = lax.all_to_all(buckets, ("gx", "gy"), split_axis=0, concat_axis=0, tiled=True)
-    got_rows = jnp.clip(arrived[:, CAP, :, 0].astype(jnp.int32), 0, rows_here - 1).reshape(-1)
-    acc = pl.pallas_call(
-        recv_kernel,
-        in_specs=[pl.BlockSpec(memory_space=pltpu.SMEM), pl.BlockSpec(memory_space=pltpu.VMEM)],
-        out_specs=pl.BlockSpec(memory_space=pltpu.VMEM),
-        out_shape=jax.ShapeDtypeStruct((rows_here, KF, CY), jnp.float32),
-    )(got_rows, arrived)
-    sent = jnp.transpose(acc, (1, 0, 2))
+    got_rows = arrived[:, CAP, :, 0].astype(jnp.int32)
+    select = (
+        got_rows[:, :, None] == jnp.arange(rows_here, dtype=jnp.int32)[None, None, :]
+    ).astype(jnp.float32)
+    sent = jnp.einsum(
+        "scr,sckj->krj", select, arrived[:, :CAP], precision=lax.Precision.HIGHEST
+    )
     received = lax.ppermute(sent, "mp", [(0, 1), (1, 0)])
 
-    w0 = state * wet[None]
-    halos0 = exchange(
-        w0[:, 0, :], w0[:, rows_here - 1, :], w0[:, :, 0], w0[:, :, cols_here - 1]
-    )
+    halos0 = exchange(*masked_edges(wet, state))
     first, en, es, ew, ee = stencil_step(coef, wet, state, halos0, with_edges=True)
     halos1 = exchange(en, es, ew, ee)
-    (second,) = stencil_step(coef, wet, first, halos1, force=received[0])
+    (second,) = stencil_step(coef, wet, first, halos1)
+    second = add_force(second, wet, received[0])
     return (second[None], received[None])
 
 

time: 160 us -> 146 us (0.912)
  blocking collectives: 0 us -> 41.2 us
  local copies, waits for them, and re-layouts: 31.2 us -> 8.16 us
  waiting for transfers between devices: 26.6 us -> 9.42 us
  starting transfers between devices: 39.7 us -> 28.3 us
  other arithmetic: 13.4 us -> 7.05 us
  matrix products: 8.82 us -> 11 us
    all_to_all x0 -> x1, blocking collectives: none -> 41.2 us  [local(): lax.all_to_all(buckets, ('gx', 'gy'), split_axis=0, concat_axis=0, tiled=...]
    all_to_all x1 -> x0, waiting for transfers between devices: 18.2 us -> none  [local(): lax.all_to_all(buckets, ('gx', 'gy'), split_axis=0, concat_axis=0, tiled=...]
    slice x4 -> x2, local copies, waits for them, and re-layouts: 15.6 us -> 0.47 us  [the longest x1 0.29 us: local(): arrived[:, :CAP]]
    all_to_all x1 -> x0, starting transfers between devices: 11 us -> none  [local(): lax.all_to_all(buckets, ('gx', 'gy'), split_axis=0, concat_axis=0, tiled=...]
    unnamed x22 -> x19, local copies, waits for them, and re-layouts: 7.36 us -> 2.02 us
    mul x1 -> x0, other arithmetic: 5.23 us -> none  [local(): w0 = state * wet[None]]
    dot_general x0 -> x1, matrix products: none -> 2.14 us  [local(): jnp.einsum('scr,sckj->krj', select, arrived[:, :CAP], precision=lax.Preci...]
    pallas_call x1 -> x2, Pallas kernels: 8.43 us -> 8.66 us  [the longest x1 7.12 us: masked_edges(): pl.pallas_call(edges_kernel, grid=(lev // LB,), in_specs=[full2((rows, co...]
  transfers between devices with their start and end apart: 10 -> 9, of which waited for: 3 -> 3; matrix products, arithmetic and copies ran while one was open for 18% -> 0% of each run, Pallas kernels for 10% -> 23%
where the time goes in v2:
time: 146 us; the launch traced here: 145 us
  blocking collectives  41.2 us (28%)
  Pallas kernels  38.9 us (27%)
  starting transfers between devices  28.3 us (19%)
  matrix products  11 us (8%)
  waiting for transfers between devices  9.42 us (6%)
  local copies, waits for them, and re-layouts  8.16 us (6%)
  other arithmetic  7.05 us (5%)
    all_to_all x1, blocking collectives, local(): lax.all_to_all(buckets, ('gx', 'gy'), split_axis=0, concat_axis=0, tiled=...  41.2 us
    pallas_call x2, Pallas kernels, stencil_step(): pl.pallas_call(functools.partial(stencil_kernel, with_edges, force is not...  25.8 us
    ppermute x2, starting transfers between devices, exchange(): hs = lax.ppermute(en, 'gx', shift_pairs(ngx, False))  9.58 us
    ppermute x2, waiting for transfers between devices, exchange(): he = lax.ppermute(ew, 'gy', shift_pairs(ngy, False))  9.28 us
    dot_general x1, matrix products, local(): jnp.einsum('tji,kti->tkj', tile_weights[0, 0, 0], picked, preferred_eleme...  8.81 us
    pallas_call x1, Pallas kernels, masked_edges(): pl.pallas_call(edges_kernel, grid=(lev // LB,), in_specs=[full2((rows, co...  7.12 us
    ppermute x2, starting transfers between devices, exchange(): hn = lax.ppermute(es, 'gx', shift_pairs(ngx, True))  6.91 us
    ppermute x2, starting transfers between devices, exchange(): he = lax.ppermute(ew, 'gy', shift_pairs(ngy, False))  6.14 us
  transfers between devices with their start and end apart: 9, of which 3 were waited for; matrix products, arithmetic and copies ran while one was open for 0% of the time, Pallas kernels for 23%

profile of v2, /device:TPU:38, one launch (start us, length us, event | category | flops | bytes accessed | tf_op | source)
XLA Modules:
  0.0 144.8 jit_solution(18234193482468168113)
XLA Ops:
  5.0 0.8 convert_select_fusion.wet_ref
  5.9 1.4 fusion.8
  7.3 0.8 gather_fusion
  8.1 2.1 %scatter_custom_fusion.1.lab_ref = s32[512]{0:T(512)} fusion(s32[256]{0:T(256)S(1)} %bitcast.68, s32[256]{0:T(256)} %bitcast.71, s32[]{:T(128)} %constant.15.clone.1), kind=kCustom, calls=%fused_computation.35 | custom fusion | bytes 2560 | tf_op jit(solution)/shard_map/scatter | solution.py:242
  10.2 2.0 %scatter_custom_fusion.inv_ref = s32[512]{0:T(512)} fusion(s32[256]{0:T(256)S(1)} %bitcast.69, s32[256]{0:T(256)S(1)} %iota.15, s32[]{:T(128)} %constant.24.clone.1), kind=kCustom, calls=%fused_computation.37 | custom fusion | bytes 2052 | tf_op jit(solution)/shard_map/scatter | solution.py:241
  12.2 8.8 %fusion.contrib_ref = f32[256,8,128]{2,1,0:T(8,128)} fusion(bf16[1,1,1,256,128,128]{5,4,3,2,1,0:T(8,128)(2,1)} %param.10, bf16[256,8,128]{2,1,0:T(8,128)(2,1)S(1)} %gather_fusion, pred[256]{0:T(512)(128)(4,1)S(1)} %compare_and_fusion), kind=kOutput, calls=%fused_computation.3 | convolution fusion | flops 67371008 | bytes 9961728 | tf_op jit(solution)/shard_map/tji,kti->tkj/dot_general | solution.py:234
  21.0 4.5 %shard_map.89 = f32[64,9,8,128]{3,2,1,0:T(8,128)} custom-call(s32[512]{0:T(512)} %scatter_custom_fusion.inv_ref, s32[512]{0:T(512)} %scatter_custom_fusion.1.lab_ref, f32[256,8,128]{2,1,0:T(8,128)} %fusion.contrib_ref), custom_call_target="tpu_custom_call" | custom-call | tf_op jit(solution)/shard_map/pallas_call | solution.py:243
  25.5 41.2 %all_to_all.5 = f32[64,9,8,128]{3,2,1,0:T(8,128)S(1)} all-to-all(f32[64,9,8,128]{3,2,1,0:T(8,128)} %shard_map.89), channel_id=1, replica_groups=mesh['mp'=2,'gx'=8,'gy'=8] {'gx','gy'}, dimensions={0} | all-to-all | bytes 4718592 | tf_op jit(solution)/shard_map/all_to_all | solution.py:253
  67.2 2.1 %fusion.4 = f32[8,128,128]{2,1,0:T(8,128)S(1)} fusion(f32[64,8,8,128]{3,2,1,0:T(8,128)S(1)} %slice.23, s32[64,8]{0,1:T(8,128)S(1)} %bitcast.63), kind=kOutput, calls=%fused_computation.7 | convolution fusion | flops 805371904 | bytes 2623488 | tf_op jit(solution)/shard_map/scr,sckj->krj/dot_general | solution.py:258
  69.4 7.1 %shard_map.86 = (f32[64,128]{1,0:T(8,128)}, f32[64,128]{1,0:T(8,128)}, f32[64,128]{1,0:T(8,128)}, f32[64,128]{1,0:T(8,128)}) custom-call(f32[128,128]{1,0:T(8,128)} %copy-done, f32[64,128,128]{2,1,0:T(8,128)} %bitcast.57), custom_call_target="tpu_custom_call" | custom-call | flops 2097152 | bytes 4194304 | tf_op jit(solution)/shard_map/pallas_call | solution.py:121
  76.5 3.5 %collective-permute-start = (f32[64,128]{1,0:T(8,128)}, f32[64,128]{1,0:T(8,128)S(1)}, u32[]{:S(2)}, u32[]{:S(2)}) collective-permute-start(f32[64,128]{1,0:T(8,128)} %get-tuple-element.11), channel_id=1, source_target_pairs={{0,8},{8,16},{16,24},{24,32},{32,40},{40,48},{48,56},{1,9},{9,17},... | collective-permute-start | bytes 98312 | tf_op jit(solution)/shard_map/ppermute | solution.py:191
  80.1 4.7 %collective-permute-start.1 = (f32[64,128]{1,0:T(8,128)}, f32[64,128]{1,0:T(8,128)S(1)}, u32[]{:S(2)}, u32[]{:S(2)}) collective-permute-start(f32[64,128]{1,0:T(8,128)} %get-tuple-element.12), channel_id=1, source_target_pairs={{8,0},{16,8},{24,16},{32,24},{40,32},{48,40},{56,48},{9,1},{17,9},... | collective-permute-start | bytes 98312 | tf_op jit(solution)/shard_map/ppermute | solution.py:192
  84.8 3.6 %collective-permute-start.2 = (f32[64,128]{1,0:T(8,128)}, f32[64,128]{1,0:T(8,128)S(1)}, u32[]{:S(2)}, u32[]{:S(2)}) collective-permute-start(f32[64,128]{1,0:T(8,128)} %get-tuple-element.13), channel_id=1, source_target_pairs={{0,1},{1,2},{2,3},{3,4},{4,5},{5,6},{6,7},{8,9},{9,10},{10,11},{11... | collective-permute-start | bytes 98312 | tf_op jit(solution)/shard_map/ppermute | solution.py:193
  88.4 2.2 %collective-permute-start.3 = (f32[64,128]{1,0:T(8,128)}, f32[64,128]{1,0:T(8,128)S(1)}, u32[]{:S(2)}, u32[]{:S(2)}) collective-permute-start(f32[64,128]{1,0:T(8,128)} %get-tuple-element.14), channel_id=1, source_target_pairs={{1,0},{2,1},{3,2},{4,3},{5,4},{6,5},{7,6},{9,8},{10,9},{11,10},{12... | collective-permute-start | bytes 98312 | tf_op jit(solution)/shard_map/ppermute | solution.py:194
  91.3 5.2 %collective-permute-done.3.he_ref = f32[64,128]{1,0:T(8,128)S(1)} collective-permute-done((f32[64,128]{1,0:T(8,128)}, f32[64,128]{1,0:T(8,128)S(1)}, u32[]{:S(2)}, u32[]{:S(2)}) %collective-permute-start.3) | collective-permute-done | bytes 32800 | tf_op jit(solution)/shard_map/ppermute | solution.py:194
  97.2 15.9 %shard_map.87 = (f32[64,128,128]{2,1,0:T(8,128)}, f32[64,128]{1,0:T(8,128)}, f32[64,128]{1,0:T(8,128)}, f32[64,128]{1,0:T(8,128)}, f32[64,128]{1,0:T(8,128)}) custom-call(f32[2]{0:T(128)} %pad_maximum_fusion.coef_ref, f32[128,128]{1,0:T(8,128)} %copy-done, f32[64,128,128]{2,1,0:T(8,128)} %bitcast.58, f32[64,128,128]{2,1,0:T(8,128)} %bitcast.59, ...), custom_call_target="tpu_custom_call" | custom-call | flops 31457280 | bytes 12582912 | tf_op jit(solution)/shard_map/pallas_call | solution.py:177
  113.1 3.4 %collective-permute-start.4 = (f32[64,128]{1,0:T(8,128)}, f32[64,128]{1,0:T(8,128)S(1)}, u32[]{:S(2)}, u32[]{:S(2)}) collective-permute-start(f32[64,128]{1,0:T(8,128)} %get-tuple-element.16), channel_id=1, source_target_pairs={{0,8},{8,16},{16,24},{24,32},{32,40},{40,48},{48,56},{1,9},{9,17},... | collective-permute-start | bytes 98312 | tf_op jit(solution)/shard_map/ppermute | solution.py:191
  116.5 4.9 %collective-permute-start.5 = (f32[64,128]{1,0:T(8,128)}, f32[64,128]{1,0:T(8,128)S(1)}, u32[]{:S(2)}, u32[]{:S(2)}) collective-permute-start(f32[64,128]{1,0:T(8,128)} %get-tuple-element.17), channel_id=1, source_target_pairs={{8,0},{16,8},{24,16},{32,24},{40,32},{48,40},{56,48},{9,1},{17,9},... | collective-permute-start | bytes 98312 | tf_op jit(solution)/shard_map/ppermute | solution.py:192
  121.4 1.9 %collective-permute-start.6 = (f32[64,128]{1,0:T(8,128)}, f32[64,128]{1,0:T(8,128)S(1)}, u32[]{:S(2)}, u32[]{:S(2)}) collective-permute-start(f32[64,128]{1,0:T(8,128)} %get-tuple-element.18), channel_id=1, source_target_pairs={{0,1},{1,2},{2,3},{3,4},{4,5},{5,6},{6,7},{8,9},{9,10},{10,11},{11... | collective-permute-start | bytes 98312 | tf_op jit(solution)/shard_map/ppermute | solution.py:193
  123.3 3.9 %collective-permute-start.7 = (f32[64,128]{1,0:T(8,128)}, f32[64,128]{1,0:T(8,128)S(1)}, u32[]{:S(2)}, u32[]{:S(2)}) collective-permute-start(f32[64,128]{1,0:T(8,128)} %get-tuple-element.19), channel_id=1, source_target_pairs={{1,0},{2,1},{3,2},{4,3},{5,4},{6,5},{7,6},{9,8},{10,9},{11,10},{12... | collective-permute-start | bytes 98312 | tf_op jit(solution)/shard_map/ppermute | solution.py:194
  127.4 4.0 %collective-permute-done.7.he_ref = f32[64,128]{1,0:T(8,128)S(1)} collective-permute-done((f32[64,128]{1,0:T(8,128)}, f32[64,128]{1,0:T(8,128)S(1)}, u32[]{:S(2)}, u32[]{:S(2)}) %collective-permute-start.7) | collective-permute-done | bytes 32800 | tf_op jit(solution)/shard_map/ppermute | solution.py:194
  132.0 9.8 %shard_map.88.x_ref = f32[64,128,128]{2,1,0:T(8,128)} custom-call(f32[2]{0:T(128)} %pad_maximum_fusion.coef_ref, f32[128,128]{1,0:T(8,128)} %copy-done, f32[64,128,128]{2,1,0:T(8,128)} %get-tuple-element.15.u_ref.above_ref.below_ref, f32[64,128,128]{2,1,0:T(8,128)} %get-tuple-element.15.u_ref.above_ref.below_ref, ...), custom_call_target="tpu_custom_call" | custom-call | flops 31457280 | bytes 12582912 | tf_op jit(solution)/shard_map/pallas_call | solution.py:177
  142.5 1.5 %shard_map.90 = f32[64,128,128]{2,1,0:T(8,128)} custom-call(f32[64,128,128]{2,1,0:T(8,128)} %shard_map.88.x_ref, f32[128,128]{1,0:T(8,128)} %copy-done, f32[128,128]{1,0:T(8,128)} %slice_bitcast_fusion.f_ref), custom_call_target="tpu_custom_call", output_to_operand_aliasing={{}: (0, {})} | custom-call | tf_op jit(solution)/shard_map/pallas_call | solution.py:142
  144.0 0.8 copy.35
  (42 shorter events, 7.5 us)
Async XLA Ops:
  5.9 15.1 %copy-start = (f32[128,128]{1,0:T(8,128)}, f32[128,128]{1,0:T(8,128)S(1)}, u32[]{:S(2)}) copy-start(f32[128,128]{1,0:T(8,128)S(1)} %convert_select_fusion.wet_ref) | copy-start | bytes 196612
  69.3 72.5 %collective-permute-start.8 = (f32[8,128,128]{2,1,0:T(8,128)S(1)}, f32[8,128,128]{2,1,0:T(8,128)S(1)}, u32[]{:S(2)}, u32[]{:S(2)}) collective-permute-start(f32[8,128,128]{2,1,0:T(8,128)S(1)} %fusion.4), channel_id=1, source_target_pairs={{0,64},{64,0},{1,65},{65,1},{2,66},{66,2},{3,67},{67,3},{4,68},{68... | collective-permute-start | bytes 1572872 | tf_op jit(solution)/shard_map/ppermute | solution.py:261
  76.5 14.7 %collective-permute-start = (f32[64,128]{1,0:T(8,128)}, f32[64,128]{1,0:T(8,128)S(1)}, u32[]{:S(2)}, u32[]{:S(2)}) collective-permute-start(f32[64,128]{1,0:T(8,128)} %get-tuple-element.11), channel_id=1, source_target_pairs={{0,8},{8,16},{16,24},{24,32},{32,40},{40,48},{48,56},{1,9},{9,17},... | collective-permute-start | bytes 98312 | tf_op jit(solution)/shard_map/ppermute | solution.py:191
  80.1 11.2 %collective-permute-start.1 = (f32[64,128]{1,0:T(8,128)}, f32[64,128]{1,0:T(8,128)S(1)}, u32[]{:S(2)}, u32[]{:S(2)}) collective-permute-start(f32[64,128]{1,0:T(8,128)} %get-tuple-element.12), channel_id=1, source_target_pairs={{8,0},{16,8},{24,16},{32,24},{40,32},{48,40},{56,48},{9,1},{17,9},... | collective-permute-start | bytes 98312 | tf_op jit(solution)/shard_map/ppermute | solution.py:192
  84.8 6.5 %collective-permute-start.2 = (f32[64,128]{1,0:T(8,128)}, f32[64,128]{1,0:T(8,128)S(1)}, u32[]{:S(2)}, u32[]{:S(2)}) collective-permute-start(f32[64,128]{1,0:T(8,128)} %get-tuple-element.13), channel_id=1, source_target_pairs={{0,1},{1,2},{2,3},{3,4},{4,5},{5,6},{6,7},{8,9},{9,10},{10,11},{11... | collective-permute-start | bytes 98312 | tf_op jit(solution)/shard_map/ppermute | solution.py:193
  88.4 8.1 %collective-permute-start.3 = (f32[64,128]{1,0:T(8,128)}, f32[64,128]{1,0:T(8,128)S(1)}, u32[]{:S(2)}, u32[]{:S(2)}) collective-permute-start(f32[64,128]{1,0:T(8,128)} %get-tuple-element.14), channel_id=1, source_target_pairs={{1,0},{2,1},{3,2},{4,3},{5,4},{6,5},{7,6},{9,8},{10,9},{11,10},{12... | collective-permute-start | bytes 98312 | tf_op jit(solution)/shard_map/ppermute | solution.py:194
  91.3 5.3 %copy-start.1 = (f32[64,128]{1,0:T(8,128)}, f32[64,128]{1,0:T(8,128)S(1)}, u32[]{:S(2)}) copy-start(f32[64,128]{1,0:T(8,128)S(1)} %collective-permute-done.hn_ref) | copy-start | bytes 98308
  91.3 5.3 %copy-start.2 = (f32[64,128]{1,0:T(8,128)}, f32[64,128]{1,0:T(8,128)S(1)}, u32[]{:S(2)}) copy-start(f32[64,128]{1,0:T(8,128)S(1)} %collective-permute-done.1.hs_ref) | copy-start | bytes 98308
  91.3 5.3 %copy-start.3 = (f32[64,128]{1,0:T(8,128)}, f32[64,128]{1,0:T(8,128)S(1)}, u32[]{:S(2)}) copy-start(f32[64,128]{1,0:T(8,128)S(1)} %collective-permute-done.2.hw_ref) | copy-start | bytes 98308
  96.6 0.6 copy-start.4
  113.1 14.1 %collective-permute-start.4 = (f32[64,128]{1,0:T(8,128)}, f32[64,128]{1,0:T(8,128)S(1)}, u32[]{:S(2)}, u32[]{:S(2)}) collective-permute-start(f32[64,128]{1,0:T(8,128)} %get-tuple-element.16), channel_id=1, source_target_pairs={{0,8},{8,16},{16,24},{24,32},{32,40},{40,48},{48,56},{1,9},{9,17},... | collective-permute-start | bytes 98312 | tf_op jit(solution)/shard_map/ppermute | solution.py:191
  116.5 10.8 %collective-permute-start.5 = (f32[64,128]{1,0:T(8,128)}, f32[64,128]{1,0:T(8,128)S(1)}, u32[]{:S(2)}, u32[]{:S(2)}) collective-permute-start(f32[64,128]{1,0:T(8,128)} %get-tuple-element.17), channel_id=1, source_target_pairs={{8,0},{16,8},{24,16},{32,24},{40,32},{48,40},{56,48},{9,1},{17,9},... | collective-permute-start | bytes 98312 | tf_op jit(solution)/shard_map/ppermute | solution.py:192
  121.4 6.0 %collective-permute-start.6 = (f32[64,128]{1,0:T(8,128)}, f32[64,128]{1,0:T(8,128)S(1)}, u32[]{:S(2)}, u32[]{:S(2)}) collective-permute-start(f32[64,128]{1,0:T(8,128)} %get-tuple-element.18), channel_id=1, source_target_pairs={{0,1},{1,2},{2,3},{3,4},{4,5},{5,6},{6,7},{8,9},{9,10},{10,11},{11... | collective-permute-start | bytes 98312 | tf_op jit(solution)/shard_map/ppermute | solution.py:193
  123.3 8.1 %collective-permute-start.7 = (f32[64,128]{1,0:T(8,128)}, f32[64,128]{1,0:T(8,128)S(1)}, u32[]{:S(2)}, u32[]{:S(2)}) collective-permute-start(f32[64,128]{1,0:T(8,128)} %get-tuple-element.19), channel_id=1, source_target_pairs={{1,0},{2,1},{3,2},{4,3},{5,4},{6,5},{7,6},{9,8},{10,9},{11,10},{12... | collective-permute-start | bytes 98312 | tf_op jit(solution)/shard_map/ppermute | solution.py:194
  127.2 4.2 %copy-start.5 = (f32[64,128]{1,0:T(8,128)}, f32[64,128]{1,0:T(8,128)S(1)}, u32[]{:S(2)}) copy-start(f32[64,128]{1,0:T(8,128)S(1)} %collective-permute-done.4.hn_ref) | copy-start | bytes 98308
  127.3 4.2 %copy-start.6 = (f32[64,128]{1,0:T(8,128)}, f32[64,128]{1,0:T(8,128)S(1)}, u32[]{:S(2)}) copy-start(f32[64,128]{1,0:T(8,128)S(1)} %collective-permute-done.5.hs_ref) | copy-start | bytes 98308
  127.4 4.0 %copy-start.7 = (f32[64,128]{1,0:T(8,128)}, f32[64,128]{1,0:T(8,128)S(1)}, u32[]{:S(2)}) copy-start(f32[64,128]{1,0:T(8,128)S(1)} %collective-permute-done.6.hw_ref) | copy-start | bytes 98308
  131.4 0.6 copy-start.8

commit v3 on v2

--- a/solution.py
+++ b/solution.py
@@ -186,13 +186,74 @@
     )(*args)
 
 
-def exchange(en, es, ew, ee):
-    ngx, ngy = lax.axis_size("gx"), lax.axis_size("gy")
-    hn = lax.ppermute(es, "gx", shift_pairs(ngx, True))
-    hs = lax.ppermute(en, "gx", shift_pairs(ngx, False))
-    hw = lax.ppermute(ee, "gy", shift_pairs(ngy, True))
-    he = lax.ppermute(ew, "gy", shift_pairs(ngy, False))
-    return hn, hs, hw, he
+def halo_kernel(en_ref, es_ref, ew_ref, ee_ref, hn_ref, hs_ref, hw_ref, he_ref,
+                buf, send_sem, recv_sem):
+    mp = lax.axis_index("mp")
+    gx = lax.axis_index("gx")
+    gy = lax.axis_index("gy")
+    ngx = lax.axis_size("gx")
+    ngy = lax.axis_size("gy")
+    mesh_id = pl.DeviceIdType.MESH
+    links = [
+        (gx < ngx - 1, (mp, gx + 1, gy), es_ref, 0),
+        (gx > 0, (mp, gx - 1, gy), en_ref, 1),
+        (gy < ngy - 1, (mp, gx, gy + 1), ee_ref, 2),
+        (gy > 0, (mp, gx, gy - 1), ew_ref, 3),
+    ]
+    barrier = pltpu.get_barrier_semaphore()
+    count = jnp.int32(0)
+    for present, dev, _, _ in links:
+        @pl.when(present)
+        def _():
+            pl.semaphore_signal(barrier, 1, device_id=dev, device_id_type=mesh_id)
+
+        count = count + present.astype(jnp.int32)
+    pl.semaphore_wait(barrier, count)
+
+    copies = []
+    for present, dev, src, slot in links:
+        copy = pltpu.make_async_remote_copy(
+            src_ref=src,
+            dst_ref=buf.at[slot],
+            send_sem=send_sem.at[slot],
+            recv_sem=recv_sem.at[slot],
+            device_id=dev,
+            device_id_type=mesh_id,
+        )
+        pl.when(present)(copy.start)
+        copies.append((present, copy))
+    for present, copy in copies:
+        pl.when(present)(copy.wait_send)
+    fills = [gx > 0, gx < ngx - 1, gy > 0, gy < ngy - 1]
+    outs = [hn_ref, hs_ref, hw_ref, he_ref]
+    for slot, (filled, out) in enumerate(zip(fills, outs)):
+        _, copy = copies[slot]
+
+        @pl.when(filled)
+        def _():
+            copy.wait_recv()
+            out[...] = buf[slot]
+
+        @pl.when(jnp.logical_not(filled))
+        def _():
+            out[...] = jnp.zeros_like(out)
+
+
+def exchange(en, es, ew, ee, call):
+    shape = jax.ShapeDtypeStruct(en.shape, en.dtype)
+    vmem = pl.BlockSpec(memory_space=pltpu.VMEM)
+    return pl.pallas_call(
+        halo_kernel,
+        in_specs=[vmem] * 4,
+        out_specs=[vmem] * 4,
+        out_shape=[shape] * 4,
+        scratch_shapes=[
+            pltpu.VMEM((4,) + en.shape, en.dtype),
+            pltpu.SemaphoreType.DMA((4,)),
+            pltpu.SemaphoreType.DMA((4,)),
+        ],
+        compiler_params=pltpu.CompilerParams(collective_id=call, has_side_effects=True),
+    )(en, es, ew, ee)
 
 
 def bucket_kernel(inv_ref, lab_ref, contrib_ref, out_ref):
@@ -260,9 +321,9 @@
     )
     received = lax.ppermute(sent, "mp", [(0, 1), (1, 0)])
 
-    halos0 = exchange(*masked_edges(wet, state))
+    halos0 = exchange(*masked_edges(wet, state), 0)
     first, en, es, ew, ee = stencil_step(coef, wet, state, halos0, with_edges=True)
-    halos1 = exchange(en, es, ew, ee)
+    halos1 = exchange(en, es, ew, ee, 1)
     (second,) = stencil_step(coef, wet, first, halos1)
     second = add_force(second, wet, received[0])
     return (second[None], received[None])

time: 146 us -> 127 us (0.87)
  the two profiles are of different devices: /device:TPU:38 before, /device:TPU:16 now
where the time goes in v3:
time: 127 us; the launch traced here: 125 us
  Pallas kernels  56.7 us (45%)
  blocking collectives  42.1 us (33%)
  matrix products  11 us (9%)
  other arithmetic  7.11 us (6%)
  local copies, waits for them, and re-layouts  6.94 us (5%)
    all_to_all x1, blocking collectives, local(): lax.all_to_all(buckets, ('gx', 'gy'), split_axis=0, concat_axis=0, tiled=...  42.1 us
    pallas_call x2, Pallas kernels, stencil_step(): pl.pallas_call(functools.partial(stencil_kernel, with_edges, force is not...  25.8 us
    pallas_call x2, Pallas kernels, exchange(): pl.pallas_call(halo_kernel, in_specs=[vmem] * 4, out_specs=[vmem] * 4, ou...  17.8 us
    dot_general x1, matrix products, local(): jnp.einsum('tji,kti->tkj', tile_weights[0, 0, 0], picked, preferred_eleme...  8.84 us
    pallas_call x1, Pallas kernels, masked_edges(): pl.pallas_call(edges_kernel, grid=(lev // LB,), in_specs=[full2((rows, co...  7.11 us
    pallas_call x1, Pallas kernels, local(): pl.pallas_call(bucket_kernel, in_specs=[pl.BlockSpec(memory_space=pltpu.S...  4.53 us
  transfers between devices with their start and end apart: 1, of which 0 were waited for; matrix products, arithmetic and copies ran while one was open for 1% of the time, Pallas kernels for 41%

profile of v3, /device:TPU:16, one launch (start us, length us, event | category | flops | bytes accessed | tf_op | source)
XLA Modules:
  0.0 124.6 jit_solution(8124865153045165906)
XLA Ops:
  0.6 0.7 compare_select_fusion
  1.3 0.7 compare_and_fusion
  2.0 0.7 fusion.18
  2.7 0.6 reduce-window.6
  3.5 0.8 fusion.17
  4.3 0.7 compare_select_fusion.1
  5.0 0.8 convert_select_fusion.wet_ref
  5.9 1.4 %fusion.8 = bf16[8,128,128]{2,0,1:T(8,128)(2,1)S(1)} fusion(f32[1,8,128,128]{3,2,1,0:T(8,128)} %param.8, f32[128,128]{1,0:T(8,128)S(1)} %convert_select_fusion.wet_ref), kind=kLoop, calls=%fused_computation.10 | loop fusion | flops 262144 | bytes 851968 | tf_op jit(solution)/shard_map/convert_element_type | solution.py:289
  7.3 0.8 gather_fusion
  8.1 2.1 %scatter_custom_fusion.1.lab_ref = s32[512]{0:T(512)} fusion(s32[256]{0:T(256)S(1)} %bitcast.68, s32[256]{0:T(256)} %bitcast.71, s32[]{:T(128)} %constant.15.clone.1), kind=kCustom, calls=%fused_computation.35 | custom fusion | bytes 2560 | tf_op jit(solution)/shard_map/scatter | solution.py:303
  10.2 2.0 %scatter_custom_fusion.inv_ref = s32[512]{0:T(512)} fusion(s32[256]{0:T(256)S(1)} %bitcast.69, s32[256]{0:T(256)S(1)} %iota.15, s32[]{:T(128)} %constant.24.clone.1), kind=kCustom, calls=%fused_computation.37 | custom fusion | bytes 2052 | tf_op jit(solution)/shard_map/scatter | solution.py:302
  12.2 8.8 %fusion.contrib_ref = f32[256,8,128]{2,1,0:T(8,128)} fusion(bf16[1,1,1,256,128,128]{5,4,3,2,1,0:T(8,128)(2,1)} %param.10, bf16[256,8,128]{2,1,0:T(8,128)(2,1)S(1)} %gather_fusion, pred[256]{0:T(512)(128)(4,1)S(1)} %compare_and_fusion), kind=kOutput, calls=%fused_computation.3 | convolution fusion | flops 67371008 | bytes 9961728 | tf_op jit(solution)/shard_map/tji,kti->tkj/dot_general | solution.py:295
  21.0 4.5 %shard_map.91 = f32[64,9,8,128]{3,2,1,0:T(8,128)} custom-call(s32[512]{0:T(512)} %scatter_custom_fusion.inv_ref, s32[512]{0:T(512)} %scatter_custom_fusion.1.lab_ref, f32[256,8,128]{2,1,0:T(8,128)} %fusion.contrib_ref), custom_call_target="tpu_custom_call" | custom-call | tf_op jit(solution)/shard_map/pallas_call | solution.py:304
  25.5 42.1 %all_to_all.5 = f32[64,9,8,128]{3,2,1,0:T(8,128)S(1)} all-to-all(f32[64,9,8,128]{3,2,1,0:T(8,128)} %shard_map.91), channel_id=1, replica_groups=mesh['mp'=2,'gx'=8,'gy'=8] {'gx','gy'}, dimensions={0} | all-to-all | bytes 4718592 | tf_op jit(solution)/shard_map/all_to_all | solution.py:314
  68.1 2.1 %fusion.4 = f32[8,128,128]{2,1,0:T(8,128)S(1)} fusion(f32[64,8,8,128]{3,2,1,0:T(8,128)S(1)} %slice.23, s32[64,8]{0,1:T(8,128)S(1)} %bitcast.63), kind=kOutput, calls=%fused_computation.7 | convolution fusion | flops 805371904 | bytes 2623488 | tf_op jit(solution)/shard_map/scr,sckj->krj/dot_general | solution.py:319
  70.3 7.1 %shard_map.86 = (f32[64,128]{1,0:T(8,128)}, f32[64,128]{1,0:T(8,128)}, f32[64,128]{1,0:T(8,128)}, f32[64,128]{1,0:T(8,128)}) custom-call(f32[128,128]{1,0:T(8,128)} %copy-done, f32[64,128,128]{2,1,0:T(8,128)} %bitcast.57), custom_call_target="tpu_custom_call" | custom-call | flops 2097152 | bytes 4194304 | tf_op jit(solution)/shard_map/pallas_call | solution.py:121
  77.5 9.2 %shard_map.87 = (f32[64,128]{1,0:T(8,128)}, f32[64,128]{1,0:T(8,128)}, f32[64,128]{1,0:T(8,128)}, f32[64,128]{1,0:T(8,128)}) custom-call(f32[64,128]{1,0:T(8,128)} %get-tuple-element.19.en_ref, f32[64,128]{1,0:T(8,128)} %get-tuple-element.20.es_ref, f32[64,128]{1,0:T(8,128)} %get-tuple-element.21.ew_ref, f32[64,128]{1,0:T(8,128)} %get-tuple-element.22.ee_ref), custom_call_target="tpu_custom_call" | custom-call | tf_op jit(solution)/shard_map/pallas_call | solution.py:245
  86.6 0.7 pad_maximum_fusion.coef_ref
  87.3 15.9 %shard_map.88 = (f32[64,128,128]{2,1,0:T(8,128)}, f32[64,128]{1,0:T(8,128)}, f32[64,128]{1,0:T(8,128)}, f32[64,128]{1,0:T(8,128)}, f32[64,128]{1,0:T(8,128)}) custom-call(f32[2]{0:T(128)} %pad_maximum_fusion.coef_ref, f32[128,128]{1,0:T(8,128)} %copy-done, f32[64,128,128]{2,1,0:T(8,128)} %bitcast.58, f32[64,128,128]{2,1,0:T(8,128)} %bitcast.59, ...), custom_call_target="tpu_custom_call" | custom-call | flops 31457280 | bytes 12582912 | tf_op jit(solution)/shard_map/pallas_call | solution.py:177
  103.2 8.6 %shard_map.89 = (f32[64,128]{1,0:T(8,128)}, f32[64,128]{1,0:T(8,128)}, f32[64,128]{1,0:T(8,128)}, f32[64,128]{1,0:T(8,128)}) custom-call(f32[64,128]{1,0:T(8,128)} %get-tuple-element.28.en_ref, f32[64,128]{1,0:T(8,128)} %get-tuple-element.29.es_ref, f32[64,128]{1,0:T(8,128)} %get-tuple-element.30.ew_ref, f32[64,128]{1,0:T(8,128)} %get-tuple-element.31.ee_ref), custom_call_target="tpu_custom_call" | custom-call | tf_op jit(solution)/shard_map/pallas_call | solution.py:245
  111.8 9.9 %shard_map.90.x_ref = f32[64,128,128]{2,1,0:T(8,128)} custom-call(f32[2]{0:T(128)} %pad_maximum_fusion.coef_ref, f32[128,128]{1,0:T(8,128)} %copy-done, f32[64,128,128]{2,1,0:T(8,128)} %get-tuple-element.27.u_ref.above_ref.below_ref, f32[64,128,128]{2,1,0:T(8,128)} %get-tuple-element.27.u_ref.above_ref.below_ref, ...), custom_call_target="tpu_custom_call" | custom-call | flops 31457280 | bytes 12582912 | tf_op jit(solution)/shard_map/pallas_call | solution.py:177
  121.7 0.6 slice_bitcast_fusion.f_ref
  122.3 1.5 %shard_map.92 = f32[64,128,128]{2,1,0:T(8,128)} custom-call(f32[64,128,128]{2,1,0:T(8,128)} %shard_map.90.x_ref, f32[128,128]{1,0:T(8,128)} %copy-done, f32[128,128]{1,0:T(8,128)} %slice_bitcast_fusion.f_ref), custom_call_target="tpu_custom_call", output_to_operand_aliasing={{}: (0, {})} | custom-call | tf_op jit(solution)/shard_map/pallas_call | solution.py:142
  123.8 0.8 copy.35
  (12 shorter events, 0.8 us)
Async XLA Ops:
  5.9 15.2 %copy-start = (f32[128,128]{1,0:T(8,128)}, f32[128,128]{1,0:T(8,128)S(1)}, u32[]{:S(2)}) copy-start(f32[128,128]{1,0:T(8,128)S(1)} %convert_select_fusion.wet_ref) | copy-start | bytes 196612
  70.2 51.4 %collective-permute-start = (f32[8,128,128]{2,1,0:T(8,128)S(1)}, f32[8,128,128]{2,1,0:T(8,128)S(1)}, u32[]{:S(2)}, u32[]{:S(2)}) collective-permute-start(f32[8,128,128]{2,1,0:T(8,128)S(1)} %fusion.4), channel_id=1, source_target_pairs={{0,64},{64,0},{1,65},{65,1},{2,66},{66,2},{3,67},{67,3},{4,68},{68... | collective-permute-start | bytes 1572872 | tf_op jit(solution)/shard_map/ppermute | solution.py:322

commit v4 on v3

--- a/solution.py
+++ b/solution.py
@@ -20,10 +20,73 @@
     return up if forward else [(j, i) for i, j in up]
 
 
+def start_spread(buckets_ref, recv, send_sem, recv_sem):
+    mp = lax.axis_index("mp")
+    ngy = lax.axis_size("gy")
+    ndev = lax.axis_size("gx") * ngy
+    me = lax.axis_index("gx") * ngy + lax.axis_index("gy")
+    mesh_id = pl.DeviceIdType.MESH
+    barrier = pltpu.get_barrier_semaphore()
+
+    def greet(d, carry):
+        @pl.when(d != me)
+        def _():
+            pl.semaphore_signal(barrier, 1, device_id=(mp, d // ngy, d % ngy), device_id_type=mesh_id)
+
+        return carry
+
+    lax.fori_loop(0, ndev, greet, 0)
+    pl.semaphore_wait(barrier, ndev - 1)
+    recv[me] = buckets_ref[me]
+
+    def send(d, carry):
+        @pl.when(d != me)
+        def _():
+            pltpu.make_async_remote_copy(
+                src_ref=buckets_ref.at[d],
+                dst_ref=recv.at[me],
+                send_sem=send_sem.at[d],
+                recv_sem=recv_sem.at[me],
+                device_id=(mp, d // ngy, d % ngy),
+                device_id_type=mesh_id,
+            ).start()
+
+        return carry
+
+    lax.fori_loop(0, ndev, send, 0)
+
+
+def finish_spread(buckets_ref, recv, send_sem, recv_sem, arrived_ref):
+    ngy = lax.axis_size("gy")
+    ndev = lax.axis_size("gx") * ngy
+    me = lax.axis_index("gx") * ngy + lax.axis_index("gy")
+
+    def wait(d, carry):
+        @pl.when(d != me)
+        def _():
+            copy = pltpu.make_async_remote_copy(
+                src_ref=buckets_ref.at[d],
+                dst_ref=recv.at[d],
+                send_sem=send_sem.at[d],
+                recv_sem=recv_sem.at[d],
+                device_id=(lax.axis_index("mp"), d // ngy, d % ngy),
+                device_id_type=pl.DeviceIdType.MESH,
+            )
+            copy.wait_send()
+            copy.wait_recv()
+
+        return carry
+
+    lax.fori_loop(0, ndev, wait, 0)
+    arrived_ref[...] = recv[...]
+
+
 def stencil_kernel(with_edges, with_force, coef_ref, wet_ref, u_ref, above_ref, below_ref,
                    hn_ref, hs_ref, hw_ref, he_ref, *rest):
     if with_force:
         force_ref, rest = rest[0], rest[1:]
+    if with_edges:
+        buckets_ref, rest = rest[0], rest[1:]
     out_ref = rest[0]
     i = pl.program_id(0)
     nblk = pl.num_programs(0)
@@ -38,10 +101,11 @@
     above = above_ref[0] * jnp.where(i > 0, 1.0, 0.0)
     below = below_ref[0] * jnp.where(i < nblk - 1, 1.0, 0.0)
     if with_edges:
-        en_ref, es_ref, ew_ref, ee_ref, qw_ref, qe_ref = rest[1:]
+        en_ref, es_ref, ew_ref, ee_ref, arrived_ref, qw_ref, qe_ref, recv, send_sem, recv_sem = rest[1:]
 
         @pl.when(i == 0)
         def _():
+            start_spread(buckets_ref, recv, send_sem, recv_sem)
             qw_ref[...] = jnp.zeros_like(qw_ref)
             qe_ref[...] = jnp.zeros_like(qe_ref)
 
@@ -81,6 +145,7 @@
             lev = ew_ref.shape[0]
             ew_ref[...] = jnp.transpose(qw_ref[...])[0:lev, :]
             ee_ref[...] = jnp.transpose(qe_ref[...])[0:lev, :]
+            finish_spread(buckets_ref, recv, send_sem, recv_sem, arrived_ref)
 
 
 def edges_kernel(wet_ref, u_ref, en_ref, es_ref, ew_ref, ee_ref, qw_ref, qe_ref):
@@ -149,7 +214,8 @@
     )(x, wet, f)
 
 
-def stencil_step(coef, wet, u, halos, force=None, with_edges=False):
+def stencil_step(coef, wet, u, halos, force=None, buckets=None):
+    with_edges = buckets is not None
     lev, rows, cols = u.shape
     nblk = lev // LB
     full2 = lambda shape: pl.BlockSpec(shape, lambda i: (0, 0))
@@ -166,14 +232,25 @@
     if force is not None:
         in_specs.append(full2((rows, cols)))
         args.append(force)
+    if with_edges:
+        in_specs.append(pl.BlockSpec(buckets.shape, lambda i: (0, 0, 0, 0)))
+        args.append(buckets)
     out_shape = [jax.ShapeDtypeStruct((lev, rows, cols), jnp.float32)]
     out_specs = [pl.BlockSpec((LB, rows, cols), lambda i: (i, 0, 0))]
     scratch = []
+    params = dict(dimension_semantics=("arbitrary",))
     if with_edges:
         out_shape += [jax.ShapeDtypeStruct((lev, cols), jnp.float32)] * 2
         out_shape += [jax.ShapeDtypeStruct((lev, rows), jnp.float32)] * 2
+        out_shape += [jax.ShapeDtypeStruct(buckets.shape, buckets.dtype)]
         out_specs += [lvl2, lvl2, full2((lev, rows)), full2((lev, rows))]
-        scratch = [pltpu.VMEM((rows, 128), jnp.float32)] * 2
+        out_specs += [pl.BlockSpec(buckets.shape, lambda i: (0, 0, 0, 0))]
+        scratch = [pltpu.VMEM((rows, 128), jnp.float32)] * 2 + [
+            pltpu.VMEM(buckets.shape, buckets.dtype),
+            pltpu.SemaphoreType.DMA((buckets.shape[0],)),
+            pltpu.SemaphoreType.DMA((buckets.shape[0],)),
+        ]
+        params.update(collective_id=2, has_side_effects=True)
     return pl.pallas_call(
         functools.partial(stencil_kernel, with_edges, force is not None),
         grid=(nblk,),
@@ -181,7 +258,7 @@
         out_specs=out_specs,
         out_shape=out_shape,
         scratch_shapes=scratch,
-        compiler_params=pltpu.CompilerParams(dimension_semantics=("arbitrary",)),
+        compiler_params=pltpu.CompilerParams(**params),
         cost_estimate=pl.CostEstimate(flops=30 * u.size, bytes_accessed=12 * u.size, transcendentals=0),
     )(*args)
 
@@ -311,7 +388,8 @@
         out_specs=pl.BlockSpec(memory_space=pltpu.VMEM),
         out_shape=jax.ShapeDtypeStruct((ndev, CAP + 1, KF, CY), jnp.float32),
     )(inv, labels, contrib)
-    arrived = lax.all_to_all(buckets, ("gx", "gy"), split_axis=0, concat_axis=0, tiled=True)
+    halos0 = exchange(*masked_edges(wet, state), 0)
+    first, en, es, ew, ee, arrived = stencil_step(coef, wet, state, halos0, buckets=buckets)
     got_rows = arrived[:, CAP, :, 0].astype(jnp.int32)
     select = (
         got_rows[:, :, None] == jnp.arange(rows_here, dtype=jnp.int32)[None, None, :]
@@ -321,8 +399,6 @@
     )
     received = lax.ppermute(sent, "mp", [(0, 1), (1, 0)])
 
-    halos0 = exchange(*masked_edges(wet, state), 0)
-    first, en, es, ew, ee = stencil_step(coef, wet, state, halos0, with_edges=True)
     halos1 = exchange(en, es, ew, ee, 1)
     (second,) = stencil_step(coef, wet, first, halos1)
     second = add_force(second, wet, received[0])

time: 127 us -> 121 us (0.953)
  the two profiles are of different devices: /device:TPU:16 before, /device:TPU:88 now
where the time goes in v4:
time: 121 us; the launch traced here: 120 us
  Pallas kernels  95.9 us (79%)
  matrix products  11 us (9%)
  local copies, waits for them, and re-layouts  8.37 us (7%)
  other arithmetic  4.3 us (4%)
    pallas_call x2, Pallas kernels, stencil_step(): pl.pallas_call(functools.partial(stencil_kernel, with_edges, force is not...  62.1 us
    pallas_call x2, Pallas kernels, exchange(): pl.pallas_call(halo_kernel, in_specs=[vmem] * 4, out_specs=[vmem] * 4, ou...  20.6 us
    dot_general x1, matrix products, local(): jnp.einsum('tji,kti->tkj', tile_weights[0, 0, 0], picked, preferred_eleme...  8.84 us
    pallas_call x1, Pallas kernels, masked_edges(): pl.pallas_call(edges_kernel, grid=(lev // LB,), in_specs=[full2((rows, co...  7.12 us
    pallas_call x1, Pallas kernels, local(): pl.pallas_call(bucket_kernel, in_specs=[pl.BlockSpec(memory_space=pltpu.S...  4.53 us
  transfers between devices with their start and end apart: 1, of which 0 were waited for; matrix products, arithmetic and copies ran while one was open for 0% of the time, Pallas kernels for 18%

profile of v4, /device:TPU:88, one launch (start us, length us, event | category | flops | bytes accessed | tf_op | source)
XLA Modules:
  0.0 120.5 jit_solution(11773394373983367671)
XLA Ops:
  0.7 1.5 %convert_select_fusion.wet_ref = f32[128,128]{1,0:T(8,128)} fusion(s32[128,128]{1,0:T(8,128)} %param.9, pred[]{:T(512)S(6)} %eq.43), kind=kLoop, calls=%fused_computation.27 | loop fusion | flops 32768 | bytes 131073 | tf_op jit(solution)/shard_map/jit(_where)/select_n | solution.py:359
  2.2 7.1 %shard_map.86 = (f32[64,128]{1,0:T(8,128)}, f32[64,128]{1,0:T(8,128)}, f32[64,128]{1,0:T(8,128)}, f32[64,128]{1,0:T(8,128)}) custom-call(f32[128,128]{1,0:T(8,128)} %convert_select_fusion.wet_ref, f32[64,128,128]{2,1,0:T(8,128)} %bitcast.57), custom_call_target="tpu_custom_call" | custom-call | flops 2097152 | bytes 4194304 | tf_op jit(solution)/shard_map/pallas_call | solution.py:186
  9.3 0.3 fusion.8
  9.8 0.6 reduce-window.6
  10.4 0.2 slice_reduce_fusion
  10.6 0.1 fusion.17
  10.7 0.8 gather_fusion
  11.6 2.1 %scatter_custom_fusion.1.lab_ref = s32[512]{0:T(512)} fusion(s32[256]{0:T(256)S(1)} %bitcast.68, s32[256]{0:T(256)} %bitcast.71, s32[]{:T(128)} %constant.15.clone.1), kind=kCustom, calls=%fused_computation.35 | custom fusion | bytes 2560 | tf_op jit(solution)/shard_map/scatter | solution.py:380
  13.7 1.9 %scatter_custom_fusion.inv_ref = s32[512]{0:T(512)} fusion(s32[256]{0:T(256)S(1)} %bitcast.69, s32[256]{0:T(256)S(1)} %iota.15, s32[]{:T(128)} %constant.24.clone.1), kind=kCustom, calls=%fused_computation.37 | custom fusion | bytes 2052 | tf_op jit(solution)/shard_map/scatter | solution.py:379
  15.6 0.7 pad_maximum_fusion.coef_ref
  16.3 8.8 %fusion.contrib_ref = f32[256,8,128]{2,1,0:T(8,128)} fusion(bf16[1,1,1,256,128,128]{5,4,3,2,1,0:T(8,128)(2,1)} %param.10, bf16[256,8,128]{2,1,0:T(8,128)(2,1)S(1)} %gather_fusion, pred[256]{0:T(512)(128)(4,1)S(1)} %compare_and_fusion), kind=kOutput, calls=%fused_computation.3 | convolution fusion | flops 67371008 | bytes 9961728 | tf_op jit(solution)/shard_map/tji,kti->tkj/dot_general | solution.py:372
  25.1 4.5 %shard_map.88.rest_0_ = f32[64,9,8,128]{3,2,1,0:T(8,128)} custom-call(s32[512]{0:T(512)} %scatter_custom_fusion.inv_ref, s32[512]{0:T(512)} %scatter_custom_fusion.1.lab_ref, f32[256,8,128]{2,1,0:T(8,128)} %fusion.contrib_ref), custom_call_target="tpu_custom_call" | custom-call | tf_op jit(solution)/shard_map/pallas_call | solution.py:381
  29.6 8.7 %shard_map.87 = (f32[64,128]{1,0:T(8,128)}, f32[64,128]{1,0:T(8,128)}, f32[64,128]{1,0:T(8,128)}, f32[64,128]{1,0:T(8,128)}) custom-call(f32[64,128]{1,0:T(8,128)} %get-tuple-element.20.en_ref, f32[64,128]{1,0:T(8,128)} %get-tuple-element.21.es_ref, f32[64,128]{1,0:T(8,128)} %get-tuple-element.22.ew_ref, f32[64,128]{1,0:T(8,128)} %get-tuple-element.23.ee_ref), custom_call_target="tpu_custom_call" | custom-call | tf_op jit(solution)/shard_map/pallas_call | solution.py:322
  38.4 52.2 %shard_map.89 = (f32[64,128,128]{2,1,0:T(8,128)}, f32[64,128]{1,0:T(8,128)}, f32[64,128]{1,0:T(8,128)}, f32[64,128]{1,0:T(8,128)}, f32[64,128]{1,0:T(8,128)}, /*index=5*/f32[64,9,8,128]{3,2,1,0:T(8,128)}) custom-call(f32[2]{0:T(128)} %pad_maximum_fusion.coef_ref, f32[128,128]{1,0:T(8,128)} %convert_select_fusion.wet_ref, f32[64,128,128]{2,1,0:T(8,128)} %bitcast.58, ...), custom_call_target="tpu_custom_call" | custom-call | flops 31457280 | bytes 12582912 | tf_op jit(solution)/shard_map/pallas_call | solution.py:254
  90.6 1.7 %slice.17 = f32[64,8,8,128]{3,2,1,0:T(8,128)S(1)} slice(f32[64,9,8,128]{3,2,1,0:T(8,128)} %get-tuple-element.37), slice={[0:64], [0:8], [0:8], [0:128]} | slice | bytes 4194304 | tf_op jit(solution)/shard_map/slice | solution.py:398
  92.3 1.0 slice_convert_fusion
  93.3 0.1 copy.21
  93.5 2.1 %fusion.4 = f32[8,128,128]{2,1,0:T(8,128)S(1)} fusion(f32[64,8,8,128]{3,2,1,0:T(8,128)S(1)} %slice.17, s32[64,8]{0,1:T(8,128)S(1)} %bitcast.63), kind=kOutput, calls=%fused_computation.7 | convolution fusion | flops 805371904 | bytes 2623488 | tf_op jit(solution)/shard_map/scr,sckj->krj/dot_general | solution.py:397
  95.6 0.1 collective-permute-start
  95.7 11.9 %shard_map.90 = (f32[64,128]{1,0:T(8,128)}, f32[64,128]{1,0:T(8,128)}, f32[64,128]{1,0:T(8,128)}, f32[64,128]{1,0:T(8,128)}) custom-call(f32[64,128]{1,0:T(8,128)} %get-tuple-element.29.en_ref, f32[64,128]{1,0:T(8,128)} %get-tuple-element.30.es_ref, f32[64,128]{1,0:T(8,128)} %get-tuple-element.31.ew_ref, f32[64,128]{1,0:T(8,128)} %get-tuple-element.32.ee_ref), custom_call_target="tpu_custom_call" | custom-call | tf_op jit(solution)/shard_map/pallas_call | solution.py:322
  107.6 9.9 %shard_map.91.x_ref = f32[64,128,128]{2,1,0:T(8,128)} custom-call(f32[2]{0:T(128)} %pad_maximum_fusion.coef_ref, f32[128,128]{1,0:T(8,128)} %convert_select_fusion.wet_ref, f32[64,128,128]{2,1,0:T(8,128)} %get-tuple-element.28.u_ref.above_ref.below_ref, f32[64,128,128]{2,1,0:T(8,128)} %get-tuple-element.28.u_ref.above_ref.below_ref, ...), custom_call_target="tpu_custom_call" | custom-call | flops 31457280 | bytes 12582912 | tf_op jit(solution)/shard_map/pallas_call | solution.py:254
  117.5 0.6 slice_bitcast_fusion.f_ref
  118.1 1.5 %shard_map.92 = f32[64,128,128]{2,1,0:T(8,128)} custom-call(f32[64,128,128]{2,1,0:T(8,128)} %shard_map.91.x_ref, f32[128,128]{1,0:T(8,128)} %convert_select_fusion.wet_ref, f32[128,128]{1,0:T(8,128)} %slice_bitcast_fusion.f_ref), custom_call_target="tpu_custom_call", output_to_operand_aliasing={{}: (0, {})} | custom-call | tf_op jit(solution)/shard_map/pallas_call | solution.py:207
  119.7 0.8 copy.35
  (17 shorter events, 0.1 us)
Async XLA Ops:
  0.6 8.7 %copy-start.1 = (f32[1,8,128,128]{3,2,1,0:T(8,128)S(1)}, f32[1,8,128,128]{3,2,1,0:T(8,128)}, u32[]{:S(2)}) copy-start(f32[1,8,128,128]{3,2,1,0:T(8,128)} %param.8) | copy-start | bytes 1572868
  0.6 9.1 %copy-start.3 = (s32[1,1,1,256]{3,2,1,0:T(1,128)S(1)}, s32[1,1,1,256]{3,2,1,0:T(1,128)}, u32[]{:S(2)}) copy-start(s32[1,1,1,256]{3,2,1,0:T(1,128)} %param.11) | copy-start | bytes 3076
  0.7 9.1 %copy-start.2 = (s32[1,1,1,256,1]{3,4,2,1,0:T(1,128)S(1)}, s32[1,1,1,256,1]{3,4,2,1,0:T(1,128)}, u32[]{:S(2)}) copy-start(s32[1,1,1,256,1]{3,4,2,1,0:T(1,128)} %param.12) | copy-start | bytes 3076
  2.2 7.1 %copy-start = (f32[128,128]{1,0:T(8,128)S(1)}, f32[128,128]{1,0:T(8,128)}, u32[]{:S(2)}) copy-start(f32[128,128]{1,0:T(8,128)} %convert_select_fusion.wet_ref) | copy-start | bytes 196612
  95.6 21.9 %collective-permute-start = (f32[8,128,128]{2,1,0:T(8,128)S(1)}, f32[8,128,128]{2,1,0:T(8,128)S(1)}, u32[]{:S(2)}, u32[]{:S(2)}) collective-permute-start(f32[8,128,128]{2,1,0:T(8,128)S(1)} %fusion.4), channel_id=1, source_target_pairs={{0,64},{64,0},{1,65},{65,1},{2,66},{66,2},{3,67},{67,3},{4,68},{68... | collective-permute-start | bytes 1572872 | tf_op jit(solution)/shard_map/ppermute | solution.py:400

commit v5 on v4

--- a/solution.py
+++ b/solution.py
@@ -39,21 +39,19 @@
     pl.semaphore_wait(barrier, ndev - 1)
     recv[me] = buckets_ref[me]
 
-    def send(d, carry):
-        @pl.when(d != me)
-        def _():
-            pltpu.make_async_remote_copy(
-                src_ref=buckets_ref.at[d],
-                dst_ref=recv.at[me],
-                send_sem=send_sem.at[d],
-                recv_sem=recv_sem.at[me],
-                device_id=(mp, d // ngy, d % ngy),
-                device_id_type=mesh_id,
-            ).start()
-
+    def send(k, carry):
+        d = (me + k) % ndev
+        pltpu.make_async_remote_copy(
+            src_ref=buckets_ref.at[d],
+            dst_ref=recv.at[me],
+            send_sem=send_sem.at[d],
+            recv_sem=recv_sem.at[me],
+            device_id=(mp, d // ngy, d % ngy),
+            device_id_type=mesh_id,
+        ).start()
         return carry
 
-    lax.fori_loop(0, ndev, send, 0)
+    lax.fori_loop(1, ndev, send, 0)
 
 
 def finish_spread(buckets_ref, recv, send_sem, recv_sem, arrived_ref):

time: 121 us -> 113 us (0.934)
  the two profiles are of different devices: /device:TPU:88 before, /device:TPU:16 now
where the time goes in v5:
time: 113 us; the launch traced here: 112 us
  Pallas kernels  87.4 us (77%)
  matrix products  11 us (10%)
  local copies, waits for them, and re-layouts  8.36 us (7%)
  other arithmetic  4.3 us (4%)
    pallas_call x2, Pallas kernels, stencil_step(): pl.pallas_call(functools.partial(stencil_kernel, with_edges, force is not...  56.6 us
    pallas_call x2, Pallas kernels, exchange(): pl.pallas_call(halo_kernel, in_specs=[vmem] * 4, out_specs=[vmem] * 4, ou...  17.6 us
    dot_general x1, matrix products, local(): jnp.einsum('tji,kti->tkj', tile_weights[0, 0, 0], picked, preferred_eleme...  8.84 us
    pallas_call x1, Pallas kernels, masked_edges(): pl.pallas_call(edges_kernel, grid=(lev // LB,), in_specs=[full2((rows, co...  7.12 us
    pallas_call x1, Pallas kernels, local(): pl.pallas_call(bucket_kernel, in_specs=[pl.BlockSpec(memory_space=pltpu.S...  4.53 us
  transfers between devices with their start and end apart: 1, of which 0 were waited for; matrix products, arithmetic and copies ran while one was open for 0% of the time, Pallas kernels for 17%

profile of v5, /device:TPU:16, one launch (start us, length us, event | category | flops | bytes accessed | tf_op | source)
XLA Modules:
  0.0 111.9 jit_solution(14795401958889637269)
XLA Ops:
  0.7 1.5 %convert_select_fusion.wet_ref = f32[128,128]{1,0:T(8,128)} fusion(s32[128,128]{1,0:T(8,128)} %param.9, pred[]{:T(512)S(6)} %eq.43), kind=kLoop, calls=%fused_computation.27 | loop fusion | flops 32768 | bytes 131073 | tf_op jit(solution)/shard_map/jit(_where)/select_n | solution.py:357
  2.2 7.1 %shard_map.86 = (f32[64,128]{1,0:T(8,128)}, f32[64,128]{1,0:T(8,128)}, f32[64,128]{1,0:T(8,128)}, f32[64,128]{1,0:T(8,128)}) custom-call(f32[128,128]{1,0:T(8,128)} %convert_select_fusion.wet_ref, f32[64,128,128]{2,1,0:T(8,128)} %bitcast.57), custom_call_target="tpu_custom_call" | custom-call | flops 2097152 | bytes 4194304 | tf_op jit(solution)/shard_map/pallas_call | solution.py:184
  9.3 0.3 fusion.8
  9.8 0.6 reduce-window.6
  10.4 0.2 slice_reduce_fusion
  10.6 0.1 fusion.17
  10.7 0.8 gather_fusion
  11.6 2.1 %scatter_custom_fusion.1.lab_ref = s32[512]{0:T(512)} fusion(s32[256]{0:T(256)S(1)} %bitcast.68, s32[256]{0:T(256)} %bitcast.71, s32[]{:T(128)} %constant.15.clone.1), kind=kCustom, calls=%fused_computation.35 | custom fusion | bytes 2560 | tf_op jit(solution)/shard_map/scatter | solution.py:378
  13.7 1.9 %scatter_custom_fusion.inv_ref = s32[512]{0:T(512)} fusion(s32[256]{0:T(256)S(1)} %bitcast.69, s32[256]{0:T(256)S(1)} %iota.15, s32[]{:T(128)} %constant.24.clone.1), kind=kCustom, calls=%fused_computation.37 | custom fusion | bytes 2052 | tf_op jit(solution)/shard_map/scatter | solution.py:377
  15.6 0.7 pad_maximum_fusion.coef_ref
  16.3 8.8 %fusion.contrib_ref = f32[256,8,128]{2,1,0:T(8,128)} fusion(bf16[1,1,1,256,128,128]{5,4,3,2,1,0:T(8,128)(2,1)} %param.10, bf16[256,8,128]{2,1,0:T(8,128)(2,1)S(1)} %gather_fusion, pred[256]{0:T(512)(128)(4,1)S(1)} %compare_and_fusion), kind=kOutput, calls=%fused_computation.3 | convolution fusion | flops 67371008 | bytes 9961728 | tf_op jit(solution)/shard_map/tji,kti->tkj/dot_general | solution.py:370
  25.1 4.5 %shard_map.88.rest_0_ = f32[64,9,8,128]{3,2,1,0:T(8,128)} custom-call(s32[512]{0:T(512)} %scatter_custom_fusion.inv_ref, s32[512]{0:T(512)} %scatter_custom_fusion.1.lab_ref, f32[256,8,128]{2,1,0:T(8,128)} %fusion.contrib_ref), custom_call_target="tpu_custom_call" | custom-call | tf_op jit(solution)/shard_map/pallas_call | solution.py:379
  29.6 8.7 %shard_map.87 = (f32[64,128]{1,0:T(8,128)}, f32[64,128]{1,0:T(8,128)}, f32[64,128]{1,0:T(8,128)}, f32[64,128]{1,0:T(8,128)}) custom-call(f32[64,128]{1,0:T(8,128)} %get-tuple-element.20.en_ref, f32[64,128]{1,0:T(8,128)} %get-tuple-element.21.es_ref, f32[64,128]{1,0:T(8,128)} %get-tuple-element.22.ew_ref, f32[64,128]{1,0:T(8,128)} %get-tuple-element.23.ee_ref), custom_call_target="tpu_custom_call" | custom-call | tf_op jit(solution)/shard_map/pallas_call | solution.py:320
  38.3 46.7 %shard_map.89 = (f32[64,128,128]{2,1,0:T(8,128)}, f32[64,128]{1,0:T(8,128)}, f32[64,128]{1,0:T(8,128)}, f32[64,128]{1,0:T(8,128)}, f32[64,128]{1,0:T(8,128)}, /*index=5*/f32[64,9,8,128]{3,2,1,0:T(8,128)}) custom-call(f32[2]{0:T(128)} %pad_maximum_fusion.coef_ref, f32[128,128]{1,0:T(8,128)} %convert_select_fusion.wet_ref, f32[64,128,128]{2,1,0:T(8,128)} %bitcast.58, ...), custom_call_target="tpu_custom_call" | custom-call | flops 31457280 | bytes 12582912 | tf_op jit(solution)/shard_map/pallas_call | solution.py:252
  85.0 1.7 %slice.17 = f32[64,8,8,128]{3,2,1,0:T(8,128)S(1)} slice(f32[64,9,8,128]{3,2,1,0:T(8,128)} %get-tuple-element.37), slice={[0:64], [0:8], [0:8], [0:128]} | slice | bytes 4194304 | tf_op jit(solution)/shard_map/slice | solution.py:396
  86.8 1.0 slice_convert_fusion
  87.7 0.1 copy.21
  87.9 2.1 %fusion.4 = f32[8,128,128]{2,1,0:T(8,128)S(1)} fusion(f32[64,8,8,128]{3,2,1,0:T(8,128)S(1)} %slice.17, s32[64,8]{0,1:T(8,128)S(1)} %bitcast.63), kind=kOutput, calls=%fused_computation.7 | convolution fusion | flops 805371904 | bytes 2623488 | tf_op jit(solution)/shard_map/scr,sckj->krj/dot_general | solution.py:395
  90.0 0.1 collective-permute-start
  90.1 9.0 %shard_map.90 = (f32[64,128]{1,0:T(8,128)}, f32[64,128]{1,0:T(8,128)}, f32[64,128]{1,0:T(8,128)}, f32[64,128]{1,0:T(8,128)}) custom-call(f32[64,128]{1,0:T(8,128)} %get-tuple-element.29.en_ref, f32[64,128]{1,0:T(8,128)} %get-tuple-element.30.es_ref, f32[64,128]{1,0:T(8,128)} %get-tuple-element.31.ew_ref, f32[64,128]{1,0:T(8,128)} %get-tuple-element.32.ee_ref), custom_call_target="tpu_custom_call" | custom-call | tf_op jit(solution)/shard_map/pallas_call | solution.py:320
  99.1 9.9 %shard_map.91.x_ref = f32[64,128,128]{2,1,0:T(8,128)} custom-call(f32[2]{0:T(128)} %pad_maximum_fusion.coef_ref, f32[128,128]{1,0:T(8,128)} %convert_select_fusion.wet_ref, f32[64,128,128]{2,1,0:T(8,128)} %get-tuple-element.28.u_ref.above_ref.below_ref, f32[64,128,128]{2,1,0:T(8,128)} %get-tuple-element.28.u_ref.above_ref.below_ref, ...), custom_call_target="tpu_custom_call" | custom-call | flops 31457280 | bytes 12582912 | tf_op jit(solution)/shard_map/pallas_call | solution.py:252
  109.0 0.6 slice_bitcast_fusion.f_ref
  109.6 1.5 %shard_map.92 = f32[64,128,128]{2,1,0:T(8,128)} custom-call(f32[64,128,128]{2,1,0:T(8,128)} %shard_map.91.x_ref, f32[128,128]{1,0:T(8,128)} %convert_select_fusion.wet_ref, f32[128,128]{1,0:T(8,128)} %slice_bitcast_fusion.f_ref), custom_call_target="tpu_custom_call", output_to_operand_aliasing={{}: (0, {})} | custom-call | tf_op jit(solution)/shard_map/pallas_call | solution.py:205
  111.1 0.8 copy.35
  (17 shorter events, 0.1 us)
Async XLA Ops:
  0.6 8.7 %copy-start.1 = (f32[1,8,128,128]{3,2,1,0:T(8,128)S(1)}, f32[1,8,128,128]{3,2,1,0:T(8,128)}, u32[]{:S(2)}) copy-start(f32[1,8,128,128]{3,2,1,0:T(8,128)} %param.8) | copy-start | bytes 1572868
  0.6 9.1 %copy-start.3 = (s32[1,1,1,256]{3,2,1,0:T(1,128)S(1)}, s32[1,1,1,256]{3,2,1,0:T(1,128)}, u32[]{:S(2)}) copy-start(s32[1,1,1,256]{3,2,1,0:T(1,128)} %param.11) | copy-start | bytes 3076
  0.7 9.1 %copy-start.2 = (s32[1,1,1,256,1]{3,4,2,1,0:T(1,128)S(1)}, s32[1,1,1,256,1]{3,4,2,1,0:T(1,128)}, u32[]{:S(2)}) copy-start(s32[1,1,1,256,1]{3,4,2,1,0:T(1,128)} %param.12) | copy-start | bytes 3076
  2.2 7.1 %copy-start = (f32[128,128]{1,0:T(8,128)S(1)}, f32[128,128]{1,0:T(8,128)}, u32[]{:S(2)}) copy-start(f32[128,128]{1,0:T(8,128)} %convert_select_fusion.wet_ref) | copy-start | bytes 196612
  90.0 18.9 %collective-permute-start = (f32[8,128,128]{2,1,0:T(8,128)S(1)}, f32[8,128,128]{2,1,0:T(8,128)S(1)}, u32[]{:S(2)}, u32[]{:S(2)}) collective-permute-start(f32[8,128,128]{2,1,0:T(8,128)S(1)} %fusion.4), channel_id=1, source_target_pairs={{0,64},{64,0},{1,65},{65,1},{2,66},{66,2},{3,67},{67,3},{4,68},{68... | collective-permute-start | bytes 1572872 | tf_op jit(solution)/shard_map/ppermute | solution.py:398

commit v6 on v5

--- a/solution.py
+++ b/solution.py
@@ -77,6 +77,176 @@
 
     lax.fori_loop(0, ndev, wait, 0)
     arrived_ref[...] = recv[...]
+
+
+def first_kernel(coef_ref, wet_ref, u_ref, above_ref, below_ref, buckets_ref,
+                 out_ref, en_ref, es_ref, ew_ref, ee_ref, arrived_ref,
+                 edge0, halo, qw_ref, qe_ref, recv, send_sem, recv_sem, hsend, hrecv):
+    p = pl.program_id(0)
+    i = pl.program_id(1)
+    nblk = pl.num_programs(1)
+    wet = wet_ref[...]
+    rows, cols = wet.shape
+    lev = ew_ref.shape[0]
+    mp = lax.axis_index("mp")
+    gx = lax.axis_index("gx")
+    gy = lax.axis_index("gy")
+    ngx = lax.axis_size("gx")
+    ngy = lax.axis_size("gy")
+    mesh_id = pl.DeviceIdType.MESH
+    links = [
+        (gx < ngx - 1, (mp, gx + 1, gy), 1, 0),
+        (gx > 0, (mp, gx - 1, gy), 0, 1),
+        (gy < ngy - 1, (mp, gx, gy + 1), 3, 2),
+        (gy > 0, (mp, gx, gy - 1), 2, 3),
+    ]
+    fills = [gx > 0, gx < ngx - 1, gy > 0, gy < ngy - 1]
+    copies = [
+        pltpu.make_async_remote_copy(
+            src_ref=edge0.at[src],
+            dst_ref=halo.at[slot],
+            send_sem=hsend.at[slot],
+            recv_sem=hrecv.at[slot],
+            device_id=dev,
+            device_id_type=mesh_id,
+        )
+        for _, dev, src, slot in links
+    ]
+    lane = lax.broadcasted_iota(jnp.int32, qw_ref.shape, 1)
+
+    @pl.when((p == 0) & (i == 0))
+    def _():
+        start_spread(buckets_ref, recv, send_sem, recv_sem)
+        qw_ref[...] = jnp.zeros_like(qw_ref)
+        qe_ref[...] = jnp.zeros_like(qe_ref)
+
+    @pl.when(p == 0)
+    def _():
+        qw = qw_ref[...]
+        qe = qe_ref[...]
+        for l in range(LB):
+            fw = wet * u_ref[l]
+            edge0[0, i, l:l + 1, :] = fw[0:1, :]
+            edge0[1, i, l:l + 1, :] = fw[rows - 1:rows, :]
+            hit = lane == i * LB + l
+            qw = jnp.where(hit, fw[:, 0:1], qw)
+            qe = jnp.where(hit, fw[:, cols - 1:cols], qe)
+        qw_ref[...] = qw
+        qe_ref[...] = qe
+
+    @pl.when((p == 0) & (i == nblk - 1))
+    def _():
+        edge0[2] = jnp.transpose(qw_ref[...])[0:lev, :].reshape(nblk, LB, rows)
+        edge0[3] = jnp.transpose(qe_ref[...])[0:lev, :].reshape(nblk, LB, rows)
+        for (present, _, _, _), copy in zip(links, copies):
+            pl.when(present)(copy.start)
+
+    @pl.when((p == 1) & (i == 0))
+    def _():
+        for (present, _, _, _), copy in zip(links, copies):
+            pl.when(present)(copy.wait_send)
+        for slot, filled in enumerate(fills):
+            pl.when(filled)(copies[slot].wait_recv)
+
+            @pl.when(jnp.logical_not(filled))
+            def _():
+                halo[slot] = jnp.zeros_like(halo[slot])
+
+        qw_ref[...] = jnp.zeros_like(qw_ref)
+        qe_ref[...] = jnp.zeros_like(qe_ref)
+
+    @pl.when(p == 1)
+    def _():
+        horiz = coef_ref[0]
+        vert = coef_ref[1]
+        row = lax.broadcasted_iota(jnp.int32, (rows, cols), 0)
+        col = lax.broadcasted_iota(jnp.int32, (rows, cols), 1)
+        hn = halo[0, i]
+        hs = halo[1, i]
+        hw_t = jnp.transpose(halo[2, i])
+        he_t = jnp.transpose(halo[3, i])
+        above = above_ref[0] * jnp.where(i > 0, 1.0, 0.0)
+        below = below_ref[0] * jnp.where(i < nblk - 1, 1.0, 0.0)
+        qw = qw_ref[...]
+        qe = qe_ref[...]
+        for l in range(LB):
+            u = u_ref[l]
+            prev = u_ref[l - 1] if l > 0 else above
+            nxt = u_ref[l + 1] if l < LB - 1 else below
+            w = wet * u
+            north = jnp.where(row == 0, hn[l:l + 1, :], pltpu.roll(w, 1, 0))
+            south = jnp.where(row == rows - 1, hs[l:l + 1, :], pltpu.roll(w, rows - 1, 0))
+            west = jnp.where(col == 0, hw_t[:, l:l + 1], pltpu.roll(w, 1, 1))
+            east = jnp.where(col == cols - 1, he_t[:, l:l + 1], pltpu.roll(w, cols - 1, 1))
+            lateral = north + south + west + east - 4.0 * w
+            vertical = prev + nxt - 2.0 * u
+            res = wet * (u + horiz * lateral + vert * vertical)
+            out_ref[l] = res
+            fw = wet * res
+            en_ref[l:l + 1, :] = fw[0:1, :]
+            es_ref[l:l + 1, :] = fw[rows - 1:rows, :]
+            hit = lane == i * LB + l
+            qw = jnp.where(hit, fw[:, 0:1], qw)
+            qe = jnp.where(hit, fw[:, cols - 1:cols], qe)
+        qw_ref[...] = qw
+        qe_ref[...] = qe
+
+    @pl.when((p == 1) & (i == nblk - 1))
+    def _():
+        ew_ref[...] = jnp.transpose(qw_ref[...])[0:lev, :]
+        ee_ref[...] = jnp.transpose(qe_ref[...])[0:lev, :]
+        finish_spread(buckets_ref, recv, send_sem, recv_sem, arrived_ref)
+
+
+def first_step(coef, wet, u, buckets):
+    lev, rows, cols = u.shape
+    nblk = lev // LB
+    full2 = lambda shape: pl.BlockSpec(shape, lambda p, i: (0, 0))
+    lvl2 = pl.BlockSpec((LB, cols), lambda p, i: (i * p, 0))
+    whole = pl.BlockSpec(buckets.shape, lambda p, i: (0, 0, 0, 0))
+    in_specs = [
+        pl.BlockSpec(memory_space=pltpu.SMEM),
+        full2((rows, cols)),
+        pl.BlockSpec((LB, rows, cols), lambda p, i: (i, 0, 0)),
+        pl.BlockSpec((1, rows, cols), lambda p, i: (jnp.maximum(i * LB - 1, 0), 0, 0)),
+        pl.BlockSpec((1, rows, cols), lambda p, i: (jnp.minimum(i * LB + LB, lev - 1), 0, 0)),
+        whole,
+    ]
+    out_shape = [
+        jax.ShapeDtypeStruct((lev, rows, cols), jnp.float32),
+        jax.ShapeDtypeStruct((lev, cols), jnp.float32),
+        jax.ShapeDtypeStruct((lev, cols), jnp.float32),
+        jax.ShapeDtypeStruct((lev, rows), jnp.float32),
+        jax.ShapeDtypeStruct((lev, rows), jnp.float32),
+        jax.ShapeDtypeStruct(buckets.shape, buckets.dtype),
+    ]
+    out_specs = [
+        pl.BlockSpec((LB, rows, cols), lambda p, i: (i * p, 0, 0)),
+        lvl2, lvl2, full2((lev, rows)), full2((lev, rows)), whole,
+    ]
+    scratch = [
+        pltpu.VMEM((4, nblk, LB, cols), jnp.float32),
+        pltpu.VMEM((4, nblk, LB, cols), jnp.float32),
+        pltpu.VMEM((rows, 128), jnp.float32),
+        pltpu.VMEM((rows, 128), jnp.float32),
+        pltpu.VMEM(buckets.shape, buckets.dtype),
+        pltpu.SemaphoreType.DMA((buckets.shape[0],)),
+        pltpu.SemaphoreType.DMA((buckets.shape[0],)),
+        pltpu.SemaphoreType.DMA((4,)),
+        pltpu.SemaphoreType.DMA((4,)),
+    ]
+    return pl.pallas_call(
+        first_kernel,
+        grid=(2, nblk),
+        in_specs=in_specs,
+        out_specs=out_specs,
+        out_shape=out_shape,
+        scratch_shapes=scratch,
+        compiler_params=pltpu.CompilerParams(
+            dimension_semantics=("arbitrary", "arbitrary"), collective_id=2, has_side_effects=True
+        ),
+        cost_estimate=pl.CostEstimate(flops=32 * u.size, bytes_accessed=16 * u.size, transcendentals=0),
+    )(coef, wet, u, u, u, buckets)
 
 
 def stencil_kernel(with_edges, with_force, coef_ref, wet_ref, u_ref, above_ref, below_ref,
@@ -386,8 +556,7 @@
         out_specs=pl.BlockSpec(memory_space=pltpu.VMEM),
         out_shape=jax.ShapeDtypeStruct((ndev, CAP + 1, KF, CY), jnp.float32),
     )(inv, labels, contrib)
-    halos0 = exchange(*masked_edges(wet, state), 0)
-    first, en, es, ew, ee, arrived = stencil_step(coef, wet, state, halos0, buckets=buckets)
+    first, en, es, ew, ee, arrived = first_step(coef, wet, state, buckets)
     got_rows = arrived[:, CAP, :, 0].astype(jnp.int32)
     select = (
         got_rows[:, :, None] == jnp.arange(rows_here, dtype=jnp.int32)[None, None, :]

time: 113 us -> 118 us (1.044)
  other arithmetic: 4.3 us -> 8.04 us
  Pallas kernels: 87.4 us -> 89.3 us
    pallas_call x1, Pallas kernels: 7.12 us -> 64.3 us  [first_step(): pl.pallas_call(first_kernel, grid=(2, nblk), in_specs=in_specs, out_specs...]
    pallas_call x2 -> x1, Pallas kernels: 56.6 us -> 9.85 us  [stencil_step(): pl.pallas_call(functools.partial(stencil_kernel, with_edges, force is not...]
    pallas_call x2 -> x1, Pallas kernels: 17.6 us -> 9.14 us  [exchange(): pl.pallas_call(halo_kernel, in_specs=[vmem] * 4, out_specs=[vmem] * 4, ou...]
  transfers between devices with their start and end apart: 1 -> 1, of which waited for: 0 -> 0; matrix products, arithmetic and copies ran while one was open for 0% -> 0% of each run, Pallas kernels for 17% -> 16%
where the time goes in v6:
time: 118 us
  Pallas kernels  89.3 us (76%)
  matrix products  11 us (9%)
  local copies, waits for them, and re-layouts  8.4 us (7%)
  other arithmetic  8.04 us (7%)
    pallas_call x1, Pallas kernels, first_step(): pl.pallas_call(first_kernel, grid=(2, nblk), in_specs=in_specs, out_specs...  64.3 us
    pallas_call x1, Pallas kernels, stencil_step(): pl.pallas_call(functools.partial(stencil_kernel, with_edges, force is not...  9.85 us
    pallas_call x1, Pallas kernels, exchange(): pl.pallas_call(halo_kernel, in_specs=[vmem] * 4, out_specs=[vmem] * 4, ou...  9.14 us
    dot_general x1, matrix products, local(): jnp.einsum('tji,kti->tkj', tile_weights[0, 0, 0], picked, preferred_eleme...  8.84 us
    pallas_call x1, Pallas kernels, local(): pl.pallas_call(bucket_kernel, in_specs=[pl.BlockSpec(memory_space=pltpu.S...  4.53 us
  transfers between devices with their start and end apart: 1, of which 0 were waited for; matrix products, arithmetic and copies ran while one was open for 0% of the time, Pallas kernels for 16%

profile of v6, /device:TPU:16, one launch (start us, length us, event | category | flops | bytes accessed | tf_op | source)
XLA Modules:
  0.0 117.6 jit_solution(1462322097155776592)
XLA Ops:
  0.6 0.7 compare_select_fusion
  1.3 0.7 compare_and_fusion
  2.0 0.8 convert_select_fusion.wet_ref
  2.9 0.7 fusion.18
  3.6 0.6 reduce-window.6
  4.2 0.2 slice_reduce_fusion
  4.4 0.8 fusion.17
  5.2 0.7 compare_select_fusion.1
  5.9 0.7 pad_maximum_fusion.coef_ref
  6.5 2.1 %scatter_custom_fusion.1.lab_ref = s32[512]{0:T(512)} fusion(s32[256]{0:T(256)S(1)} %bitcast.69, s32[256]{0:T(256)} %bitcast.72, s32[]{:T(128)} %constant.15.clone.1), kind=kCustom, calls=%fused_computation.35 | custom fusion | bytes 2560 | tf_op jit(solution)/shard_map/scatter | solution.py:548
  8.7 2.0 %scatter_custom_fusion.inv_ref = s32[512]{0:T(512)} fusion(s32[256]{0:T(256)S(1)} %bitcast.70, s32[256]{0:T(256)S(1)} %iota.15, s32[]{:T(128)} %constant.24.clone.1), kind=kCustom, calls=%fused_computation.37 | custom fusion | bytes 2052 | tf_op jit(solution)/shard_map/scatter | solution.py:547
  10.6 1.4 %fusion.8 = bf16[8,128,128]{2,0,1:T(8,128)(2,1)S(1)} fusion(f32[1,8,128,128]{3,2,1,0:T(8,128)} %param.8, f32[128,128]{1,0:T(8,128)S(1)} %convert_select_fusion.wet_ref), kind=kLoop, calls=%fused_computation.10 | loop fusion | flops 262144 | bytes 851968 | tf_op jit(solution)/shard_map/convert_element_type | solution.py:534
  12.0 0.8 gather_fusion
  12.8 8.8 %fusion.contrib_ref = f32[256,8,128]{2,1,0:T(8,128)} fusion(bf16[1,1,1,256,128,128]{5,4,3,2,1,0:T(8,128)(2,1)} %param.10, bf16[256,8,128]{2,1,0:T(8,128)(2,1)S(1)} %gather_fusion, pred[256]{0:T(512)(128)(4,1)S(1)} %compare_and_fusion), kind=kOutput, calls=%fused_computation.3 | convolution fusion | flops 67371008 | bytes 9961728 | tf_op jit(solution)/shard_map/tji,kti->tkj/dot_general | solution.py:540
  21.7 4.5 %shard_map.86.buckets_ref = f32[64,9,8,128]{3,2,1,0:T(8,128)} custom-call(s32[512]{0:T(512)} %scatter_custom_fusion.inv_ref, s32[512]{0:T(512)} %scatter_custom_fusion.1.lab_ref, f32[256,8,128]{2,1,0:T(8,128)} %fusion.contrib_ref), custom_call_target="tpu_custom_call" | custom-call | tf_op jit(solution)/shard_map/pallas_call | solution.py:549
  26.2 64.3 %shard_map.87 = (f32[64,128,128]{2,1,0:T(8,128)}, f32[64,128]{1,0:T(8,128)}, f32[64,128]{1,0:T(8,128)}, f32[64,128]{1,0:T(8,128)}, f32[64,128]{1,0:T(8,128)}, /*index=5*/f32[64,9,8,128]{3,2,1,0:T(8,128)}) custom-call(f32[2]{0:T(128)} %pad_maximum_fusion.coef_ref, f32[128,128]{1,0:T(8,128)} %copy-done, f32[64,128,128]{2,1,0:T(8,128)} %bitcast.59, ...), custom_call_target="tpu_custom_call" | custom-call | flops 33554432 | bytes 16777216 | tf_op jit(solution)/shard_map/pallas_call | solution.py:238
  90.5 1.0 slice_convert_fusion
  91.5 1.7 %slice.17 = f32[64,8,8,128]{3,2,1,0:T(8,128)S(1)} slice(f32[64,9,8,128]{3,2,1,0:T(8,128)} %get-tuple-element.21), slice={[0:64], [0:8], [0:8], [0:128]} | slice | bytes 4194304 | tf_op jit(solution)/shard_map/slice | solution.py:565
  93.3 2.1 %fusion.4 = f32[8,128,128]{2,1,0:T(8,128)S(1)} fusion(f32[64,8,8,128]{3,2,1,0:T(8,128)S(1)} %slice.17, s32[64,8]{0,1:T(8,128)S(1)} %bitcast.64), kind=kOutput, calls=%fused_computation.7 | convolution fusion | flops 805371904 | bytes 2623488 | tf_op jit(solution)/shard_map/scr,sckj->krj/dot_general | solution.py:564
  95.6 9.1 %shard_map.88 = (f32[64,128]{1,0:T(8,128)}, f32[64,128]{1,0:T(8,128)}, f32[64,128]{1,0:T(8,128)}, f32[64,128]{1,0:T(8,128)}) custom-call(f32[64,128]{1,0:T(8,128)} %get-tuple-element.13.en_ref, f32[64,128]{1,0:T(8,128)} %get-tuple-element.14.es_ref, f32[64,128]{1,0:T(8,128)} %get-tuple-element.15.ew_ref, f32[64,128]{1,0:T(8,128)} %get-tuple-element.16.ee_ref), custom_call_target="tpu_custom_call" | custom-call | tf_op jit(solution)/shard_map/pallas_call | solution.py:490
  104.7 9.9 %shard_map.89.x_ref = f32[64,128,128]{2,1,0:T(8,128)} custom-call(f32[2]{0:T(128)} %pad_maximum_fusion.coef_ref, f32[128,128]{1,0:T(8,128)} %copy-done, f32[64,128,128]{2,1,0:T(8,128)} %get-tuple-element.12.u_ref.above_ref.below_ref, f32[64,128,128]{2,1,0:T(8,128)} %get-tuple-element.12.u_ref.above_ref.below_ref, ...), custom_call_target="tpu_custom_call" | custom-call | flops 31457280 | bytes 12582912 | tf_op jit(solution)/shard_map/pallas_call | solution.py:422
  114.6 0.6 slice_bitcast_fusion.f_ref
  115.2 1.5 %shard_map.90 = f32[64,128,128]{2,1,0:T(8,128)} custom-call(f32[64,128,128]{2,1,0:T(8,128)} %shard_map.89.x_ref, f32[128,128]{1,0:T(8,128)} %copy-done, f32[128,128]{1,0:T(8,128)} %slice_bitcast_fusion.f_ref), custom_call_target="tpu_custom_call", output_to_operand_aliasing={{}: (0, {})} | custom-call | tf_op jit(solution)/shard_map/pallas_call | solution.py:375
  116.8 0.8 copy.35
  (9 shorter events, 0.3 us)
Async XLA Ops:
  2.9 18.8 %copy-start = (f32[128,128]{1,0:T(8,128)}, f32[128,128]{1,0:T(8,128)S(1)}, u32[]{:S(2)}) copy-start(f32[128,128]{1,0:T(8,128)S(1)} %convert_select_fusion.wet_ref) | copy-start | bytes 196612
  95.5 19.1 %collective-permute-start = (f32[8,128,128]{2,1,0:T(8,128)S(1)}, f32[8,128,128]{2,1,0:T(8,128)S(1)}, u32[]{:S(2)}, u32[]{:S(2)}) collective-permute-start(f32[8,128,128]{2,1,0:T(8,128)S(1)} %fusion.4), channel_id=1, source_target_pairs={{0,64},{64,0},{1,65},{65,1},{2,66},{66,2},{3,67},{67,3},{4,68},{68... | collective-permute-start | bytes 1572872 | tf_op jit(solution)/shard_map/ppermute | solution.py:567

commit v7 on v6

--- a/solution.py
+++ b/solution.py
@@ -20,7 +20,7 @@
     return up if forward else [(j, i) for i, j in up]
 
 
-def start_spread(buckets_ref, recv, send_sem, recv_sem):
+def start_spread(buckets_ref, recv, send_sem, recv_sem, first_out=None):
     mp = lax.axis_index("mp")
     ngy = lax.axis_size("gy")
     ndev = lax.axis_size("gx") * ngy
@@ -37,6 +37,8 @@
 
     lax.fori_loop(0, ndev, greet, 0)
     pl.semaphore_wait(barrier, ndev - 1)
+    if first_out is not None:
+        first_out()
     recv[me] = buckets_ref[me]
 
     def send(k, carry):
@@ -80,11 +82,12 @@
 
 
 def first_kernel(coef_ref, wet_ref, u_ref, above_ref, below_ref, buckets_ref,
+                 e0n, e0s, e0w, e0e,
                  out_ref, en_ref, es_ref, ew_ref, ee_ref, arrived_ref,
-                 edge0, halo, qw_ref, qe_ref, recv, send_sem, recv_sem, hsend, hrecv):
-    p = pl.program_id(0)
-    i = pl.program_id(1)
-    nblk = pl.num_programs(1)
+                 halo, qw_ref, qe_ref, recv, send_sem, recv_sem, hsend, hrecv):
+    i = pl.program_id(0)
+    nblk = pl.num_programs(0)
+    edge0 = [e0n, e0s, e0w, e0e]
     wet = wet_ref[...]
     rows, cols = wet.shape
     lev = ew_ref.shape[0]
@@ -103,7 +106,7 @@
     fills = [gx > 0, gx < ngx - 1, gy > 0, gy < ngy - 1]
     copies = [
         pltpu.make_async_remote_copy(
-            src_ref=edge0.at[src],
+            src_ref=edge0[src],
             dst_ref=halo.at[slot],
             send_sem=hsend.at[slot],
             recv_sem=hrecv.at[slot],
@@ -114,35 +117,13 @@
     ]
     lane = lax.broadcasted_iota(jnp.int32, qw_ref.shape, 1)
 
-    @pl.when((p == 0) & (i == 0))
-    def _():
-        start_spread(buckets_ref, recv, send_sem, recv_sem)
-        qw_ref[...] = jnp.zeros_like(qw_ref)
-        qe_ref[...] = jnp.zeros_like(qe_ref)
-
-    @pl.when(p == 0)
-    def _():
-        qw = qw_ref[...]
-        qe = qe_ref[...]
-        for l in range(LB):
-            fw = wet * u_ref[l]
-            edge0[0, i, l:l + 1, :] = fw[0:1, :]
-            edge0[1, i, l:l + 1, :] = fw[rows - 1:rows, :]
-            hit = lane == i * LB + l
-            qw = jnp.where(hit, fw[:, 0:1], qw)
-            qe = jnp.where(hit, fw[:, cols - 1:cols], qe)
-        qw_ref[...] = qw
-        qe_ref[...] = qe
-
-    @pl.when((p == 0) & (i == nblk - 1))
-    def _():
-        edge0[2] = jnp.transpose(qw_ref[...])[0:lev, :].reshape(nblk, LB, rows)
-        edge0[3] = jnp.transpose(qe_ref[...])[0:lev, :].reshape(nblk, LB, rows)
+    def send_halos():
         for (present, _, _, _), copy in zip(links, copies):
             pl.when(present)(copy.start)
 
-    @pl.when((p == 1) & (i == 0))
+    @pl.when(i == 0)
     def _():
+        start_spread(buckets_ref, recv, send_sem, recv_sem, send_halos)
         for (present, _, _, _), copy in zip(links, copies):
             pl.when(present)(copy.wait_send)
         for slot, filled in enumerate(fills):
@@ -155,16 +136,15 @@
         qw_ref[...] = jnp.zeros_like(qw_ref)
         qe_ref[...] = jnp.zeros_like(qe_ref)
 
-    @pl.when(p == 1)
     def _():
         horiz = coef_ref[0]
         vert = coef_ref[1]
         row = lax.broadcasted_iota(jnp.int32, (rows, cols), 0)
         col = lax.broadcasted_iota(jnp.int32, (rows, cols), 1)
-        hn = halo[0, i]
-        hs = halo[1, i]
-        hw_t = jnp.transpose(halo[2, i])
-        he_t = jnp.transpose(halo[3, i])
+        hn = halo[0, pl.ds(i * LB, LB)]
+        hs = halo[1, pl.ds(i * LB, LB)]
+        hw_t = jnp.transpose(halo[2, pl.ds(i * LB, LB)])
+        he_t = jnp.transpose(halo[3, pl.ds(i * LB, LB)])
         above = above_ref[0] * jnp.where(i > 0, 1.0, 0.0)
         below = below_ref[0] * jnp.where(i < nblk - 1, 1.0, 0.0)
         qw = qw_ref[...]
@@ -191,27 +171,29 @@
         qw_ref[...] = qw
         qe_ref[...] = qe
 
-    @pl.when((p == 1) & (i == nblk - 1))
+    _()
+
+    @pl.when(i == nblk - 1)
     def _():
         ew_ref[...] = jnp.transpose(qw_ref[...])[0:lev, :]
         ee_ref[...] = jnp.transpose(qe_ref[...])[0:lev, :]
         finish_spread(buckets_ref, recv, send_sem, recv_sem, arrived_ref)
 
 
-def first_step(coef, wet, u, buckets):
+def first_step(coef, wet, u, buckets, edges):
     lev, rows, cols = u.shape
     nblk = lev // LB
-    full2 = lambda shape: pl.BlockSpec(shape, lambda p, i: (0, 0))
-    lvl2 = pl.BlockSpec((LB, cols), lambda p, i: (i * p, 0))
-    whole = pl.BlockSpec(buckets.shape, lambda p, i: (0, 0, 0, 0))
+    full2 = lambda shape: pl.BlockSpec(shape, lambda i: (0, 0))
+    lvl2 = pl.BlockSpec((LB, cols), lambda i: (i, 0))
+    whole = pl.BlockSpec(buckets.shape, lambda i: (0, 0, 0, 0))
     in_specs = [
         pl.BlockSpec(memory_space=pltpu.SMEM),
         full2((rows, cols)),
-        pl.BlockSpec((LB, rows, cols), lambda p, i: (i, 0, 0)),
-        pl.BlockSpec((1, rows, cols), lambda p, i: (jnp.maximum(i * LB - 1, 0), 0, 0)),
-        pl.BlockSpec((1, rows, cols), lambda p, i: (jnp.minimum(i * LB + LB, lev - 1), 0, 0)),
+        pl.BlockSpec((LB, rows, cols), lambda i: (i, 0, 0)),
+        pl.BlockSpec((1, rows, cols), lambda i: (jnp.maximum(i * LB - 1, 0), 0, 0)),
+        pl.BlockSpec((1, rows, cols), lambda i: (jnp.minimum(i * LB + LB, lev - 1), 0, 0)),
         whole,
-    ]
+    ] + [full2((lev, cols))] * 4
     out_shape = [
         jax.ShapeDtypeStruct((lev, rows, cols), jnp.float32),
         jax.ShapeDtypeStruct((lev, cols), jnp.float32),
@@ -221,12 +203,11 @@
         jax.ShapeDtypeStruct(buckets.shape, buckets.dtype),
     ]
     out_specs = [
-        pl.BlockSpec((LB, rows, cols), lambda p, i: (i * p, 0, 0)),
+        pl.BlockSpec((LB, rows, cols), lambda i: (i, 0, 0)),
         lvl2, lvl2, full2((lev, rows)), full2((lev, rows)), whole,
     ]
     scratch = [
-        pltpu.VMEM((4, nblk, LB, cols), jnp.float32),
-        pltpu.VMEM((4, nblk, LB, cols), jnp.float32),
+        pltpu.VMEM((4, lev, cols), jnp.float32),
         pltpu.VMEM((rows, 128), jnp.float32),
         pltpu.VMEM((rows, 128), jnp.float32),
         pltpu.VMEM(buckets.shape, buckets.dtype),
@@ -237,16 +218,16 @@
     ]
     return pl.pallas_call(
         first_kernel,
-        grid=(2, nblk),
+        grid=(nblk,),
         in_specs=in_specs,
         out_specs=out_specs,
         out_shape=out_shape,
         scratch_shapes=scratch,
         compiler_params=pltpu.CompilerParams(
-            dimension_semantics=("arbitrary", "arbitrary"), collective_id=2, has_side_effects=True
+            dimension_semantics=("arbitrary",), collective_id=2, has_side_effects=True
         ),
-        cost_estimate=pl.CostEstimate(flops=32 * u.size, bytes_accessed=16 * u.size, transcendentals=0),
-    )(coef, wet, u, u, u, buckets)
+        cost_estimate=pl.CostEstimate(flops=30 * u.size, bytes_accessed=12 * u.size, transcendentals=0),
+    )(coef, wet, u, u, u, buckets, *edges)
 
 
 def stencil_kernel(with_edges, with_force, coef_ref, wet_ref, u_ref, above_ref, below_ref,
@@ -556,7 +537,7 @@
         out_specs=pl.BlockSpec(memory_space=pltpu.VMEM),
         out_shape=jax.ShapeDtypeStruct((ndev, CAP + 1, KF, CY), jnp.float32),
     )(inv, labels, contrib)
-    first, en, es, ew, ee, arrived = first_step(coef, wet, state, buckets)
+    first, en, es, ew, ee, arrived = first_step(coef, wet, state, buckets, masked_edges(wet, state))
     got_rows = arrived[:, CAP, :, 0].astype(jnp.int32)
     select = (
         got_rows[:, :, None] == jnp.arange(rows_here, dtype=jnp.int32)[None, None, :]

time: 118 us -> 114 us (0.966)
  the two profiles are of different devices: /device:TPU:16 before, /device:TPU:32 now
where the time goes in v7:
time: 114 us
  Pallas kernels  85.3 us (75%)
  matrix products  11 us (10%)
  local copies, waits for them, and re-layouts  8.4 us (7%)
  other arithmetic  8.07 us (7%)
    pallas_call x1, Pallas kernels, first_step(): pl.pallas_call(first_kernel, grid=(nblk,), in_specs=in_specs, out_specs=o...  48.1 us
    pallas_call x1, Pallas kernels, exchange(): pl.pallas_call(halo_kernel, in_specs=[vmem] * 4, out_specs=[vmem] * 4, ou...  14.2 us
    pallas_call x1, Pallas kernels, stencil_step(): pl.pallas_call(functools.partial(stencil_kernel, with_edges, force is not...  9.85 us
    dot_general x1, matrix products, local(): jnp.einsum('tji,kti->tkj', tile_weights[0, 0, 0], picked, preferred_eleme...  8.84 us
    pallas_call x1, Pallas kernels, masked_edges(): pl.pallas_call(edges_kernel, grid=(lev // LB,), in_specs=[full2((rows, co...  7.14 us
    pallas_call x1, Pallas kernels, local(): pl.pallas_call(bucket_kernel, in_specs=[pl.BlockSpec(memory_space=pltpu.S...  4.53 us
  transfers between devices with their start and end apart: 1, of which 0 were waited for; matrix products, arithmetic and copies ran while one was open for 0% of the time, Pallas kernels for 21%

profile of v7, /device:TPU:32, one launch (start us, length us, event | category | flops | bytes accessed | tf_op | source)
XLA Modules:
  0.0 113.6 jit_solution(5227103970985608770)
XLA Ops:
  0.6 0.7 compare_select_fusion
  1.3 0.7 compare_and_fusion
  2.0 0.7 fusion.18
  2.7 0.6 reduce-window.6
  3.5 0.8 fusion.17
  4.3 0.7 compare_select_fusion.1
  5.0 0.8 convert_select_fusion.wet_ref
  5.9 1.4 %fusion.8 = bf16[8,128,128]{2,0,1:T(8,128)(2,1)S(1)} fusion(f32[1,8,128,128]{3,2,1,0:T(8,128)} %param.8, f32[128,128]{1,0:T(8,128)S(1)} %convert_select_fusion.wet_ref), kind=kLoop, calls=%fused_computation.10 | loop fusion | flops 262144 | bytes 851968 | tf_op jit(solution)/shard_map/convert_element_type | solution.py:515
  7.3 7.1 %shard_map.87 = (f32[64,128]{1,0:T(8,128)}, f32[64,128]{1,0:T(8,128)}, f32[64,128]{1,0:T(8,128)}, f32[64,128]{1,0:T(8,128)}) custom-call(f32[128,128]{1,0:T(8,128)} %copy-done, f32[64,128,128]{2,1,0:T(8,128)} %bitcast.57), custom_call_target="tpu_custom_call" | custom-call | flops 2097152 | bytes 4194304 | tf_op jit(solution)/shard_map/pallas_call | solution.py:335
  14.4 0.8 gather_fusion
  15.3 2.1 %scatter_custom_fusion.1.lab_ref = s32[512]{0:T(512)} fusion(s32[256]{0:T(256)S(1)} %bitcast.68, s32[256]{0:T(256)} %bitcast.71, s32[]{:T(128)} %constant.15.clone.1), kind=kCustom, calls=%fused_computation.35 | custom fusion | bytes 2560 | tf_op jit(solution)/shard_map/scatter | solution.py:529
  17.4 2.0 %scatter_custom_fusion.inv_ref = s32[512]{0:T(512)} fusion(s32[256]{0:T(256)S(1)} %bitcast.69, s32[256]{0:T(256)S(1)} %iota.15, s32[]{:T(128)} %constant.24.clone.1), kind=kCustom, calls=%fused_computation.37 | custom fusion | bytes 2052 | tf_op jit(solution)/shard_map/scatter | solution.py:528
  19.3 0.7 pad_maximum_fusion.coef_ref
  20.0 8.8 %fusion.contrib_ref = f32[256,8,128]{2,1,0:T(8,128)} fusion(bf16[1,1,1,256,128,128]{5,4,3,2,1,0:T(8,128)(2,1)} %param.10, bf16[256,8,128]{2,1,0:T(8,128)(2,1)S(1)} %gather_fusion, pred[256]{0:T(512)(128)(4,1)S(1)} %compare_and_fusion), kind=kOutput, calls=%fused_computation.3 | convolution fusion | flops 67371008 | bytes 9961728 | tf_op jit(solution)/shard_map/tji,kti->tkj/dot_general | solution.py:521
  28.8 4.5 %shard_map.86.buckets_ref = f32[64,9,8,128]{3,2,1,0:T(8,128)} custom-call(s32[512]{0:T(512)} %scatter_custom_fusion.inv_ref, s32[512]{0:T(512)} %scatter_custom_fusion.1.lab_ref, f32[256,8,128]{2,1,0:T(8,128)} %fusion.contrib_ref), custom_call_target="tpu_custom_call" | custom-call | tf_op jit(solution)/shard_map/pallas_call | solution.py:530
  33.4 48.1 %shard_map.88 = (f32[64,128,128]{2,1,0:T(8,128)}, f32[64,128]{1,0:T(8,128)}, f32[64,128]{1,0:T(8,128)}, f32[64,128]{1,0:T(8,128)}, f32[64,128]{1,0:T(8,128)}, /*index=5*/f32[64,9,8,128]{3,2,1,0:T(8,128)}) custom-call(f32[2]{0:T(128)} %pad_maximum_fusion.coef_ref, f32[128,128]{1,0:T(8,128)} %copy-done, f32[64,128,128]{2,1,0:T(8,128)} %bitcast.58, ...), custom_call_target="tpu_custom_call" | custom-call | flops 31457280 | bytes 12582912 | tf_op jit(solution)/shard_map/pallas_call | solution.py:219
  81.5 1.7 %slice.17 = f32[64,8,8,128]{3,2,1,0:T(8,128)S(1)} slice(f32[64,9,8,128]{3,2,1,0:T(8,128)} %get-tuple-element.29), slice={[0:64], [0:8], [0:8], [0:128]} | slice | bytes 4194304 | tf_op jit(solution)/shard_map/slice | solution.py:546
  83.2 1.0 slice_convert_fusion
  84.3 2.1 %fusion.4 = f32[8,128,128]{2,1,0:T(8,128)S(1)} fusion(f32[64,8,8,128]{3,2,1,0:T(8,128)S(1)} %slice.17, s32[64,8]{0,1:T(8,128)S(1)} %bitcast.63), kind=kOutput, calls=%fused_computation.7 | convolution fusion | flops 805371904 | bytes 2623488 | tf_op jit(solution)/shard_map/scr,sckj->krj/dot_general | solution.py:545
  86.6 14.2 %shard_map.89 = (f32[64,128]{1,0:T(8,128)}, f32[64,128]{1,0:T(8,128)}, f32[64,128]{1,0:T(8,128)}, f32[64,128]{1,0:T(8,128)}) custom-call(f32[64,128]{1,0:T(8,128)} %get-tuple-element.21.en_ref, f32[64,128]{1,0:T(8,128)} %get-tuple-element.22.es_ref, f32[64,128]{1,0:T(8,128)} %get-tuple-element.23.ew_ref, f32[64,128]{1,0:T(8,128)} %get-tuple-element.24.ee_ref), custom_call_target="tpu_custom_call" | custom-call | tf_op jit(solution)/shard_map/pallas_call | solution.py:471
  100.8 9.9 %shard_map.90.x_ref = f32[64,128,128]{2,1,0:T(8,128)} custom-call(f32[2]{0:T(128)} %pad_maximum_fusion.coef_ref, f32[128,128]{1,0:T(8,128)} %copy-done, f32[64,128,128]{2,1,0:T(8,128)} %get-tuple-element.20.u_ref.above_ref.below_ref, f32[64,128,128]{2,1,0:T(8,128)} %get-tuple-element.20.u_ref.above_ref.below_ref, ...), custom_call_target="tpu_custom_call" | custom-call | flops 31457280 | bytes 12582912 | tf_op jit(solution)/shard_map/pallas_call | solution.py:403
  110.6 0.6 slice_bitcast_fusion.f_ref
  111.2 1.5 %shard_map.91 = f32[64,128,128]{2,1,0:T(8,128)} custom-call(f32[64,128,128]{2,1,0:T(8,128)} %shard_map.90.x_ref, f32[128,128]{1,0:T(8,128)} %copy-done, f32[128,128]{1,0:T(8,128)} %slice_bitcast_fusion.f_ref), custom_call_target="tpu_custom_call", output_to_operand_aliasing={{}: (0, {})} | custom-call | tf_op jit(solution)/shard_map/pallas_call | solution.py:356
  112.8 0.8 copy.35
  (10 shorter events, 0.5 us)
Async XLA Ops:
  5.9 1.4 %copy-start = (f32[128,128]{1,0:T(8,128)}, f32[128,128]{1,0:T(8,128)S(1)}, u32[]{:S(2)}) copy-start(f32[128,128]{1,0:T(8,128)S(1)} %convert_select_fusion.wet_ref) | copy-start | bytes 196612
  86.5 24.1 %collective-permute-start = (f32[8,128,128]{2,1,0:T(8,128)S(1)}, f32[8,128,128]{2,1,0:T(8,128)S(1)}, u32[]{:S(2)}, u32[]{:S(2)}) collective-permute-start(f32[8,128,128]{2,1,0:T(8,128)S(1)} %fusion.4), channel_id=1, source_target_pairs={{0,64},{64,0},{1,65},{65,1},{2,66},{66,2},{3,67},{67,3},{4,68},{68... | collective-permute-start | bytes 1572872 | tf_op jit(solution)/shard_map/ppermute | solution.py:548

commit v8 on v7

--- a/solution.py
+++ b/solution.py
@@ -79,6 +79,237 @@
 
     lax.fori_loop(0, ndev, wait, 0)
     arrived_ref[...] = recv[...]
+
+
+def interval_kernel(coef_ref, wet_ref, u_ref, above_ref, below_ref, buckets_ref,
+                    e0n, e0s, e0w, e0e,
+                    out_ref, arrived_ref,
+                    first, edge1, halo0, halo1, qw_ref, qe_ref, recv,
+                    send_sem, recv_sem, hsend, hrecv):
+    p = pl.program_id(0)
+    i = pl.program_id(1)
+    nblk = pl.num_programs(1)
+    wet = wet_ref[...]
+    rows, cols = wet.shape
+    lev = first.shape[0]
+    mp = lax.axis_index("mp")
+    gx = lax.axis_index("gx")
+    gy = lax.axis_index("gy")
+    ngx = lax.axis_size("gx")
+    ngy = lax.axis_size("gy")
+    ndev = ngx * ngy
+    me = gx * ngy + gy
+    mesh_id = pl.DeviceIdType.MESH
+    links = [
+        (gx < ngx - 1, (mp, gx + 1, gy), 1, 0),
+        (gx > 0, (mp, gx - 1, gy), 0, 1),
+        (gy < ngy - 1, (mp, gx, gy + 1), 3, 2),
+        (gy > 0, (mp, gx, gy - 1), 2, 3),
+    ]
+    fills = [gx > 0, gx < ngx - 1, gy > 0, gy < ngy - 1]
+    edge0 = [e0n, e0s, e0w, e0e]
+
+    def halo_copy(stage, src, slot, dev):
+        srcs = edge0[src] if stage == 0 else edge1.at[src]
+        dsts = halo0.at[slot] if stage == 0 else halo1.at[slot]
+        return pltpu.make_async_remote_copy(
+            src_ref=srcs,
+            dst_ref=dsts,
+            send_sem=hsend.at[stage, slot],
+            recv_sem=hrecv.at[stage, slot],
+            device_id=dev,
+            device_id_type=mesh_id,
+        )
+
+    def send_halos(stage):
+        for present, dev, src, slot in links:
+            pl.when(present)(halo_copy(stage, src, slot, dev).start)
+
+    def take_halos(stage, dst):
+        for present, dev, src, slot in links:
+            pl.when(present)(halo_copy(stage, src, slot, dev).wait_send)
+        for slot, filled in enumerate(fills):
+            _, dev, src, _ = links[slot]
+            pl.when(filled)(halo_copy(stage, src, slot, dev).wait_recv)
+
+            @pl.when(jnp.logical_not(filled))
+            def _():
+                dst[slot] = jnp.zeros_like(dst[slot])
+
+    def bucket_copy(d):
+        return pltpu.make_async_remote_copy(
+            src_ref=buckets_ref.at[d],
+            dst_ref=recv.at[me],
+            send_sem=send_sem.at[d],
+            recv_sem=recv_sem.at[me],
+            device_id=(mp, d // ngy, d % ngy),
+            device_id_type=mesh_id,
+        )
+
+    def issue(k0, count):
+        for n in range(count):
+            k = k0 + n
+
+            @pl.when(k < ndev)
+            def _():
+                bucket_copy((me + k) % ndev).start()
+
+    lane = lax.broadcasted_iota(jnp.int32, qw_ref.shape, 1)
+    row = lax.broadcasted_iota(jnp.int32, (rows, cols), 0)
+    col = lax.broadcasted_iota(jnp.int32, (rows, cols), 1)
+    horiz = coef_ref[0]
+    vert = coef_ref[1]
+
+    def step(load, above, below, hn, hs, hw_t, he_t, store):
+        for l in range(LB):
+            u = load(l)
+            prev = load(l - 1) if l > 0 else above
+            nxt = load(l + 1) if l < LB - 1 else below
+            w = wet * u
+            north = jnp.where(row == 0, hn[l:l + 1, :], pltpu.roll(w, 1, 0))
+            south = jnp.where(row == rows - 1, hs[l:l + 1, :], pltpu.roll(w, rows - 1, 0))
+            west = jnp.where(col == 0, hw_t[:, l:l + 1], pltpu.roll(w, 1, 1))
+            east = jnp.where(col == cols - 1, he_t[:, l:l + 1], pltpu.roll(w, cols - 1, 1))
+            lateral = north + south + west + east - 4.0 * w
+            vertical = prev + nxt - 2.0 * u
+            store(l, wet * (u + horiz * lateral + vert * vertical))
+
+    @pl.when((p == 0) & (i == 0))
+    def _():
+        barrier = pltpu.get_barrier_semaphore()
+
+        def greet(d, carry):
+            @pl.when(d != me)
+            def _():
+                pl.semaphore_signal(barrier, 1, device_id=(mp, d // ngy, d % ngy), device_id_type=mesh_id)
+
+            return carry
+
+        lax.fori_loop(0, ndev, greet, 0)
+        pl.semaphore_wait(barrier, ndev - 1)
+        send_halos(0)
+        recv[me] = buckets_ref[me]
+        take_halos(0, halo0)
+        qw_ref[...] = jnp.zeros_like(qw_ref)
+        qe_ref[...] = jnp.zeros_like(qe_ref)
+
+    @pl.when(p == 0)
+    def _():
+        issue(1 + 2 * i, 2)
+        blk = pl.ds(pl.multiple_of(i * LB, LB), LB)
+        hn = halo0[0, blk]
+        hs = halo0[1, blk]
+        hw_t = jnp.transpose(halo0[2, blk])
+        he_t = jnp.transpose(halo0[3, blk])
+        above = above_ref[0] * jnp.where(i > 0, 1.0, 0.0)
+        below = below_ref[0] * jnp.where(i < nblk - 1, 1.0, 0.0)
+        qs = [qw_ref[...], qe_ref[...]]
+
+        def store(l, res):
+            first[i * LB + l] = res
+            fw = wet * res
+            edge1[0, i, l:l + 1, :] = fw[0:1, :]
+            edge1[1, i, l:l + 1, :] = fw[rows - 1:rows, :]
+            hit = lane == i * LB + l
+            qs[0] = jnp.where(hit, fw[:, 0:1], qs[0])
+            qs[1] = jnp.where(hit, fw[:, cols - 1:cols], qs[1])
+
+        step(lambda l: u_ref[l], above, below, hn, hs, hw_t, he_t, store)
+        qw_ref[...] = qs[0]
+        qe_ref[...] = qs[1]
+
+    @pl.when((p == 0) & (i == nblk - 1))
+    def _():
+        edge1[2] = jnp.transpose(qw_ref[...])[0:lev, :].reshape(nblk, LB, rows)
+        edge1[3] = jnp.transpose(qe_ref[...])[0:lev, :].reshape(nblk, LB, rows)
+        send_halos(1)
+
+    @pl.when((p == 1) & (i == 0))
+    def _():
+        take_halos(1, halo1)
+
+    @pl.when(p == 1)
+    def _():
+        issue(1 + 2 * nblk + 6 * i, 6)
+        base = i * LB
+        above = first[jnp.maximum(base - 1, 0)] * jnp.where(i > 0, 1.0, 0.0)
+        below = first[jnp.minimum(base + LB, lev - 1)] * jnp.where(i < nblk - 1, 1.0, 0.0)
+        hw_t = jnp.transpose(halo1[2, i])
+        he_t = jnp.transpose(halo1[3, i])
+
+        def store(l, res):
+            out_ref[l] = res
+
+        step(lambda l: first[base + l], above, below, halo1[0, i], halo1[1, i], hw_t, he_t, store)
+
+    @pl.when((p == 1) & (i == nblk - 1))
+    def _():
+        def wait(d, carry):
+            @pl.when(d != me)
+            def _():
+                copy = pltpu.make_async_remote_copy(
+                    src_ref=buckets_ref.at[d],
+                    dst_ref=recv.at[d],
+                    send_sem=send_sem.at[d],
+                    recv_sem=recv_sem.at[d],
+                    device_id=(mp, d // ngy, d % ngy),
+                    device_id_type=mesh_id,
+                )
+                copy.wait_send()
+                copy.wait_recv()
+
+            return carry
+
+        lax.fori_loop(0, ndev, wait, 0)
+        arrived_ref[...] = recv[...]
+
+
+def interval(coef, wet, u, buckets, edges):
+    lev, rows, cols = u.shape
+    nblk = lev // LB
+    assert 1 + 2 * nblk + 6 * nblk >= buckets.shape[0]
+    full2 = lambda shape: pl.BlockSpec(shape, lambda p, i: (0, 0))
+    whole = pl.BlockSpec(buckets.shape, lambda p, i: (0, 0, 0, 0))
+    held = lambda p, i: i + p * (nblk - 1 - i)
+    in_specs = [
+        pl.BlockSpec(memory_space=pltpu.SMEM),
+        full2((rows, cols)),
+        pl.BlockSpec((LB, rows, cols), lambda p, i: (held(p, i), 0, 0)),
+        pl.BlockSpec((1, rows, cols), lambda p, i: (jnp.maximum(held(p, i) * LB - 1, 0), 0, 0)),
+        pl.BlockSpec((1, rows, cols), lambda p, i: (jnp.minimum(held(p, i) * LB + LB, lev - 1), 0, 0)),
+        whole,
+    ] + [full2((lev, cols))] * 4
+    out_shape = [
+        jax.ShapeDtypeStruct((lev, rows, cols), jnp.float32),
+        jax.ShapeDtypeStruct(buckets.shape, buckets.dtype),
+    ]
+    out_specs = [pl.BlockSpec((LB, rows, cols), lambda p, i: (i * p, 0, 0)), whole]
+    scratch = [
+        pltpu.VMEM((lev, rows, cols), jnp.float32),
+        pltpu.VMEM((4, nblk, LB, cols), jnp.float32),
+        pltpu.VMEM((4, lev, cols), jnp.float32),
+        pltpu.VMEM((4, nblk, LB, cols), jnp.float32),
+        pltpu.VMEM((rows, 128), jnp.float32),
+        pltpu.VMEM((rows, 128), jnp.float32),
+        pltpu.VMEM(buckets.shape, buckets.dtype),
+        pltpu.SemaphoreType.DMA((buckets.shape[0],)),
+        pltpu.SemaphoreType.DMA((buckets.shape[0],)),
+        pltpu.SemaphoreType.DMA((2, 4)),
+        pltpu.SemaphoreType.DMA((2, 4)),
+    ]
+    return pl.pallas_call(
+        interval_kernel,
+        grid=(2, nblk),
+        in_specs=in_specs,
+        out_specs=out_specs,
+        out_shape=out_shape,
+        scratch_shapes=scratch,
+        compiler_params=pltpu.CompilerParams(
+            dimension_semantics=("arbitrary", "arbitrary"), collective_id=3, has_side_effects=True,
+            vmem_limit_bytes=48 * 1024 * 1024,
+        ),
+        cost_estimate=pl.CostEstimate(flops=60 * u.size, bytes_accessed=12 * u.size, transcendentals=0),
+    )(coef, wet, u, u, u, buckets, *edges)
 
 
 def first_kernel(coef_ref, wet_ref, u_ref, above_ref, below_ref, buckets_ref,
@@ -537,7 +768,7 @@
         out_specs=pl.BlockSpec(memory_space=pltpu.VMEM),
         out_shape=jax.ShapeDtypeStruct((ndev, CAP + 1, KF, CY), jnp.float32),
     )(inv, labels, contrib)
-    first, en, es, ew, ee, arrived = first_step(coef, wet, state, buckets, masked_edges(wet, state))
+    second, arrived = interval(coef, wet, state, buckets, masked_edges(wet, state))
     got_rows = arrived[:, CAP, :, 0].astype(jnp.int32)
     select = (
         got_rows[:, :, None] == jnp.arange(rows_here, dtype=jnp.int32)[None, None, :]
@@ -547,8 +778,6 @@
     )
     received = lax.ppermute(sent, "mp", [(0, 1), (1, 0)])
 
-    halos1 = exchange(en, es, ew, ee, 1)
-    (second,) = stencil_step(coef, wet, first, halos1)
     second = add_force(second, wet, received[0])
     return (second[None], received[None])
 

time: 114 us -> 111 us (0.974)
  the two profiles are of different devices: /device:TPU:32 before, /device:TPU:1 now
where the time goes in v8:
time: 111 us
  Pallas kernels  77.5 us (70%)
  local copies, waits for them, and re-layouts  13.3 us (12%)
  matrix products  11 us (10%)
  other arithmetic  6.18 us (6%)
  waiting for transfers between devices  1.54 us (1%)
    pallas_call x1, Pallas kernels, interval(): pl.pallas_call(interval_kernel, grid=(2, nblk), in_specs=in_specs, out_sp...  64.4 us
    dot_general x1, matrix products, local(): jnp.einsum('tji,kti->tkj', tile_weights[0, 0, 0], picked, preferred_eleme...  8.86 us
    unnamed x16, local copies, waits for them, and re-layouts  7.18 us
    pallas_call x1, Pallas kernels, masked_edges(): pl.pallas_call(edges_kernel, grid=(lev // LB,), in_specs=[full2((rows, co...  7.09 us
    pallas_call x1, Pallas kernels, local(): pl.pallas_call(bucket_kernel, in_specs=[pl.BlockSpec(memory_space=pltpu.S...  4.53 us
  transfers between devices with their start and end apart: 1, of which 1 were waited for; matrix products, arithmetic and copies ran while one was open for 0% of the time, Pallas kernels for 0%

profile of v8, /device:TPU:1, one launch (start us, length us, event | category | flops | bytes accessed | tf_op | source)
XLA Modules:
  0.0 110.9 jit_solution(5784605745234034469)
XLA Ops:
  0.7 0.7 compare_select_fusion
  1.4 0.7 compare_and_fusion
  2.1 1.5 %convert_select_fusion.wet_ref = f32[128,128]{1,0:T(8,128)} fusion(s32[128,128]{1,0:T(8,128)} %param.9, pred[]{:T(512)S(6)} %eq.43), kind=kLoop, calls=%fused_computation.27 | loop fusion | flops 32768 | bytes 131073 | tf_op jit(solution)/shard_map/jit(_where)/select_n | solution.py:739
  3.6 0.7 fusion.18
  4.3 0.6 reduce-window.6
  5.1 0.8 fusion.17
  5.9 0.7 compare_select_fusion.1
  6.6 7.1 %shard_map.87 = (f32[64,128]{1,0:T(8,128)}, f32[64,128]{1,0:T(8,128)}, f32[64,128]{1,0:T(8,128)}, f32[64,128]{1,0:T(8,128)}) custom-call(f32[128,128]{1,0:T(8,128)} %convert_select_fusion.wet_ref, f32[64,128,128]{2,1,0:T(8,128)} %bitcast.59), custom_call_target="tpu_custom_call" | custom-call | flops 2097152 | bytes 4194304 | tf_op jit(solution)/shard_map/pallas_call | solution.py:566
  13.7 0.3 fusion.8
  14.1 2.1 %scatter_custom_fusion.1.lab_ref = s32[512]{0:T(512)} fusion(s32[256]{0:T(256)S(1)} %bitcast.70, s32[256]{0:T(256)} %bitcast.73, s32[]{:T(128)} %constant.15.clone.1), kind=kCustom, calls=%fused_computation.35 | custom fusion | bytes 2560 | tf_op jit(solution)/shard_map/scatter | solution.py:760
  16.2 1.9 %scatter_custom_fusion.inv_ref = s32[512]{0:T(512)} fusion(s32[256]{0:T(256)S(1)} %bitcast.71, s32[256]{0:T(256)S(1)} %iota.15, s32[]{:T(128)} %constant.24.clone.1), kind=kCustom, calls=%fused_computation.37 | custom fusion | bytes 2052 | tf_op jit(solution)/shard_map/scatter | solution.py:759
  18.2 0.8 gather_fusion
  19.0 8.9 %fusion.contrib_ref = f32[256,8,128]{2,1,0:T(8,128)} fusion(bf16[1,1,1,256,128,128]{5,4,3,2,1,0:T(8,128)(2,1)} %param.10, bf16[256,8,128]{2,1,0:T(8,128)(2,1)S(1)} %gather_fusion, pred[256]{0:T(512)(128)(4,1)S(1)} %compare_and_fusion), kind=kOutput, calls=%fused_computation.3 | convolution fusion | flops 67371008 | bytes 9961728 | tf_op jit(solution)/shard_map/tji,kti->tkj/dot_general | solution.py:752
  27.9 4.5 %shard_map.86.buckets_ref = f32[64,9,8,128]{3,2,1,0:T(8,128)} custom-call(s32[512]{0:T(512)} %scatter_custom_fusion.inv_ref, s32[512]{0:T(512)} %scatter_custom_fusion.1.lab_ref, f32[256,8,128]{2,1,0:T(8,128)} %fusion.contrib_ref), custom_call_target="tpu_custom_call" | custom-call | tf_op jit(solution)/shard_map/pallas_call | solution.py:761
  32.5 1.7 %copy-done = f32[64,9,8,128]{3,2,1,0:T(8,128)S(1)} copy-done((f32[64,9,8,128]{3,2,1,0:T(8,128)S(1)}, f32[64,9,8,128]{3,2,1,0:T(8,128)}, u32[]{:S(2)}) %copy-start) | copy-done | bytes 2359320
  34.1 64.4 %shard_map.88 = (f32[64,128,128]{2,1,0:T(8,128)}, f32[64,9,8,128]{3,2,1,0:T(8,128)S(1)}) custom-call(f32[2]{0:T(128)S(1)} %pad_maximum_fusion.coef_ref, f32[128,128]{1,0:T(8,128)S(1)} %copy-done.1, f32[64,128,128]{2,1,0:T(8,128)} %bitcast.60, f32[64,128,128]{2,1,0:T(8,128)} %bitcast.61, f32[64,128,128]{2,1,0:T(8,128)} %bitcast.62, ...), custom_call_target="tpu_custom_call" | custom-call | flops 62914560 | bytes 12582912 | tf_op jit(solution)/shard_map/pallas_call | solution.py:300
  98.5 0.3 slice.17
  99.0 2.2 %fusion.4 = f32[8,128,128]{2,1,0:T(8,128)S(1)} fusion(f32[64,8,8,128]{3,2,1,0:T(8,128)S(1)} %slice.17, s32[64,8]{0,1:T(8,128)S(1)} %bitcast.65), kind=kOutput, calls=%fused_computation.7 | convolution fusion | flops 805371904 | bytes 2623488 | tf_op jit(solution)/shard_map/scr,sckj->krj/dot_general | solution.py:776
  101.1 0.6 collective-permute-start
  101.7 1.5 %collective-permute-done = f32[8,128,128]{2,1,0:T(8,128)S(1)} collective-permute-done((f32[8,128,128]{2,1,0:T(8,128)S(1)}, f32[8,128,128]{2,1,0:T(8,128)S(1)}, u32[]{:S(2)}, u32[]{:S(2)}) %collective-permute-start) | collective-permute-done | bytes 524320 | tf_op jit(solution)/shard_map/ppermute | solution.py:779
  103.2 0.6 slice_bitcast_fusion.f_ref
  103.9 1.5 %shard_map.89 = f32[64,128,128]{2,1,0:T(8,128)} custom-call(f32[64,128,128]{2,1,0:T(8,128)} %get-tuple-element.12.x_ref, f32[128,128]{1,0:T(8,128)} %convert_select_fusion.wet_ref, f32[128,128]{1,0:T(8,128)} %slice_bitcast_fusion.f_ref), custom_call_target="tpu_custom_call", output_to_operand_aliasing={{}: (0, {})} | custom-call | tf_op jit(solution)/shard_map/pallas_call | solution.py:587
  105.4 4.7 %copy.36 = f32[1,64,128,128]{3,2,1,0:T(8,128)} copy(f32[1,64,128,128]{3,2,1,0:T(8,128)} %bitcast.63) | data formatting | bytes 8388608
  110.1 0.8 copy.37
  (21 shorter events, 0.5 us)
Async XLA Ops:
  0.6 13.1 %copy-start.6 = (f32[1,8,128,128]{3,2,1,0:T(8,128)S(1)}, f32[1,8,128,128]{3,2,1,0:T(8,128)}, u32[]{:S(2)}) copy-start(f32[1,8,128,128]{3,2,1,0:T(8,128)} %param.8) | copy-start | bytes 1572868
  3.6 10.1 %copy-start.1 = (f32[128,128]{1,0:T(8,128)S(1)}, f32[128,128]{1,0:T(8,128)}, u32[]{:S(2)}) copy-start(f32[128,128]{1,0:T(8,128)} %convert_select_fusion.wet_ref) | copy-start | bytes 196612
  19.0 13.4 %copy-start.2 = (f32[64,128]{1,0:T(8,128)S(1)}, f32[64,128]{1,0:T(8,128)}, u32[]{:S(2)}) copy-start(f32[64,128]{1,0:T(8,128)} %get-tuple-element.8.e0n) | copy-start | bytes 98308
  19.0 13.4 %copy-start.3 = (f32[64,128]{1,0:T(8,128)S(1)}, f32[64,128]{1,0:T(8,128)}, u32[]{:S(2)}) copy-start(f32[64,128]{1,0:T(8,128)} %get-tuple-element.9.e0s) | copy-start | bytes 98308
  19.0 13.4 %copy-start.4 = (f32[64,128]{1,0:T(8,128)S(1)}, f32[64,128]{1,0:T(8,128)}, u32[]{:S(2)}) copy-start(f32[64,128]{1,0:T(8,128)} %get-tuple-element.10.e0w) | copy-start | bytes 98308
  19.0 13.4 %copy-start.5 = (f32[64,128]{1,0:T(8,128)S(1)}, f32[64,128]{1,0:T(8,128)}, u32[]{:S(2)}) copy-start(f32[64,128]{1,0:T(8,128)} %get-tuple-element.11.e0e) | copy-start | bytes 98308
  32.5 1.7 %copy-start = (f32[64,9,8,128]{3,2,1,0:T(8,128)S(1)}, f32[64,9,8,128]{3,2,1,0:T(8,128)}, u32[]{:S(2)}) copy-start(f32[64,9,8,128]{3,2,1,0:T(8,128)} %shard_map.86.buckets_ref) | copy-start | bytes 7077892
  101.1 2.1 %collective-permute-start = (f32[8,128,128]{2,1,0:T(8,128)S(1)}, f32[8,128,128]{2,1,0:T(8,128)S(1)}, u32[]{:S(2)}, u32[]{:S(2)}) collective-permute-start(f32[8,128,128]{2,1,0:T(8,128)S(1)} %fusion.4), channel_id=1, source_target_pairs={{0,64},{64,0},{1,65},{65,1},{2,66},{66,2},{3,67},{67,3},{4,68},{68... | collective-permute-start | bytes 1572872 | tf_op jit(solution)/shard_map/ppermute | solution.py:779

commit v9 on v8

--- a/solution.py
+++ b/solution.py
@@ -195,7 +195,7 @@
 
     @pl.when(p == 0)
     def _():
-        issue(1 + 2 * i, 2)
+        issue(1 + 3 * i, 3)
         blk = pl.ds(pl.multiple_of(i * LB, LB), LB)
         hn = halo0[0, blk]
         hs = halo0[1, blk]
@@ -228,9 +228,14 @@
     def _():
         take_halos(1, halo1)
 
+        def late(k, carry):
+            bucket_copy((me + k) % ndev).start()
+            return carry
+
+        lax.fori_loop(min(1 + 3 * nblk, ndev), ndev, late, 0)
+
     @pl.when(p == 1)
     def _():
-        issue(1 + 2 * nblk + 6 * i, 6)
         base = i * LB
         above = first[jnp.maximum(base - 1, 0)] * jnp.where(i > 0, 1.0, 0.0)
         below = first[jnp.minimum(base + LB, lev - 1)] * jnp.where(i < nblk - 1, 1.0, 0.0)
@@ -267,7 +272,6 @@
 def interval(coef, wet, u, buckets, edges):
     lev, rows, cols = u.shape
     nblk = lev // LB
-    assert 1 + 2 * nblk + 6 * nblk >= buckets.shape[0]
     full2 = lambda shape: pl.BlockSpec(shape, lambda p, i: (0, 0))
     whole = pl.BlockSpec(buckets.shape, lambda p, i: (0, 0, 0, 0))
     held = lambda p, i: i + p * (nblk - 1 - i)

time: 111 us -> 110 us (level)
  the two profiles are of different devices: /device:TPU:1 before, /device:TPU:16 now
where the time goes in v9:
time: 110 us; the launch traced here: 109 us
  Pallas kernels  75.7 us (69%)
  local copies, waits for them, and re-layouts  13.3 us (12%)
  matrix products  11 us (10%)
  other arithmetic  6.18 us (6%)
  waiting for transfers between devices  1.89 us (2%)
    pallas_call x1, Pallas kernels, interval(): pl.pallas_call(interval_kernel, grid=(2, nblk), in_specs=in_specs, out_sp...  62.6 us
    dot_general x1, matrix products, local(): jnp.einsum('tji,kti->tkj', tile_weights[0, 0, 0], picked, preferred_eleme...  8.86 us
    unnamed x16, local copies, waits for them, and re-layouts  7.18 us
    pallas_call x1, Pallas kernels, masked_edges(): pl.pallas_call(edges_kernel, grid=(lev // LB,), in_specs=[full2((rows, co...  7.09 us
    pallas_call x1, Pallas kernels, local(): pl.pallas_call(bucket_kernel, in_specs=[pl.BlockSpec(memory_space=pltpu.S...  4.53 us
  transfers between devices with their start and end apart: 1, of which 1 were waited for; matrix products, arithmetic and copies ran while one was open for 0% of the time, Pallas kernels for 0%

profile of v9, /device:TPU:16, one launch (start us, length us, event | category | flops | bytes accessed | tf_op | source)
XLA Modules:
  0.0 108.9 jit_solution(16015311819147693074)
XLA Ops:
  0.7 0.7 compare_select_fusion
  1.4 0.7 compare_and_fusion
  2.1 1.5 %convert_select_fusion.wet_ref = f32[128,128]{1,0:T(8,128)} fusion(s32[128,128]{1,0:T(8,128)} %param.9, pred[]{:T(512)S(6)} %eq.43), kind=kLoop, calls=%fused_computation.27 | loop fusion | flops 32768 | bytes 131073 | tf_op jit(solution)/shard_map/jit(_where)/select_n | solution.py:743
  3.6 0.7 fusion.18
  4.3 0.6 reduce-window.6
  4.9 0.2 slice_reduce_fusion
  5.1 0.8 fusion.17
  5.9 0.7 compare_select_fusion.1
  6.6 7.1 %shard_map.87 = (f32[64,128]{1,0:T(8,128)}, f32[64,128]{1,0:T(8,128)}, f32[64,128]{1,0:T(8,128)}, f32[64,128]{1,0:T(8,128)}) custom-call(f32[128,128]{1,0:T(8,128)} %convert_select_fusion.wet_ref, f32[64,128,128]{2,1,0:T(8,128)} %bitcast.59), custom_call_target="tpu_custom_call" | custom-call | flops 2097152 | bytes 4194304 | tf_op jit(solution)/shard_map/pallas_call | solution.py:570
  13.7 0.3 fusion.8
  14.1 2.1 %scatter_custom_fusion.1.lab_ref = s32[512]{0:T(512)} fusion(s32[256]{0:T(256)S(1)} %bitcast.70, s32[256]{0:T(256)} %bitcast.73, s32[]{:T(128)} %constant.15.clone.1), kind=kCustom, calls=%fused_computation.35 | custom fusion | bytes 2560 | tf_op jit(solution)/shard_map/scatter | solution.py:764
  16.2 1.9 %scatter_custom_fusion.inv_ref = s32[512]{0:T(512)} fusion(s32[256]{0:T(256)S(1)} %bitcast.71, s32[256]{0:T(256)S(1)} %iota.15, s32[]{:T(128)} %constant.24.clone.1), kind=kCustom, calls=%fused_computation.37 | custom fusion | bytes 2052 | tf_op jit(solution)/shard_map/scatter | solution.py:763
  18.2 0.8 gather_fusion
  19.0 8.9 %fusion.contrib_ref = f32[256,8,128]{2,1,0:T(8,128)} fusion(bf16[1,1,1,256,128,128]{5,4,3,2,1,0:T(8,128)(2,1)} %param.10, bf16[256,8,128]{2,1,0:T(8,128)(2,1)S(1)} %gather_fusion, pred[256]{0:T(512)(128)(4,1)S(1)} %compare_and_fusion), kind=kOutput, calls=%fused_computation.3 | convolution fusion | flops 67371008 | bytes 9961728 | tf_op jit(solution)/shard_map/tji,kti->tkj/dot_general | solution.py:756
  27.9 4.5 %shard_map.86.buckets_ref = f32[64,9,8,128]{3,2,1,0:T(8,128)} custom-call(s32[512]{0:T(512)} %scatter_custom_fusion.inv_ref, s32[512]{0:T(512)} %scatter_custom_fusion.1.lab_ref, f32[256,8,128]{2,1,0:T(8,128)} %fusion.contrib_ref), custom_call_target="tpu_custom_call" | custom-call | tf_op jit(solution)/shard_map/pallas_call | solution.py:765
  32.5 1.7 %copy-done = f32[64,9,8,128]{3,2,1,0:T(8,128)S(1)} copy-done((f32[64,9,8,128]{3,2,1,0:T(8,128)S(1)}, f32[64,9,8,128]{3,2,1,0:T(8,128)}, u32[]{:S(2)}) %copy-start) | copy-done | bytes 2359320
  34.1 62.6 %shard_map.88 = (f32[64,128,128]{2,1,0:T(8,128)}, f32[64,9,8,128]{3,2,1,0:T(8,128)S(1)}) custom-call(f32[2]{0:T(128)S(1)} %pad_maximum_fusion.coef_ref, f32[128,128]{1,0:T(8,128)S(1)} %copy-done.1, f32[64,128,128]{2,1,0:T(8,128)} %bitcast.60, f32[64,128,128]{2,1,0:T(8,128)} %bitcast.61, f32[64,128,128]{2,1,0:T(8,128)} %bitcast.62, ...), custom_call_target="tpu_custom_call" | custom-call | flops 62914560 | bytes 12582912 | tf_op jit(solution)/shard_map/pallas_call | solution.py:304
  96.7 0.3 slice.17
  97.1 2.2 %fusion.4 = f32[8,128,128]{2,1,0:T(8,128)S(1)} fusion(f32[64,8,8,128]{3,2,1,0:T(8,128)S(1)} %slice.17, s32[64,8]{0,1:T(8,128)S(1)} %bitcast.65), kind=kOutput, calls=%fused_computation.7 | convolution fusion | flops 805371904 | bytes 2623488 | tf_op jit(solution)/shard_map/scr,sckj->krj/dot_general | solution.py:780
  99.4 1.9 %collective-permute-done = f32[8,128,128]{2,1,0:T(8,128)S(1)} collective-permute-done((f32[8,128,128]{2,1,0:T(8,128)S(1)}, f32[8,128,128]{2,1,0:T(8,128)S(1)}, u32[]{:S(2)}, u32[]{:S(2)}) %collective-permute-start) | collective-permute-done | bytes 524320 | tf_op jit(solution)/shard_map/ppermute | solution.py:783
  101.3 0.6 slice_bitcast_fusion.f_ref
  101.9 1.5 %shard_map.89 = f32[64,128,128]{2,1,0:T(8,128)} custom-call(f32[64,128,128]{2,1,0:T(8,128)} %get-tuple-element.12.x_ref, f32[128,128]{1,0:T(8,128)} %convert_select_fusion.wet_ref, f32[128,128]{1,0:T(8,128)} %slice_bitcast_fusion.f_ref), custom_call_target="tpu_custom_call", output_to_operand_aliasing={{}: (0, {})} | custom-call | tf_op jit(solution)/shard_map/pallas_call | solution.py:591
  103.5 4.7 %copy.36 = f32[1,64,128,128]{3,2,1,0:T(8,128)} copy(f32[1,64,128,128]{3,2,1,0:T(8,128)} %bitcast.63) | data formatting | bytes 8388608
  108.2 0.8 copy.37
  (21 shorter events, 0.4 us)
Async XLA Ops:
  0.6 13.1 %copy-start.6 = (f32[1,8,128,128]{3,2,1,0:T(8,128)S(1)}, f32[1,8,128,128]{3,2,1,0:T(8,128)}, u32[]{:S(2)}) copy-start(f32[1,8,128,128]{3,2,1,0:T(8,128)} %param.8) | copy-start | bytes 1572868
  3.6 10.1 %copy-start.1 = (f32[128,128]{1,0:T(8,128)S(1)}, f32[128,128]{1,0:T(8,128)}, u32[]{:S(2)}) copy-start(f32[128,128]{1,0:T(8,128)} %convert_select_fusion.wet_ref) | copy-start | bytes 196612
  19.0 13.4 %copy-start.2 = (f32[64,128]{1,0:T(8,128)S(1)}, f32[64,128]{1,0:T(8,128)}, u32[]{:S(2)}) copy-start(f32[64,128]{1,0:T(8,128)} %get-tuple-element.8.e0n) | copy-start | bytes 98308
  19.0 13.4 %copy-start.3 = (f32[64,128]{1,0:T(8,128)S(1)}, f32[64,128]{1,0:T(8,128)}, u32[]{:S(2)}) copy-start(f32[64,128]{1,0:T(8,128)} %get-tuple-element.9.e0s) | copy-start | bytes 98308
  19.0 13.4 %copy-start.4 = (f32[64,128]{1,0:T(8,128)S(1)}, f32[64,128]{1,0:T(8,128)}, u32[]{:S(2)}) copy-start(f32[64,128]{1,0:T(8,128)} %get-tuple-element.10.e0w) | copy-start | bytes 98308
  19.0 13.4 %copy-start.5 = (f32[64,128]{1,0:T(8,128)S(1)}, f32[64,128]{1,0:T(8,128)}, u32[]{:S(2)}) copy-start(f32[64,128]{1,0:T(8,128)} %get-tuple-element.11.e0e) | copy-start | bytes 98308
  32.5 1.7 %copy-start = (f32[64,9,8,128]{3,2,1,0:T(8,128)S(1)}, f32[64,9,8,128]{3,2,1,0:T(8,128)}, u32[]{:S(2)}) copy-start(f32[64,9,8,128]{3,2,1,0:T(8,128)} %shard_map.86.buckets_ref) | copy-start | bytes 7077892
  99.3 2.0 %collective-permute-start = (f32[8,128,128]{2,1,0:T(8,128)S(1)}, f32[8,128,128]{2,1,0:T(8,128)S(1)}, u32[]{:S(2)}, u32[]{:S(2)}) collective-permute-start(f32[8,128,128]{2,1,0:T(8,128)S(1)} %fusion.4), channel_id=1, source_target_pairs={{0,64},{64,0},{1,65},{65,1},{2,66},{66,2},{3,67},{67,3},{4,68},{68... | collective-permute-start | bytes 1572872 | tf_op jit(solution)/shard_map/ppermute | solution.py:783

commit v10 on v9

--- a/solution.py
+++ b/solution.py
@@ -581,20 +581,24 @@
 
 
 def force_kernel(x_ref, wet_ref, f_ref, out_ref):
-    out_ref[0] = x_ref[0] + force_gain * wet_ref[...] * f_ref[...]
+    out_ref[...] = x_ref[...]
+
+    @pl.when(pl.program_id(0) == 0)
+    def _():
+        out_ref[0] = x_ref[0] + force_gain * wet_ref[...] * f_ref[...]
 
 
 def add_force(x, wet, f):
     lev, rows, cols = x.shape
     plane = pl.BlockSpec((rows, cols), lambda i: (0, 0))
-    level0 = pl.BlockSpec((1, rows, cols), lambda i: (0, 0, 0))
+    blocks = pl.BlockSpec((LB, rows, cols), lambda i: (i, 0, 0))
     return pl.pallas_call(
         force_kernel,
-        grid=(1,),
-        in_specs=[level0, plane, plane],
-        out_specs=level0,
+        grid=(lev // LB,),
+        in_specs=[blocks, plane, plane],
+        out_specs=blocks,
         out_shape=jax.ShapeDtypeStruct(x.shape, x.dtype),
-        input_output_aliases={0: 0},
+        cost_estimate=pl.CostEstimate(flops=x.size, bytes_accessed=8 * x.size, transcendentals=0),
     )(x, wet, f)
 
 

time: 110 us -> 110 us (level)
  Pallas kernels: 75.7 us -> 80.8 us
  local copies, waits for them, and re-layouts: 13.3 us -> 8.57 us
    pallas_call x1, Pallas kernels: 1.53 us -> 6.61 us  [add_force(): pl.pallas_call(force_kernel, grid=(lev // LB,), in_specs=[blocks, plane,...]
    unnamed x16 -> x15, local copies, waits for them, and re-layouts: 7.18 us -> 2.48 us
where the time goes in v10:
time: 110 us; the launch traced here: 109 us
  Pallas kernels  80.8 us (73%)
  matrix products  11 us (10%)
  local copies, waits for them, and re-layouts  8.57 us (8%)
  other arithmetic  6.19 us (6%)
  waiting for transfers between devices  1.88 us (2%)
    pallas_call x1, Pallas kernels, interval(): pl.pallas_call(interval_kernel, grid=(2, nblk), in_specs=in_specs, out_sp...  62.6 us
    dot_general x1, matrix products, local(): jnp.einsum('tji,kti->tkj', tile_weights[0, 0, 0], picked, preferred_eleme...  8.84 us
    pallas_call x1, Pallas kernels, masked_edges(): pl.pallas_call(edges_kernel, grid=(lev // LB,), in_specs=[full2((rows, co...  7.09 us
    pallas_call x1, Pallas kernels, add_force(): pl.pallas_call(force_kernel, grid=(lev // LB,), in_specs=[blocks, plane,...  6.61 us
    pallas_call x1, Pallas kernels, local(): pl.pallas_call(bucket_kernel, in_specs=[pl.BlockSpec(memory_space=pltpu.S...  4.55 us
    unnamed x15, local copies, waits for them, and re-layouts  2.48 us
  transfers between devices with their start and end apart: 1, of which 1 were waited for; matrix products, arithmetic and copies ran while one was open for 0% of the time, Pallas kernels for 0%

profile of v10, /device:TPU:16, one launch (start us, length us, event | category | flops | bytes accessed | tf_op | source)
XLA Modules:
  0.0 109.3 jit_solution(10388883542783964362)
XLA Ops:
  0.6 0.7 compare_select_fusion
  1.3 0.7 compare_and_fusion
  2.0 1.5 %convert_select_fusion.wet_ref = f32[128,128]{1,0:T(8,128)} fusion(s32[128,128]{1,0:T(8,128)} %param.9, pred[]{:T(512)S(6)} %eq.43), kind=kLoop, calls=%fused_computation.27 | loop fusion | flops 32768 | bytes 131073 | tf_op jit(solution)/shard_map/jit(_where)/select_n | solution.py:747
  3.6 0.7 fusion.18
  4.3 0.6 reduce-window.6
  4.9 0.2 slice_reduce_fusion
  5.1 0.8 fusion.17
  5.9 0.7 compare_select_fusion.1
  6.6 7.1 %shard_map.87 = (f32[64,128]{1,0:T(8,128)}, f32[64,128]{1,0:T(8,128)}, f32[64,128]{1,0:T(8,128)}, f32[64,128]{1,0:T(8,128)}) custom-call(f32[128,128]{1,0:T(8,128)} %convert_select_fusion.wet_ref, f32[64,128,128]{2,1,0:T(8,128)} %bitcast.59), custom_call_target="tpu_custom_call" | custom-call | flops 2097152 | bytes 4194304 | tf_op jit(solution)/shard_map/pallas_call | solution.py:570
  13.7 0.3 fusion.8
  14.1 2.1 %scatter_custom_fusion.1.lab_ref = s32[512]{0:T(512)} fusion(s32[256]{0:T(256)S(1)} %bitcast.70, s32[256]{0:T(256)} %bitcast.73, s32[]{:T(128)} %constant.15.clone.1), kind=kCustom, calls=%fused_computation.35 | custom fusion | bytes 2560 | tf_op jit(solution)/shard_map/scatter | solution.py:768
  16.2 1.9 %scatter_custom_fusion.inv_ref = s32[512]{0:T(512)} fusion(s32[256]{0:T(256)S(1)} %bitcast.71, s32[256]{0:T(256)S(1)} %iota.15, s32[]{:T(128)} %constant.24.clone.1), kind=kCustom, calls=%fused_computation.37 | custom fusion | bytes 2052 | tf_op jit(solution)/shard_map/scatter | solution.py:767
  18.2 0.8 gather_fusion
  19.0 8.8 %fusion.contrib_ref = f32[256,8,128]{2,1,0:T(8,128)} fusion(bf16[1,1,1,256,128,128]{5,4,3,2,1,0:T(8,128)(2,1)} %param.10, bf16[256,8,128]{2,1,0:T(8,128)(2,1)S(1)} %gather_fusion, pred[256]{0:T(512)(128)(4,1)S(1)} %compare_and_fusion), kind=kOutput, calls=%fused_computation.3 | convolution fusion | flops 67371008 | bytes 9961728 | tf_op jit(solution)/shard_map/tji,kti->tkj/dot_general | solution.py:760
  27.9 4.6 %shard_map.86.buckets_ref = f32[64,9,8,128]{3,2,1,0:T(8,128)} custom-call(s32[512]{0:T(512)} %scatter_custom_fusion.inv_ref, s32[512]{0:T(512)} %scatter_custom_fusion.1.lab_ref, f32[256,8,128]{2,1,0:T(8,128)} %fusion.contrib_ref), custom_call_target="tpu_custom_call" | custom-call | tf_op jit(solution)/shard_map/pallas_call | solution.py:769
  32.4 1.7 %copy-done = f32[64,9,8,128]{3,2,1,0:T(8,128)S(1)} copy-done((f32[64,9,8,128]{3,2,1,0:T(8,128)S(1)}, f32[64,9,8,128]{3,2,1,0:T(8,128)}, u32[]{:S(2)}) %copy-start) | copy-done | bytes 2359320
  34.1 62.6 %shard_map.88 = (f32[64,128,128]{2,1,0:T(8,128)}, f32[64,9,8,128]{3,2,1,0:T(8,128)S(1)}) custom-call(f32[2]{0:T(128)S(1)} %pad_maximum_fusion.coef_ref, f32[128,128]{1,0:T(8,128)S(1)} %copy-done.1, f32[64,128,128]{2,1,0:T(8,128)} %bitcast.60, f32[64,128,128]{2,1,0:T(8,128)} %bitcast.61, f32[64,128,128]{2,1,0:T(8,128)} %bitcast.62, ...), custom_call_target="tpu_custom_call" | custom-call | flops 62914560 | bytes 12582912 | tf_op jit(solution)/shard_map/pallas_call | solution.py:304
  96.7 0.3 slice.17
  97.0 0.1 copy.20
  97.1 2.1 %fusion.4 = f32[8,128,128]{2,1,0:T(8,128)S(1)} fusion(f32[64,8,8,128]{3,2,1,0:T(8,128)S(1)} %slice.17, s32[64,8]{0,1:T(8,128)S(1)} %bitcast.65), kind=kOutput, calls=%fused_computation.7 | convolution fusion | flops 805371904 | bytes 2623488 | tf_op jit(solution)/shard_map/scr,sckj->krj/dot_general | solution.py:784
  99.4 1.9 %collective-permute-done = f32[8,128,128]{2,1,0:T(8,128)S(1)} collective-permute-done((f32[8,128,128]{2,1,0:T(8,128)S(1)}, f32[8,128,128]{2,1,0:T(8,128)S(1)}, u32[]{:S(2)}, u32[]{:S(2)}) %collective-permute-start) | collective-permute-done | bytes 524320 | tf_op jit(solution)/shard_map/ppermute | solution.py:787
  101.3 0.6 slice_bitcast_fusion.f_ref
  101.9 6.6 %shard_map.89 = f32[64,128,128]{2,1,0:T(8,128)} custom-call(f32[64,128,128]{2,1,0:T(8,128)} %get-tuple-element.12.x_ref, f32[128,128]{1,0:T(8,128)} %convert_select_fusion.wet_ref, f32[128,128]{1,0:T(8,128)} %slice_bitcast_fusion.f_ref), custom_call_target="tpu_custom_call" | custom-call | flops 1048576 | bytes 8388608 | tf_op jit(solution)/shard_map/pallas_call | solution.py:595
  108.5 0.8 copy.33
  (20 shorter events, 0.3 us)
Async XLA Ops:
  2.0 11.7 %copy-start.6 = (f32[1,8,128,128]{3,2,1,0:T(8,128)S(1)}, f32[1,8,128,128]{3,2,1,0:T(8,128)}, u32[]{:S(2)}) copy-start(f32[1,8,128,128]{3,2,1,0:T(8,128)} %param.8) | copy-start | bytes 1572868
  3.6 10.1 %copy-start.1 = (f32[128,128]{1,0:T(8,128)S(1)}, f32[128,128]{1,0:T(8,128)}, u32[]{:S(2)}) copy-start(f32[128,128]{1,0:T(8,128)} %convert_select_fusion.wet_ref) | copy-start | bytes 196612
  27.8 4.6 %copy-start.2 = (f32[64,128]{1,0:T(8,128)S(1)}, f32[64,128]{1,0:T(8,128)}, u32[]{:S(2)}) copy-start(f32[64,128]{1,0:T(8,128)} %get-tuple-element.8.e0n) | copy-start | bytes 98308
  27.8 4.6 %copy-start.3 = (f32[64,128]{1,0:T(8,128)S(1)}, f32[64,128]{1,0:T(8,128)}, u32[]{:S(2)}) copy-start(f32[64,128]{1,0:T(8,128)} %get-tuple-element.9.e0s) | copy-start | bytes 98308
  27.8 4.6 %copy-start.4 = (f32[64,128]{1,0:T(8,128)S(1)}, f32[64,128]{1,0:T(8,128)}, u32[]{:S(2)}) copy-start(f32[64,128]{1,0:T(8,128)} %get-tuple-element.10.e0w) | copy-start | bytes 98308
  27.9 4.6 %copy-start.5 = (f32[64,128]{1,0:T(8,128)S(1)}, f32[64,128]{1,0:T(8,128)}, u32[]{:S(2)}) copy-start(f32[64,128]{1,0:T(8,128)} %get-tuple-element.11.e0e) | copy-start | bytes 98308
  32.4 1.7 %copy-start = (f32[64,9,8,128]{3,2,1,0:T(8,128)S(1)}, f32[64,9,8,128]{3,2,1,0:T(8,128)}, u32[]{:S(2)}) copy-start(f32[64,9,8,128]{3,2,1,0:T(8,128)} %shard_map.86.buckets_ref) | copy-start | bytes 7077892
  99.3 2.0 %collective-permute-start = (f32[8,128,128]{2,1,0:T(8,128)S(1)}, f32[8,128,128]{2,1,0:T(8,128)S(1)}, u32[]{:S(2)}, u32[]{:S(2)}) collective-permute-start(f32[8,128,128]{2,1,0:T(8,128)S(1)} %fusion.4), channel_id=1, source_target_pairs={{0,64},{64,0},{1,65},{65,1},{2,66},{66,2},{3,67},{67,3},{4,68},{68... | collective-permute-start | bytes 1572872 | tf_op jit(solution)/shard_map/ppermute | solution.py:787

commit v11 on v9

--- a/solution.py
+++ b/solution.py
@@ -532,35 +532,28 @@
             finish_spread(buckets_ref, recv, send_sem, recv_sem, arrived_ref)
 
 
-def edges_kernel(wet_ref, u_ref, en_ref, es_ref, ew_ref, ee_ref, qw_ref, qe_ref):
-    i = pl.program_id(0)
-    nblk = pl.num_programs(0)
+def edges_kernel(wet_ref, u_ref, en_ref, es_ref, ew_ref, ee_ref):
     wet = wet_ref[...]
     rows, cols = wet.shape
-
-    @pl.when(i == 0)
-    def _():
-        qw_ref[...] = jnp.zeros_like(qw_ref)
-        qe_ref[...] = jnp.zeros_like(qe_ref)
-
-    lane = lax.broadcasted_iota(jnp.int32, qw_ref.shape, 1)
-    qw = qw_ref[...]
-    qe = qe_ref[...]
+    fw = wet[None] * u_ref[...]
     for l in range(LB):
-        fw = wet * u_ref[l]
-        en_ref[l:l + 1, :] = fw[0:1, :]
-        es_ref[l:l + 1, :] = fw[rows - 1:rows, :]
-        hit = lane == i * LB + l
-        qw = jnp.where(hit, fw[:, 0:1], qw)
-        qe = jnp.where(hit, fw[:, cols - 1:cols], qe)
-    qw_ref[...] = qw
-    qe_ref[...] = qe
-
-    @pl.when(i == nblk - 1)
-    def _():
-        lev = ew_ref.shape[0]
-        ew_ref[...] = jnp.transpose(qw_ref[...])[0:lev, :]
-        ee_ref[...] = jnp.transpose(qe_ref[...])[0:lev, :]
+        en_ref[l:l + 1, :] = fw[l, 0:1, :]
+        es_ref[l:l + 1, :] = fw[l, rows - 1:rows, :]
+    pick_r = lax.broadcasted_iota(jnp.int32, (8, cols), 0)
+    pick_c = lax.broadcasted_iota(jnp.int32, (8, cols), 1)
+    pick = jnp.where(
+        ((pick_r == 0) & (pick_c == 0)) | ((pick_r == 1) & (pick_c == cols - 1)), 1.0, 0.0
+    ).astype(jnp.float32)
+    picked = lax.dot_general(
+        pick,
+        fw.reshape(LB * rows, cols),
+        (((1,), (1,)), ((), ())),
+        precision=lax.Precision.HIGHEST,
+        preferred_element_type=jnp.float32,
+    )
+    for l in range(LB):
+        ew_ref[l:l + 1, :] = picked[0:1, l * rows:(l + 1) * rows]
+        ee_ref[l:l + 1, :] = picked[1:2, l * rows:(l + 1) * rows]
 
 
 def masked_edges(wet, u):
@@ -571,10 +564,9 @@
         edges_kernel,
         grid=(lev // LB,),
         in_specs=[full2((rows, cols)), pl.BlockSpec((LB, rows, cols), lambda i: (i, 0, 0))],
-        out_specs=[lvl2, lvl2, full2((lev, rows)), full2((lev, rows))],
+        out_specs=[lvl2] * 4,
         out_shape=[jax.ShapeDtypeStruct((lev, cols), jnp.float32)] * 2
         + [jax.ShapeDtypeStruct((lev, rows), jnp.float32)] * 2,
-        scratch_shapes=[pltpu.VMEM((rows, 128), jnp.float32)] * 2,
         compiler_params=pltpu.CompilerParams(dimension_semantics=("arbitrary",)),
         cost_estimate=pl.CostEstimate(flops=2 * u.size, bytes_accessed=4 * u.size, transcendentals=0),
     )(wet, u)

time: 110 us -> 110 us (level)
  no operation moved by 1% of the time
where the time goes in v11:
time: 110 us; the launch traced here: 109 us
  Pallas kernels  76.2 us (69%)
  local copies, waits for them, and re-layouts  13.3 us (12%)
  matrix products  11 us (10%)
  other arithmetic  6.18 us (6%)
  waiting for transfers between devices  1.89 us (2%)
    pallas_call x1, Pallas kernels, interval(): pl.pallas_call(interval_kernel, grid=(2, nblk), in_specs=in_specs, out_sp...  62.5 us
    dot_general x1, matrix products, local(): jnp.einsum('tji,kti->tkj', tile_weights[0, 0, 0], picked, preferred_eleme...  8.86 us
    pallas_call x1, Pallas kernels, masked_edges(): pl.pallas_call(edges_kernel, grid=(lev // LB,), in_specs=[full2((rows, co...  7.62 us
    unnamed x16, local copies, waits for them, and re-layouts  7.18 us
    pallas_call x1, Pallas kernels, local(): pl.pallas_call(bucket_kernel, in_specs=[pl.BlockSpec(memory_space=pltpu.S...  4.53 us
  transfers between devices with their start and end apart: 1, of which 1 were waited for; matrix products, arithmetic and copies ran while one was open for 0% of the time, Pallas kernels for 0%

profile of v11, /device:TPU:16, one launch (start us, length us, event | category | flops | bytes accessed | tf_op | source)
XLA Modules:
  0.0 109.4 jit_solution(15930409923016011780)
XLA Ops:
  0.7 0.7 compare_select_fusion
  1.4 0.7 compare_and_fusion
  2.1 1.5 %convert_select_fusion.wet_ref = f32[128,128]{1,0:T(8,128)} fusion(s32[128,128]{1,0:T(8,128)} %param.9, pred[]{:T(512)S(6)} %eq.43), kind=kLoop, calls=%fused_computation.27 | loop fusion | flops 32768 | bytes 131073 | tf_op jit(solution)/shard_map/jit(_where)/select_n | solution.py:735
  3.6 0.7 fusion.18
  4.3 0.6 reduce-window.6
  4.9 0.2 slice_reduce_fusion
  5.1 0.8 fusion.17
  5.9 0.7 compare_select_fusion.1
  6.6 7.6 %shard_map.87 = (f32[64,128]{1,0:T(8,128)}, f32[64,128]{1,0:T(8,128)}, f32[64,128]{1,0:T(8,128)}, f32[64,128]{1,0:T(8,128)}) custom-call(f32[128,128]{1,0:T(8,128)} %convert_select_fusion.wet_ref, f32[64,128,128]{2,1,0:T(8,128)} %bitcast.59), custom_call_target="tpu_custom_call" | custom-call | flops 2097152 | bytes 4194304 | tf_op jit(solution)/shard_map/pallas_call | solution.py:563
  14.2 0.3 fusion.8
  14.6 2.1 %scatter_custom_fusion.1.lab_ref = s32[512]{0:T(512)} fusion(s32[256]{0:T(256)S(1)} %bitcast.70, s32[256]{0:T(256)} %bitcast.73, s32[]{:T(128)} %constant.15.clone.1), kind=kCustom, calls=%fused_computation.35 | custom fusion | bytes 2560 | tf_op jit(solution)/shard_map/scatter | solution.py:756
  16.7 1.9 %scatter_custom_fusion.inv_ref = s32[512]{0:T(512)} fusion(s32[256]{0:T(256)S(1)} %bitcast.71, s32[256]{0:T(256)S(1)} %iota.15, s32[]{:T(128)} %constant.24.clone.1), kind=kCustom, calls=%fused_computation.37 | custom fusion | bytes 2052 | tf_op jit(solution)/shard_map/scatter | solution.py:755
  18.7 0.8 gather_fusion
  19.6 8.9 %fusion.contrib_ref = f32[256,8,128]{2,1,0:T(8,128)} fusion(bf16[1,1,1,256,128,128]{5,4,3,2,1,0:T(8,128)(2,1)} %param.10, bf16[256,8,128]{2,1,0:T(8,128)(2,1)S(1)} %gather_fusion, pred[256]{0:T(512)(128)(4,1)S(1)} %compare_and_fusion), kind=kOutput, calls=%fused_computation.3 | convolution fusion | flops 67371008 | bytes 9961728 | tf_op jit(solution)/shard_map/tji,kti->tkj/dot_general | solution.py:748
  28.4 4.5 %shard_map.86.buckets_ref = f32[64,9,8,128]{3,2,1,0:T(8,128)} custom-call(s32[512]{0:T(512)} %scatter_custom_fusion.inv_ref, s32[512]{0:T(512)} %scatter_custom_fusion.1.lab_ref, f32[256,8,128]{2,1,0:T(8,128)} %fusion.contrib_ref), custom_call_target="tpu_custom_call" | custom-call | tf_op jit(solution)/shard_map/pallas_call | solution.py:757
  33.0 1.7 %copy-done = f32[64,9,8,128]{3,2,1,0:T(8,128)S(1)} copy-done((f32[64,9,8,128]{3,2,1,0:T(8,128)S(1)}, f32[64,9,8,128]{3,2,1,0:T(8,128)}, u32[]{:S(2)}) %copy-start) | copy-done | bytes 2359320
  34.6 62.5 %shard_map.88 = (f32[64,128,128]{2,1,0:T(8,128)}, f32[64,9,8,128]{3,2,1,0:T(8,128)S(1)}) custom-call(f32[2]{0:T(128)S(1)} %pad_maximum_fusion.coef_ref, f32[128,128]{1,0:T(8,128)S(1)} %copy-done.1, f32[64,128,128]{2,1,0:T(8,128)} %bitcast.60, f32[64,128,128]{2,1,0:T(8,128)} %bitcast.61, f32[64,128,128]{2,1,0:T(8,128)} %bitcast.62, ...), custom_call_target="tpu_custom_call" | custom-call | flops 62914560 | bytes 12582912 | tf_op jit(solution)/shard_map/pallas_call | solution.py:304
  97.2 0.3 slice.17
  97.6 2.1 %fusion.4 = f32[8,128,128]{2,1,0:T(8,128)S(1)} fusion(f32[64,8,8,128]{3,2,1,0:T(8,128)S(1)} %slice.17, s32[64,8]{0,1:T(8,128)S(1)} %bitcast.65), kind=kOutput, calls=%fused_computation.7 | convolution fusion | flops 805371904 | bytes 2623488 | tf_op jit(solution)/shard_map/scr,sckj->krj/dot_general | solution.py:772
  99.9 1.9 %collective-permute-done = f32[8,128,128]{2,1,0:T(8,128)S(1)} collective-permute-done((f32[8,128,128]{2,1,0:T(8,128)S(1)}, f32[8,128,128]{2,1,0:T(8,128)S(1)}, u32[]{:S(2)}, u32[]{:S(2)}) %collective-permute-start) | collective-permute-done | bytes 524320 | tf_op jit(solution)/shard_map/ppermute | solution.py:775
  101.7 0.6 slice_bitcast_fusion.f_ref
  102.4 1.5 %shard_map.89 = f32[64,128,128]{2,1,0:T(8,128)} custom-call(f32[64,128,128]{2,1,0:T(8,128)} %get-tuple-element.12.x_ref, f32[128,128]{1,0:T(8,128)} %convert_select_fusion.wet_ref, f32[128,128]{1,0:T(8,128)} %slice_bitcast_fusion.f_ref), custom_call_target="tpu_custom_call", output_to_operand_aliasing={{}: (0, {})} | custom-call | tf_op jit(solution)/shard_map/pallas_call | solution.py:583
  103.9 4.7 %copy.36 = f32[1,64,128,128]{3,2,1,0:T(8,128)} copy(f32[1,64,128,128]{3,2,1,0:T(8,128)} %bitcast.63) | data formatting | bytes 8388608
  108.6 0.8 copy.37
  (21 shorter events, 0.4 us)
Async XLA Ops:
  0.6 13.6 %copy-start.6 = (f32[1,8,128,128]{3,2,1,0:T(8,128)S(1)}, f32[1,8,128,128]{3,2,1,0:T(8,128)}, u32[]{:S(2)}) copy-start(f32[1,8,128,128]{3,2,1,0:T(8,128)} %param.8) | copy-start | bytes 1572868
  3.6 10.7 %copy-start.1 = (f32[128,128]{1,0:T(8,128)S(1)}, f32[128,128]{1,0:T(8,128)}, u32[]{:S(2)}) copy-start(f32[128,128]{1,0:T(8,128)} %convert_select_fusion.wet_ref) | copy-start | bytes 196612
  19.5 13.4 %copy-start.2 = (f32[64,128]{1,0:T(8,128)S(1)}, f32[64,128]{1,0:T(8,128)}, u32[]{:S(2)}) copy-start(f32[64,128]{1,0:T(8,128)} %get-tuple-element.8.e0n) | copy-start | bytes 98308
  19.5 13.4 %copy-start.3 = (f32[64,128]{1,0:T(8,128)S(1)}, f32[64,128]{1,0:T(8,128)}, u32[]{:S(2)}) copy-start(f32[64,128]{1,0:T(8,128)} %get-tuple-element.9.e0s) | copy-start | bytes 98308
  19.5 13.4 %copy-start.4 = (f32[64,128]{1,0:T(8,128)S(1)}, f32[64,128]{1,0:T(8,128)}, u32[]{:S(2)}) copy-start(f32[64,128]{1,0:T(8,128)} %get-tuple-element.10.e0w) | copy-start | bytes 98308
  19.5 13.4 %copy-start.5 = (f32[64,128]{1,0:T(8,128)S(1)}, f32[64,128]{1,0:T(8,128)}, u32[]{:S(2)}) copy-start(f32[64,128]{1,0:T(8,128)} %get-tuple-element.11.e0e) | copy-start | bytes 98308
  33.0 1.7 %copy-start = (f32[64,9,8,128]{3,2,1,0:T(8,128)S(1)}, f32[64,9,8,128]{3,2,1,0:T(8,128)}, u32[]{:S(2)}) copy-start(f32[64,9,8,128]{3,2,1,0:T(8,128)} %shard_map.86.buckets_ref) | copy-start | bytes 7077892
  99.8 2.0 %collective-permute-start = (f32[8,128,128]{2,1,0:T(8,128)S(1)}, f32[8,128,128]{2,1,0:T(8,128)S(1)}, u32[]{:S(2)}, u32[]{:S(2)}) collective-permute-start(f32[8,128,128]{2,1,0:T(8,128)S(1)} %fusion.4), channel_id=1, source_target_pairs={{0,64},{64,0},{1,65},{65,1},{2,66},{66,2},{3,67},{67,3},{4,68},{68... | collective-permute-start | bytes 1572872 | tf_op jit(solution)/shard_map/ppermute | solution.py:775

commit v12 on v9

--- a/solution.py
+++ b/solution.py
@@ -717,22 +717,20 @@
     )(en, es, ew, ee)
 
 
-def bucket_kernel(inv_ref, lab_ref, contrib_ref, out_ref):
-    ndest = out_ref.shape[0]
+def bucket_kernel(slot_ref, row_ref, contrib_ref, out_ref):
     ntiles = contrib_ref.shape[0]
     sub = lax.broadcasted_iota(jnp.int32, (KF, CY), 0)
-
-    def body(d, carry):
-        labv = jnp.zeros((KF, CY), jnp.float32)
-        for c in range(CAP):
-            t = inv_ref[d * CAP + c]
-            val = contrib_ref[jnp.minimum(t, ntiles - 1)]
-            out_ref[d, c] = jnp.where(t < ntiles, val, 0.0)
-            labv = jnp.where(sub == c, lab_ref[d * CAP + c].astype(jnp.float32), labv)
-        out_ref[d, CAP] = labv
+    out_ref[...] = jnp.zeros_like(out_ref)
+
+    def body(t, carry):
+        s = slot_ref[t]
+        d = s // CAP
+        c = s % CAP
+        out_ref[d, c] = contrib_ref[t]
+        out_ref[d, CAP] = jnp.where(sub == c, row_ref[t].astype(jnp.float32), out_ref[d, CAP])
         return carry
 
-    lax.fori_loop(0, ndest, body, 0)
+    lax.fori_loop(0, ntiles, body, 0)
 
 
 def local(states, surface, land_mask, tile_weights, tile_source, tile_target, tile_row):
@@ -760,8 +758,6 @@
     earlier = jnp.cumsum(onehot, axis=0) - onehot
     rank = jnp.sum(earlier * onehot, axis=1)
     slot = target * CAP + rank
-    inv = jnp.full((ndev * CAP,), ntiles, jnp.int32).at[slot].set(jnp.arange(ntiles, dtype=jnp.int32))
-    labels = jnp.zeros((ndev * CAP,), jnp.int32).at[slot].set(dest_row)
     buckets = pl.pallas_call(
         bucket_kernel,
         in_specs=[
@@ -771,7 +767,7 @@
         ],
         out_specs=pl.BlockSpec(memory_space=pltpu.VMEM),
         out_shape=jax.ShapeDtypeStruct((ndev, CAP + 1, KF, CY), jnp.float32),
-    )(inv, labels, contrib)
+    )(slot, dest_row, contrib)
     second, arrived = interval(coef, wet, state, buckets, masked_edges(wet, state))
     got_rows = arrived[:, CAP, :, 0].astype(jnp.int32)
     select = (

time: 110 us -> 109 us (level)
  local copies, waits for them, and re-layouts: 13.3 us -> 9.22 us
  Pallas kernels: 75.7 us -> 78.1 us
    scatter x2 -> x0, local copies, waits for them, and re-layouts: 4.04 us -> none  [the longest x1 2.1 us: local(): labels = jnp.zeros((ndev * CAP,), jnp.int32).at[slot].set(dest_row)]
    pallas_call x1, Pallas kernels: 4.53 us -> 6.97 us  [local(): pl.pallas_call(bucket_kernel, in_specs=[pl.BlockSpec(memory_space=pltpu.S...]
    add x0 -> x1, other arithmetic: none -> 1.26 us  [local(): slot = target * CAP + rank]
where the time goes in v12:
time: 109 us; the launch traced here: 108 us
  Pallas kernels  78.1 us (72%)
  matrix products  11 us (10%)
  local copies, waits for them, and re-layouts  9.22 us (8%)
  other arithmetic  6.75 us (6%)
  waiting for transfers between devices  1.89 us (2%)
    pallas_call x1, Pallas kernels, interval(): pl.pallas_call(interval_kernel, grid=(2, nblk), in_specs=in_specs, out_sp...  62.5 us
    dot_general x1, matrix products, local(): jnp.einsum('tji,kti->tkj', tile_weights[0, 0, 0], picked, preferred_eleme...  8.86 us
    unnamed x16, local copies, waits for them, and re-layouts  7.18 us
    pallas_call x1, Pallas kernels, masked_edges(): pl.pallas_call(edges_kernel, grid=(lev // LB,), in_specs=[full2((rows, co...  7.09 us
    pallas_call x1, Pallas kernels, local(): pl.pallas_call(bucket_kernel, in_specs=[pl.BlockSpec(memory_space=pltpu.S...  6.97 us
  transfers between devices with their start and end apart: 1, of which 1 were waited for; matrix products, arithmetic and copies ran while one was open for 0% of the time, Pallas kernels for 0%

profile of v12, /device:TPU:16, one launch (start us, length us, event | category | flops | bytes accessed | tf_op | source)
XLA Modules:
  0.0 107.8 jit_solution(2818496016771415371)
XLA Ops:
  0.7 0.7 compare_select_fusion
  1.4 0.7 compare_and_fusion
  2.1 1.5 %convert_select_fusion.wet_ref = f32[128,128]{1,0:T(8,128)} fusion(s32[128,128]{1,0:T(8,128)} %param.9, pred[]{:T(512)S(6)} %eq.41), kind=kLoop, calls=%fused_computation.25 | loop fusion | flops 32768 | bytes 131073 | tf_op jit(solution)/shard_map/jit(_where)/select_n | solution.py:741
  3.6 0.7 fusion.18
  4.3 0.6 reduce-window.6
  4.9 0.2 slice_reduce_fusion
  5.1 0.8 fusion.17
  5.9 1.3 %multiply_add_fusion.slot_ref = s32[256]{0:T(256)} fusion(s32[256]{0:T(256)S(1)} %fusion.17, s32[256]{0:T(256)} %bitcast.60), kind=kLoop, calls=%fused_computation.31 | loop fusion | flops 512 | bytes 3072 | tf_op jit(solution)/shard_map/add | solution.py:760
  7.2 7.1 %shard_map.87 = (f32[64,128]{1,0:T(8,128)}, f32[64,128]{1,0:T(8,128)}, f32[64,128]{1,0:T(8,128)}, f32[64,128]{1,0:T(8,128)}) custom-call(f32[128,128]{1,0:T(8,128)} %convert_select_fusion.wet_ref, f32[64,128,128]{2,1,0:T(8,128)} %bitcast.51), custom_call_target="tpu_custom_call" | custom-call | flops 2097152 | bytes 4194304 | tf_op jit(solution)/shard_map/pallas_call | solution.py:570
  14.3 0.3 fusion.8
  14.7 0.8 gather_fusion
  15.6 8.9 %fusion.contrib_ref = f32[256,8,128]{2,1,0:T(8,128)} fusion(bf16[1,1,1,256,128,128]{5,4,3,2,1,0:T(8,128)(2,1)} %param.10, bf16[256,8,128]{2,1,0:T(8,128)(2,1)S(1)} %gather_fusion, pred[256]{0:T(512)(128)(4,1)S(1)} %compare_and_fusion), kind=kOutput, calls=%fused_computation.1 | convolution fusion | flops 67371008 | bytes 9961728 | tf_op jit(solution)/shard_map/tji,kti->tkj/dot_general | solution.py:754
  24.4 7.0 %shard_map.86.buckets_ref = f32[64,9,8,128]{3,2,1,0:T(8,128)} custom-call(s32[256]{0:T(256)} %multiply_add_fusion.slot_ref, s32[256]{0:T(256)} %bitcast.62, f32[256,8,128]{2,1,0:T(8,128)} %fusion.contrib_ref), custom_call_target="tpu_custom_call" | custom-call | tf_op jit(solution)/shard_map/pallas_call | solution.py:761
  31.4 1.7 %copy-done = f32[64,9,8,128]{3,2,1,0:T(8,128)S(1)} copy-done((f32[64,9,8,128]{3,2,1,0:T(8,128)S(1)}, f32[64,9,8,128]{3,2,1,0:T(8,128)}, u32[]{:S(2)}) %copy-start) | copy-done | bytes 2359320
  33.1 62.5 %shard_map.88 = (f32[64,128,128]{2,1,0:T(8,128)}, f32[64,9,8,128]{3,2,1,0:T(8,128)S(1)}) custom-call(f32[2]{0:T(128)S(1)} %pad_maximum_fusion.coef_ref, f32[128,128]{1,0:T(8,128)S(1)} %copy-done.1, f32[64,128,128]{2,1,0:T(8,128)} %bitcast.52, f32[64,128,128]{2,1,0:T(8,128)} %bitcast.53, f32[64,128,128]{2,1,0:T(8,128)} %bitcast.54, ...), custom_call_target="tpu_custom_call" | custom-call | flops 62914560 | bytes 12582912 | tf_op jit(solution)/shard_map/pallas_call | solution.py:304
  95.6 0.3 slice.17
  95.9 0.1 copy.21
  96.0 2.1 %fusion.4 = f32[8,128,128]{2,1,0:T(8,128)S(1)} fusion(f32[64,8,8,128]{3,2,1,0:T(8,128)S(1)} %slice.17, s32[64,8]{0,1:T(8,128)S(1)} %bitcast.57), kind=kOutput, calls=%fused_computation.5 | convolution fusion | flops 805371904 | bytes 2623488 | tf_op jit(solution)/shard_map/scr,sckj->krj/dot_general | solution.py:776
  98.2 0.1 collective-permute-start
  98.3 1.9 %collective-permute-done = f32[8,128,128]{2,1,0:T(8,128)S(1)} collective-permute-done((f32[8,128,128]{2,1,0:T(8,128)S(1)}, f32[8,128,128]{2,1,0:T(8,128)S(1)}, u32[]{:S(2)}, u32[]{:S(2)}) %collective-permute-start) | collective-permute-done | bytes 524320 | tf_op jit(solution)/shard_map/ppermute | solution.py:779
  100.2 0.6 slice_bitcast_fusion.f_ref
  100.8 1.5 %shard_map.89 = f32[64,128,128]{2,1,0:T(8,128)} custom-call(f32[64,128,128]{2,1,0:T(8,128)} %get-tuple-element.12.x_ref, f32[128,128]{1,0:T(8,128)} %convert_select_fusion.wet_ref, f32[128,128]{1,0:T(8,128)} %slice_bitcast_fusion.f_ref), custom_call_target="tpu_custom_call", output_to_operand_aliasing={{}: (0, {})} | custom-call | tf_op jit(solution)/shard_map/pallas_call | solution.py:591
  102.4 4.7 %copy.36 = f32[1,64,128,128]{3,2,1,0:T(8,128)} copy(f32[1,64,128,128]{3,2,1,0:T(8,128)} %bitcast.55) | data formatting | bytes 8388608
  107.1 0.8 copy.37
  (18 shorter events, 0.2 us)
Async XLA Ops:
  0.6 13.6 %copy-start.6 = (f32[1,8,128,128]{3,2,1,0:T(8,128)S(1)}, f32[1,8,128,128]{3,2,1,0:T(8,128)}, u32[]{:S(2)}) copy-start(f32[1,8,128,128]{3,2,1,0:T(8,128)} %param.8) | copy-start | bytes 1572868
  3.6 10.7 %copy-start.1 = (f32[128,128]{1,0:T(8,128)S(1)}, f32[128,128]{1,0:T(8,128)}, u32[]{:S(2)}) copy-start(f32[128,128]{1,0:T(8,128)} %convert_select_fusion.wet_ref) | copy-start | bytes 196612
  15.5 15.9 %copy-start.2 = (f32[64,128]{1,0:T(8,128)S(1)}, f32[64,128]{1,0:T(8,128)}, u32[]{:S(2)}) copy-start(f32[64,128]{1,0:T(8,128)} %get-tuple-element.8.e0n) | copy-start | bytes 98308
  15.5 15.9 %copy-start.3 = (f32[64,128]{1,0:T(8,128)S(1)}, f32[64,128]{1,0:T(8,128)}, u32[]{:S(2)}) copy-start(f32[64,128]{1,0:T(8,128)} %get-tuple-element.9.e0s) | copy-start | bytes 98308
  15.5 15.9 %copy-start.4 = (f32[64,128]{1,0:T(8,128)S(1)}, f32[64,128]{1,0:T(8,128)}, u32[]{:S(2)}) copy-start(f32[64,128]{1,0:T(8,128)} %get-tuple-element.10.e0w) | copy-start | bytes 98308
  15.6 15.9 %copy-start.5 = (f32[64,128]{1,0:T(8,128)S(1)}, f32[64,128]{1,0:T(8,128)}, u32[]{:S(2)}) copy-start(f32[64,128]{1,0:T(8,128)} %get-tuple-element.11.e0e) | copy-start | bytes 98308
  31.4 1.7 %copy-start = (f32[64,9,8,128]{3,2,1,0:T(8,128)S(1)}, f32[64,9,8,128]{3,2,1,0:T(8,128)}, u32[]{:S(2)}) copy-start(f32[64,9,8,128]{3,2,1,0:T(8,128)} %shard_map.86.buckets_ref) | copy-start | bytes 7077892
  98.2 2.0 %collective-permute-start = (f32[8,128,128]{2,1,0:T(8,128)S(1)}, f32[8,128,128]{2,1,0:T(8,128)S(1)}, u32[]{:S(2)}, u32[]{:S(2)}) collective-permute-start(f32[8,128,128]{2,1,0:T(8,128)S(1)} %fusion.4), channel_id=1, source_target_pairs={{0,64},{64,0},{1,65},{65,1},{2,66},{66,2},{3,67},{67,3},{4,68},{68... | collective-permute-start | bytes 1572872 | tf_op jit(solution)/shard_map/ppermute | solution.py:779

commit v13 on v12

--- a/solution.py
+++ b/solution.py
@@ -717,15 +717,22 @@
     )(en, es, ew, ee)
 
 
-def bucket_kernel(slot_ref, row_ref, contrib_ref, out_ref):
+def bucket_kernel(target_ref, row_ref, contrib_ref, out_ref, count_ref):
     ntiles = contrib_ref.shape[0]
+    ndest = out_ref.shape[0]
     sub = lax.broadcasted_iota(jnp.int32, (KF, CY), 0)
     out_ref[...] = jnp.zeros_like(out_ref)
 
+    def clear(d, carry):
+        count_ref[d] = 0
+        return carry
+
+    lax.fori_loop(0, ndest, clear, 0)
+
     def body(t, carry):
-        s = slot_ref[t]
-        d = s // CAP
-        c = s % CAP
+        d = target_ref[t]
+        c = count_ref[d]
+        count_ref[d] = c + 1
         out_ref[d, c] = contrib_ref[t]
         out_ref[d, CAP] = jnp.where(sub == c, row_ref[t].astype(jnp.float32), out_ref[d, CAP])
         return carry
@@ -754,10 +761,6 @@
     contrib = jnp.einsum(
         "tji,kti->tkj", tile_weights[0, 0, 0], picked, preferred_element_type=jnp.float32
     )
-    onehot = (target[:, None] == jnp.arange(ndev, dtype=jnp.int32)[None, :]).astype(jnp.int32)
-    earlier = jnp.cumsum(onehot, axis=0) - onehot
-    rank = jnp.sum(earlier * onehot, axis=1)
-    slot = target * CAP + rank
     buckets = pl.pallas_call(
         bucket_kernel,
         in_specs=[
@@ -767,7 +770,8 @@
         ],
         out_specs=pl.BlockSpec(memory_space=pltpu.VMEM),
         out_shape=jax.ShapeDtypeStruct((ndev, CAP + 1, KF, CY), jnp.float32),
-    )(slot, dest_row, contrib)
+        scratch_shapes=[pltpu.SMEM((ndev,), jnp.int32)],
+    )(target, dest_row, contrib)
     second, arrived = interval(coef, wet, state, buckets, masked_edges(wet, state))
     got_rows = arrived[:, CAP, :, 0].astype(jnp.int32)
     select = (

time: 109 us -> 105 us (0.963)
  other arithmetic: 6.75 us -> 3.35 us
    add x1 -> x0, other arithmetic: 1.26 us -> none  [local(): slot = target * CAP + rank]
where the time goes in v13:
time: 105 us; the launch traced here: 104 us
  Pallas kernels  77.7 us (74%)
  matrix products  11 us (10%)
  local copies, waits for them, and re-layouts  9.03 us (9%)
  other arithmetic  3.35 us (3%)
  waiting for transfers between devices  1.9 us (2%)
    pallas_call x1, Pallas kernels, interval(): pl.pallas_call(interval_kernel, grid=(2, nblk), in_specs=in_specs, out_sp...  62.6 us
    dot_general x1, matrix products, local(): jnp.einsum('tji,kti->tkj', tile_weights[0, 0, 0], picked, preferred_eleme...  8.83 us
    unnamed x16, local copies, waits for them, and re-layouts  7.18 us
    pallas_call x1, Pallas kernels, masked_edges(): pl.pallas_call(edges_kernel, grid=(lev // LB,), in_specs=[full2((rows, co...  7.14 us
    pallas_call x1, Pallas kernels, local(): pl.pallas_call(bucket_kernel, in_specs=[pl.BlockSpec(memory_space=pltpu.S...  6.43 us
    dot_general x1, matrix products, local(): jnp.einsum('scr,sckj->krj', select, arrived[:, :CAP], precision=lax.Preci...  2.16 us
  transfers between devices with their start and end apart: 1, of which 1 were waited for; matrix products, arithmetic and copies ran while one was open for 0% of the time, Pallas kernels for 0%

profile of v13, /device:TPU:16, one launch (start us, length us, event | category | flops | bytes accessed | tf_op | source)
XLA Modules:
  0.0 103.8 jit_solution(15306852340950647875)
XLA Ops:
  0.6 0.0 copy-start.6
  0.7 0.7 compare_select_fusion
  1.4 0.7 compare_and_fusion
  2.1 1.5 %convert_select_fusion.wet_ref = f32[128,128]{1,0:T(8,128)} fusion(s32[128,128]{1,0:T(8,128)} %param.9, pred[]{:T(512)S(6)} %eq.8), kind=kLoop, calls=%fused_computation.17 | loop fusion | flops 32768 | bytes 131073 | tf_op jit(solution)/shard_map/jit(_where)/select_n | solution.py:748
  3.6 7.1 %shard_map.87 = (f32[64,128]{1,0:T(8,128)}, f32[64,128]{1,0:T(8,128)}, f32[64,128]{1,0:T(8,128)}, f32[64,128]{1,0:T(8,128)}) custom-call(f32[128,128]{1,0:T(8,128)} %convert_select_fusion.wet_ref, f32[64,128,128]{2,1,0:T(8,128)} %bitcast.31), custom_call_target="tpu_custom_call" | custom-call | flops 2097152 | bytes 4194304 | tf_op jit(solution)/shard_map/pallas_call | solution.py:570
  10.7 0.0 copy-done.6
  10.7 0.3 fusion.8
  11.1 0.1 pad_maximum_fusion.coef_ref
  11.2 0.8 gather_fusion
  12.0 8.8 %fusion.contrib_ref = f32[256,8,128]{2,1,0:T(8,128)} fusion(bf16[1,1,1,256,128,128]{5,4,3,2,1,0:T(8,128)(2,1)} %param.10, bf16[256,8,128]{2,1,0:T(8,128)(2,1)S(1)} %gather_fusion, pred[256]{0:T(512)(128)(4,1)S(1)} %compare_and_fusion), kind=kOutput, calls=%fused_computation.1 | convolution fusion | flops 67371008 | bytes 9961728 | tf_op jit(solution)/shard_map/tji,kti->tkj/dot_general | solution.py:761
  20.9 6.4 %shard_map.86.buckets_ref = f32[64,9,8,128]{3,2,1,0:T(8,128)} custom-call(s32[256]{0:T(256)} %bitcast.39, s32[256]{0:T(256)} %bitcast.40, f32[256,8,128]{2,1,0:T(8,128)} %fusion.contrib_ref), custom_call_target="tpu_custom_call" | custom-call | tf_op jit(solution)/shard_map/pallas_call | solution.py:764
  27.3 0.0 copy-done.3
  27.3 0.0 copy-start
  27.3 1.7 %copy-done = f32[64,9,8,128]{3,2,1,0:T(8,128)S(1)} copy-done((f32[64,9,8,128]{3,2,1,0:T(8,128)S(1)}, f32[64,9,8,128]{3,2,1,0:T(8,128)}, u32[]{:S(2)}) %copy-start) | copy-done | bytes 2359320
  29.0 62.6 %shard_map.88 = (f32[64,128,128]{2,1,0:T(8,128)}, f32[64,9,8,128]{3,2,1,0:T(8,128)S(1)}) custom-call(f32[2]{0:T(128)S(1)} %pad_maximum_fusion.coef_ref, f32[128,128]{1,0:T(8,128)S(1)} %copy-done.1, f32[64,128,128]{2,1,0:T(8,128)} %bitcast.32, f32[64,128,128]{2,1,0:T(8,128)} %bitcast.33, f32[64,128,128]{2,1,0:T(8,128)} %bitcast.34, ...), custom_call_target="tpu_custom_call" | custom-call | flops 62914560 | bytes 12582912 | tf_op jit(solution)/shard_map/pallas_call | solution.py:304
  91.6 0.3 slice.9
  91.8 0.1 copy.19
  92.0 2.2 %fusion.4 = f32[8,128,128]{2,1,0:T(8,128)S(1)} fusion(f32[64,8,8,128]{3,2,1,0:T(8,128)S(1)} %slice.9, s32[64,8]{0,1:T(8,128)S(1)} %bitcast.37), kind=kOutput, calls=%fused_computation.5 | convolution fusion | flops 805371904 | bytes 2623488 | tf_op jit(solution)/shard_map/scr,sckj->krj/dot_general | solution.py:780
  94.1 0.1 collective-permute-start
  94.2 1.9 %collective-permute-done = f32[8,128,128]{2,1,0:T(8,128)S(1)} collective-permute-done((f32[8,128,128]{2,1,0:T(8,128)S(1)}, f32[8,128,128]{2,1,0:T(8,128)S(1)}, u32[]{:S(2)}, u32[]{:S(2)}) %collective-permute-start) | collective-permute-done | bytes 524320 | tf_op jit(solution)/shard_map/ppermute | solution.py:783
  96.1 0.6 slice_bitcast_fusion.f_ref
  96.8 1.5 %shard_map.89 = f32[64,128,128]{2,1,0:T(8,128)} custom-call(f32[64,128,128]{2,1,0:T(8,128)} %get-tuple-element.12.x_ref, f32[128,128]{1,0:T(8,128)} %convert_select_fusion.wet_ref, f32[128,128]{1,0:T(8,128)} %slice_bitcast_fusion.f_ref), custom_call_target="tpu_custom_call", output_to_operand_aliasing={{}: (0, {})} | custom-call | tf_op jit(solution)/shard_map/pallas_call | solution.py:591
  98.3 4.7 %copy.32 = f32[1,64,128,128]{3,2,1,0:T(8,128)} copy(f32[1,64,128,128]{3,2,1,0:T(8,128)} %bitcast.35) | data formatting | bytes 8388608
  103.0 0.8 copy.33
  (11 shorter events, 0.0 us)
Async XLA Ops:
  0.6 10.1 %copy-start.6 = (f32[1,8,128,128]{3,2,1,0:T(8,128)S(1)}, f32[1,8,128,128]{3,2,1,0:T(8,128)}, u32[]{:S(2)}) copy-start(f32[1,8,128,128]{3,2,1,0:T(8,128)} %param.8) | copy-start | bytes 1572868
  3.6 7.2 %copy-start.1 = (f32[128,128]{1,0:T(8,128)S(1)}, f32[128,128]{1,0:T(8,128)}, u32[]{:S(2)}) copy-start(f32[128,128]{1,0:T(8,128)} %convert_select_fusion.wet_ref) | copy-start | bytes 196612
  12.0 15.3 %copy-start.2 = (f32[64,128]{1,0:T(8,128)S(1)}, f32[64,128]{1,0:T(8,128)}, u32[]{:S(2)}) copy-start(f32[64,128]{1,0:T(8,128)} %get-tuple-element.8.e0n) | copy-start | bytes 98308
  12.0 15.3 %copy-start.3 = (f32[64,128]{1,0:T(8,128)S(1)}, f32[64,128]{1,0:T(8,128)}, u32[]{:S(2)}) copy-start(f32[64,128]{1,0:T(8,128)} %get-tuple-element.9.e0s) | copy-start | bytes 98308
  12.0 15.3 %copy-start.4 = (f32[64,128]{1,0:T(8,128)S(1)}, f32[64,128]{1,0:T(8,128)}, u32[]{:S(2)}) copy-start(f32[64,128]{1,0:T(8,128)} %get-tuple-element.10.e0w) | copy-start | bytes 98308
  12.0 15.3 %copy-start.5 = (f32[64,128]{1,0:T(8,128)S(1)}, f32[64,128]{1,0:T(8,128)}, u32[]{:S(2)}) copy-start(f32[64,128]{1,0:T(8,128)} %get-tuple-element.11.e0e) | copy-start | bytes 98308
  27.3 1.7 %copy-start = (f32[64,9,8,128]{3,2,1,0:T(8,128)S(1)}, f32[64,9,8,128]{3,2,1,0:T(8,128)}, u32[]{:S(2)}) copy-start(f32[64,9,8,128]{3,2,1,0:T(8,128)} %shard_map.86.buckets_ref) | copy-start | bytes 7077892
  94.1 2.0 %collective-permute-start = (f32[8,128,128]{2,1,0:T(8,128)S(1)}, f32[8,128,128]{2,1,0:T(8,128)S(1)}, u32[]{:S(2)}, u32[]{:S(2)}) collective-permute-start(f32[8,128,128]{2,1,0:T(8,128)S(1)} %fusion.4), channel_id=1, source_target_pairs={{0,64},{64,0},{1,65},{65,1},{2,66},{66,2},{3,67},{67,3},{4,68},{68... | collective-permute-start | bytes 1572872 | tf_op jit(solution)/shard_map/ppermute | solution.py:783

commit v14 on v13

--- a/solution.py
+++ b/solution.py
@@ -737,7 +737,7 @@
         out_ref[d, CAP] = jnp.where(sub == c, row_ref[t].astype(jnp.float32), out_ref[d, CAP])
         return carry
 
-    lax.fori_loop(0, ntiles, body, 0)
+    lax.fori_loop(0, ntiles, body, 0, unroll=8)
 
 
 def local(states, surface, land_mask, tile_weights, tile_source, tile_target, tile_row):

time: 105 us -> 103 us (0.981)
  Pallas kernels: 77.7 us -> 75.9 us
    pallas_call x1, Pallas kernels: 6.43 us -> 4.66 us  [local(): pl.pallas_call(bucket_kernel, in_specs=[pl.BlockSpec(memory_space=pltpu.S...]
where the time goes in v14:
time: 103 us; the launch traced here: 102 us
  Pallas kernels  75.9 us (74%)
  matrix products  11 us (11%)
  local copies, waits for them, and re-layouts  9.03 us (9%)
  other arithmetic  3.35 us (3%)
  waiting for transfers between devices  1.89 us (2%)
    pallas_call x1, Pallas kernels, interval(): pl.pallas_call(interval_kernel, grid=(2, nblk), in_specs=in_specs, out_sp...  62.6 us
    dot_general x1, matrix products, local(): jnp.einsum('tji,kti->tkj', tile_weights[0, 0, 0], picked, preferred_eleme...  8.83 us
    unnamed x16, local copies, waits for them, and re-layouts  7.18 us
    pallas_call x1, Pallas kernels, masked_edges(): pl.pallas_call(edges_kernel, grid=(lev // LB,), in_specs=[full2((rows, co...  7.14 us
    pallas_call x1, Pallas kernels, local(): pl.pallas_call(bucket_kernel, in_specs=[pl.BlockSpec(memory_space=pltpu.S...  4.66 us
    dot_general x1, matrix products, local(): jnp.einsum('scr,sckj->krj', select, arrived[:, :CAP], precision=lax.Preci...  2.15 us
  transfers between devices with their start and end apart: 1, of which 1 were waited for; matrix products, arithmetic and copies ran while one was open for 0% of the time, Pallas kernels for 0%

profile of v14, /device:TPU:16, one launch (start us, length us, event | category | flops | bytes accessed | tf_op | source)
XLA Modules:
  0.0 102.0 jit_solution(4693234709787044234)
XLA Ops:
  0.7 0.7 compare_select_fusion
  1.4 0.7 compare_and_fusion
  2.1 1.5 %convert_select_fusion.wet_ref = f32[128,128]{1,0:T(8,128)} fusion(s32[128,128]{1,0:T(8,128)} %param.9, pred[]{:T(512)S(6)} %eq.8), kind=kLoop, calls=%fused_computation.17 | loop fusion | flops 32768 | bytes 131073 | tf_op jit(solution)/shard_map/jit(_where)/select_n | solution.py:748
  3.6 7.1 %shard_map.87 = (f32[64,128]{1,0:T(8,128)}, f32[64,128]{1,0:T(8,128)}, f32[64,128]{1,0:T(8,128)}, f32[64,128]{1,0:T(8,128)}) custom-call(f32[128,128]{1,0:T(8,128)} %convert_select_fusion.wet_ref, f32[64,128,128]{2,1,0:T(8,128)} %bitcast.31), custom_call_target="tpu_custom_call" | custom-call | flops 2097152 | bytes 4194304 | tf_op jit(solution)/shard_map/pallas_call | solution.py:570
  10.7 0.3 fusion.8
  11.1 0.1 pad_maximum_fusion.coef_ref
  11.2 0.8 gather_fusion
  12.0 0.0 copy-start.2
  12.0 0.0 copy-start.3
  12.0 0.0 copy-start.4
  12.0 8.8 %fusion.contrib_ref = f32[256,8,128]{2,1,0:T(8,128)} fusion(bf16[1,1,1,256,128,128]{5,4,3,2,1,0:T(8,128)(2,1)} %param.10, bf16[256,8,128]{2,1,0:T(8,128)(2,1)S(1)} %gather_fusion, pred[256]{0:T(512)(128)(4,1)S(1)} %compare_and_fusion), kind=kOutput, calls=%fused_computation.1 | convolution fusion | flops 67371008 | bytes 9961728 | tf_op jit(solution)/shard_map/tji,kti->tkj/dot_general | solution.py:761
  20.9 4.7 %shard_map.86.buckets_ref = f32[64,9,8,128]{3,2,1,0:T(8,128)} custom-call(s32[256]{0:T(256)} %bitcast.39, s32[256]{0:T(256)} %bitcast.40, f32[256,8,128]{2,1,0:T(8,128)} %fusion.contrib_ref), custom_call_target="tpu_custom_call" | custom-call | tf_op jit(solution)/shard_map/pallas_call | solution.py:764
  25.5 0.0 copy-start
  25.5 1.7 %copy-done = f32[64,9,8,128]{3,2,1,0:T(8,128)S(1)} copy-done((f32[64,9,8,128]{3,2,1,0:T(8,128)S(1)}, f32[64,9,8,128]{3,2,1,0:T(8,128)}, u32[]{:S(2)}) %copy-start) | copy-done | bytes 2359320
  27.2 62.6 %shard_map.88 = (f32[64,128,128]{2,1,0:T(8,128)}, f32[64,9,8,128]{3,2,1,0:T(8,128)S(1)}) custom-call(f32[2]{0:T(128)S(1)} %pad_maximum_fusion.coef_ref, f32[128,128]{1,0:T(8,128)S(1)} %copy-done.1, f32[64,128,128]{2,1,0:T(8,128)} %bitcast.32, f32[64,128,128]{2,1,0:T(8,128)} %bitcast.33, f32[64,128,128]{2,1,0:T(8,128)} %bitcast.34, ...), custom_call_target="tpu_custom_call" | custom-call | flops 62914560 | bytes 12582912 | tf_op jit(solution)/shard_map/pallas_call | solution.py:304
  89.8 0.3 slice.9
  90.1 0.1 copy.19
  90.2 2.1 %fusion.4 = f32[8,128,128]{2,1,0:T(8,128)S(1)} fusion(f32[64,8,8,128]{3,2,1,0:T(8,128)S(1)} %slice.9, s32[64,8]{0,1:T(8,128)S(1)} %bitcast.37), kind=kOutput, calls=%fused_computation.5 | convolution fusion | flops 805371904 | bytes 2623488 | tf_op jit(solution)/shard_map/scr,sckj->krj/dot_general | solution.py:780
  92.4 0.1 collective-permute-start
  92.5 1.9 %collective-permute-done = f32[8,128,128]{2,1,0:T(8,128)S(1)} collective-permute-done((f32[8,128,128]{2,1,0:T(8,128)S(1)}, f32[8,128,128]{2,1,0:T(8,128)S(1)}, u32[]{:S(2)}, u32[]{:S(2)}) %collective-permute-start) | collective-permute-done | bytes 524320 | tf_op jit(solution)/shard_map/ppermute | solution.py:783
  94.4 0.6 slice_bitcast_fusion.f_ref
  95.0 1.5 %shard_map.89 = f32[64,128,128]{2,1,0:T(8,128)} custom-call(f32[64,128,128]{2,1,0:T(8,128)} %get-tuple-element.12.x_ref, f32[128,128]{1,0:T(8,128)} %convert_select_fusion.wet_ref, f32[128,128]{1,0:T(8,128)} %slice_bitcast_fusion.f_ref), custom_call_target="tpu_custom_call", output_to_operand_aliasing={{}: (0, {})} | custom-call | tf_op jit(solution)/shard_map/pallas_call | solution.py:591
  96.5 4.7 %copy.32 = f32[1,64,128,128]{3,2,1,0:T(8,128)} copy(f32[1,64,128,128]{3,2,1,0:T(8,128)} %bitcast.35) | data formatting | bytes 8388608
  101.2 0.8 copy.33
  (11 shorter events, 0.0 us)
Async XLA Ops:
  0.6 10.1 %copy-start.6 = (f32[1,8,128,128]{3,2,1,0:T(8,128)S(1)}, f32[1,8,128,128]{3,2,1,0:T(8,128)}, u32[]{:S(2)}) copy-start(f32[1,8,128,128]{3,2,1,0:T(8,128)} %param.8) | copy-start | bytes 1572868
  3.6 7.2 %copy-start.1 = (f32[128,128]{1,0:T(8,128)S(1)}, f32[128,128]{1,0:T(8,128)}, u32[]{:S(2)}) copy-start(f32[128,128]{1,0:T(8,128)} %convert_select_fusion.wet_ref) | copy-start | bytes 196612
  12.0 13.5 %copy-start.2 = (f32[64,128]{1,0:T(8,128)S(1)}, f32[64,128]{1,0:T(8,128)}, u32[]{:S(2)}) copy-start(f32[64,128]{1,0:T(8,128)} %get-tuple-element.8.e0n) | copy-start | bytes 98308
  12.0 13.5 %copy-start.3 = (f32[64,128]{1,0:T(8,128)S(1)}, f32[64,128]{1,0:T(8,128)}, u32[]{:S(2)}) copy-start(f32[64,128]{1,0:T(8,128)} %get-tuple-element.9.e0s) | copy-start | bytes 98308
  12.0 13.5 %copy-start.4 = (f32[64,128]{1,0:T(8,128)S(1)}, f32[64,128]{1,0:T(8,128)}, u32[]{:S(2)}) copy-start(f32[64,128]{1,0:T(8,128)} %get-tuple-element.10.e0w) | copy-start | bytes 98308
  12.0 13.5 %copy-start.5 = (f32[64,128]{1,0:T(8,128)S(1)}, f32[64,128]{1,0:T(8,128)}, u32[]{:S(2)}) copy-start(f32[64,128]{1,0:T(8,128)} %get-tuple-element.11.e0e) | copy-start | bytes 98308
  25.5 1.7 %copy-start = (f32[64,9,8,128]{3,2,1,0:T(8,128)S(1)}, f32[64,9,8,128]{3,2,1,0:T(8,128)}, u32[]{:S(2)}) copy-start(f32[64,9,8,128]{3,2,1,0:T(8,128)} %shard_map.86.buckets_ref) | copy-start | bytes 7077892
  92.4 2.0 %collective-permute-start = (f32[8,128,128]{2,1,0:T(8,128)S(1)}, f32[8,128,128]{2,1,0:T(8,128)S(1)}, u32[]{:S(2)}, u32[]{:S(2)}) collective-permute-start(f32[8,128,128]{2,1,0:T(8,128)S(1)} %fusion.4), channel_id=1, source_target_pairs={{0,64},{64,0},{1,65},{65,1},{2,66},{66,2},{3,67},{67,3},{4,68},{68... | collective-permute-start | bytes 1572872 | tf_op jit(solution)/shard_map/ppermute | solution.py:783

commit v15 on v14

--- a/solution.py
+++ b/solution.py
@@ -11,6 +11,7 @@
 KF = 8
 CAP = 8
 LB = 8
+EB = 16
 
 force_gain = 0.5
 
@@ -546,11 +547,11 @@
     lane = lax.broadcasted_iota(jnp.int32, qw_ref.shape, 1)
     qw = qw_ref[...]
     qe = qe_ref[...]
-    for l in range(LB):
+    for l in range(EB):
         fw = wet * u_ref[l]
         en_ref[l:l + 1, :] = fw[0:1, :]
         es_ref[l:l + 1, :] = fw[rows - 1:rows, :]
-        hit = lane == i * LB + l
+        hit = lane == i * EB + l
         qw = jnp.where(hit, fw[:, 0:1], qw)
         qe = jnp.where(hit, fw[:, cols - 1:cols], qe)
     qw_ref[...] = qw
@@ -565,12 +566,12 @@
 
 def masked_edges(wet, u):
     lev, rows, cols = u.shape
-    lvl2 = pl.BlockSpec((LB, cols), lambda i: (i, 0))
+    lvl2 = pl.BlockSpec((EB, cols), lambda i: (i, 0))
     full2 = lambda shape: pl.BlockSpec(shape, lambda i: (0, 0))
     return pl.pallas_call(
         edges_kernel,
-        grid=(lev // LB,),
-        in_specs=[full2((rows, cols)), pl.BlockSpec((LB, rows, cols), lambda i: (i, 0, 0))],
+        grid=(lev // EB,),
+        in_specs=[full2((rows, cols)), pl.BlockSpec((EB, rows, cols), lambda i: (i, 0, 0))],
         out_specs=[lvl2, lvl2, full2((lev, rows)), full2((lev, rows))],
         out_shape=[jax.ShapeDtypeStruct((lev, cols), jnp.float32)] * 2
         + [jax.ShapeDtypeStruct((lev, rows), jnp.float32)] * 2,

time: 103 us -> 101 us (0.981)
  Pallas kernels: 75.9 us -> 74.1 us
    pallas_call x1, Pallas kernels: 7.14 us -> 5.34 us  [masked_edges(): pl.pallas_call(edges_kernel, grid=(lev // EB,), in_specs=[full2((rows, co...]
where the time goes in v15:
time: 101 us; the launch traced here: 100 us
  Pallas kernels  74.1 us (73%)
  matrix products  11 us (11%)
  local copies, waits for them, and re-layouts  9.04 us (9%)
  other arithmetic  3.35 us (3%)
  waiting for transfers between devices  1.89 us (2%)
    pallas_call x1, Pallas kernels, interval(): pl.pallas_call(interval_kernel, grid=(2, nblk), in_specs=in_specs, out_sp...  62.5 us
    dot_general x1, matrix products, local(): jnp.einsum('tji,kti->tkj', tile_weights[0, 0, 0], picked, preferred_eleme...  8.83 us
    unnamed x16, local copies, waits for them, and re-layouts  7.18 us
    pallas_call x1, Pallas kernels, masked_edges(): pl.pallas_call(edges_kernel, grid=(lev // EB,), in_specs=[full2((rows, co...  5.34 us
    pallas_call x1, Pallas kernels, local(): pl.pallas_call(bucket_kernel, in_specs=[pl.BlockSpec(memory_space=pltpu.S...  4.66 us
    dot_general x1, matrix products, local(): jnp.einsum('scr,sckj->krj', select, arrived[:, :CAP], precision=lax.Preci...  2.15 us
  transfers between devices with their start and end apart: 1, of which 1 were waited for; matrix products, arithmetic and copies ran while one was open for 0% of the time, Pallas kernels for 0%

profile of v15, /device:TPU:16, one launch (start us, length us, event | category | flops | bytes accessed | tf_op | source)
XLA Modules:
  0.0 100.2 jit_solution(49386109040551719)
XLA Ops:
  0.7 0.7 compare_select_fusion
  1.4 0.7 compare_and_fusion
  2.1 1.5 %convert_select_fusion.wet_ref = f32[128,128]{1,0:T(8,128)} fusion(s32[128,128]{1,0:T(8,128)} %param.9, pred[]{:T(512)S(6)} %eq.8), kind=kLoop, calls=%fused_computation.17 | loop fusion | flops 32768 | bytes 131073 | tf_op jit(solution)/shard_map/jit(_where)/select_n | solution.py:749
  3.6 5.3 %shard_map.87 = (f32[64,128]{1,0:T(8,128)}, f32[64,128]{1,0:T(8,128)}, f32[64,128]{1,0:T(8,128)}, f32[64,128]{1,0:T(8,128)}) custom-call(f32[128,128]{1,0:T(8,128)} %convert_select_fusion.wet_ref, f32[64,128,128]{2,1,0:T(8,128)} %bitcast.31), custom_call_target="tpu_custom_call" | custom-call | flops 2097152 | bytes 4194304 | tf_op jit(solution)/shard_map/pallas_call | solution.py:571
  8.9 0.0 copy-done.6
  8.9 0.0 copy-done.1
  8.9 0.3 fusion.8
  9.3 0.1 pad_maximum_fusion.coef_ref
  9.4 0.8 gather_fusion
  10.2 0.0 copy-start.2
  10.2 8.8 %fusion.contrib_ref = f32[256,8,128]{2,1,0:T(8,128)} fusion(bf16[1,1,1,256,128,128]{5,4,3,2,1,0:T(8,128)(2,1)} %param.10, bf16[256,8,128]{2,1,0:T(8,128)(2,1)S(1)} %gather_fusion, pred[256]{0:T(512)(128)(4,1)S(1)} %compare_and_fusion), kind=kOutput, calls=%fused_computation.1 | convolution fusion | flops 67371008 | bytes 9961728 | tf_op jit(solution)/shard_map/tji,kti->tkj/dot_general | solution.py:762
  19.1 4.7 %shard_map.86.buckets_ref = f32[64,9,8,128]{3,2,1,0:T(8,128)} custom-call(s32[256]{0:T(256)} %bitcast.39, s32[256]{0:T(256)} %bitcast.40, f32[256,8,128]{2,1,0:T(8,128)} %fusion.contrib_ref), custom_call_target="tpu_custom_call" | custom-call | tf_op jit(solution)/shard_map/pallas_call | solution.py:765
  23.7 0.0 copy-start
  23.7 1.7 %copy-done = f32[64,9,8,128]{3,2,1,0:T(8,128)S(1)} copy-done((f32[64,9,8,128]{3,2,1,0:T(8,128)S(1)}, f32[64,9,8,128]{3,2,1,0:T(8,128)}, u32[]{:S(2)}) %copy-start) | copy-done | bytes 2359320
  25.4 62.5 %shard_map.88 = (f32[64,128,128]{2,1,0:T(8,128)}, f32[64,9,8,128]{3,2,1,0:T(8,128)S(1)}) custom-call(f32[2]{0:T(128)S(1)} %pad_maximum_fusion.coef_ref, f32[128,128]{1,0:T(8,128)S(1)} %copy-done.1, f32[64,128,128]{2,1,0:T(8,128)} %bitcast.32, f32[64,128,128]{2,1,0:T(8,128)} %bitcast.33, f32[64,128,128]{2,1,0:T(8,128)} %bitcast.34, ...), custom_call_target="tpu_custom_call" | custom-call | flops 62914560 | bytes 12582912 | tf_op jit(solution)/shard_map/pallas_call | solution.py:305
  88.0 0.3 slice.9
  88.2 0.1 copy.19
  88.4 2.2 %fusion.4 = f32[8,128,128]{2,1,0:T(8,128)S(1)} fusion(f32[64,8,8,128]{3,2,1,0:T(8,128)S(1)} %slice.9, s32[64,8]{0,1:T(8,128)S(1)} %bitcast.37), kind=kOutput, calls=%fused_computation.5 | convolution fusion | flops 805371904 | bytes 2623488 | tf_op jit(solution)/shard_map/scr,sckj->krj/dot_general | solution.py:781
  90.6 0.1 collective-permute-start
  90.7 1.9 %collective-permute-done = f32[8,128,128]{2,1,0:T(8,128)S(1)} collective-permute-done((f32[8,128,128]{2,1,0:T(8,128)S(1)}, f32[8,128,128]{2,1,0:T(8,128)S(1)}, u32[]{:S(2)}, u32[]{:S(2)}) %collective-permute-start) | collective-permute-done | bytes 524320 | tf_op jit(solution)/shard_map/ppermute | solution.py:784
  92.5 0.6 slice_bitcast_fusion.f_ref
  93.2 1.5 %shard_map.89 = f32[64,128,128]{2,1,0:T(8,128)} custom-call(f32[64,128,128]{2,1,0:T(8,128)} %get-tuple-element.12.x_ref, f32[128,128]{1,0:T(8,128)} %convert_select_fusion.wet_ref, f32[128,128]{1,0:T(8,128)} %slice_bitcast_fusion.f_ref), custom_call_target="tpu_custom_call", output_to_operand_aliasing={{}: (0, {})} | custom-call | tf_op jit(solution)/shard_map/pallas_call | solution.py:592
  94.7 4.7 %copy.32 = f32[1,64,128,128]{3,2,1,0:T(8,128)} copy(f32[1,64,128,128]{3,2,1,0:T(8,128)} %bitcast.35) | data formatting | bytes 8388608
  99.4 0.8 copy.33
  (11 shorter events, 0.0 us)
Async XLA Ops:
  0.6 8.3 %copy-start.6 = (f32[1,8,128,128]{3,2,1,0:T(8,128)S(1)}, f32[1,8,128,128]{3,2,1,0:T(8,128)}, u32[]{:S(2)}) copy-start(f32[1,8,128,128]{3,2,1,0:T(8,128)} %param.8) | copy-start | bytes 1572868
  3.6 5.4 %copy-start.1 = (f32[128,128]{1,0:T(8,128)S(1)}, f32[128,128]{1,0:T(8,128)}, u32[]{:S(2)}) copy-start(f32[128,128]{1,0:T(8,128)} %convert_select_fusion.wet_ref) | copy-start | bytes 196612
  10.2 13.5 %copy-start.2 = (f32[64,128]{1,0:T(8,128)S(1)}, f32[64,128]{1,0:T(8,128)}, u32[]{:S(2)}) copy-start(f32[64,128]{1,0:T(8,128)} %get-tuple-element.8.e0n) | copy-start | bytes 98308
  10.2 13.5 %copy-start.3 = (f32[64,128]{1,0:T(8,128)S(1)}, f32[64,128]{1,0:T(8,128)}, u32[]{:S(2)}) copy-start(f32[64,128]{1,0:T(8,128)} %get-tuple-element.9.e0s) | copy-start | bytes 98308
  10.2 13.5 %copy-start.4 = (f32[64,128]{1,0:T(8,128)S(1)}, f32[64,128]{1,0:T(8,128)}, u32[]{:S(2)}) copy-start(f32[64,128]{1,0:T(8,128)} %get-tuple-element.10.e0w) | copy-start | bytes 98308
  10.2 13.5 %copy-start.5 = (f32[64,128]{1,0:T(8,128)S(1)}, f32[64,128]{1,0:T(8,128)}, u32[]{:S(2)}) copy-start(f32[64,128]{1,0:T(8,128)} %get-tuple-element.11.e0e) | copy-start | bytes 98308
  23.7 1.7 %copy-start = (f32[64,9,8,128]{3,2,1,0:T(8,128)S(1)}, f32[64,9,8,128]{3,2,1,0:T(8,128)}, u32[]{:S(2)}) copy-start(f32[64,9,8,128]{3,2,1,0:T(8,128)} %shard_map.86.buckets_ref) | copy-start | bytes 7077892
  90.6 2.0 %collective-permute-start = (f32[8,128,128]{2,1,0:T(8,128)S(1)}, f32[8,128,128]{2,1,0:T(8,128)S(1)}, u32[]{:S(2)}, u32[]{:S(2)}) collective-permute-start(f32[8,128,128]{2,1,0:T(8,128)S(1)} %fusion.4), channel_id=1, source_target_pairs={{0,64},{64,0},{1,65},{65,1},{2,66},{66,2},{3,67},{67,3},{4,68},{68... | collective-permute-start | bytes 1572872 | tf_op jit(solution)/shard_map/ppermute | solution.py:784

commit v16 on v15

--- a/solution.py
+++ b/solution.py
@@ -11,7 +11,7 @@
 KF = 8
 CAP = 8
 LB = 8
-EB = 16
+EB = 32
 
 force_gain = 0.5
 

time: 101 us -> 100 us (0.990)
  no operation moved by 1% of the time
where the time goes in v16:
time: 100 us; the launch traced here: 99.8 us
  Pallas kernels  73.6 us (74%)
  matrix products  11 us (11%)
  local copies, waits for them, and re-layouts  9.03 us (9%)
  other arithmetic  3.35 us (3%)
  waiting for transfers between devices  1.9 us (2%)
    pallas_call x1, Pallas kernels, interval(): pl.pallas_call(interval_kernel, grid=(2, nblk), in_specs=in_specs, out_sp...  62.5 us
    dot_general x1, matrix products, local(): jnp.einsum('tji,kti->tkj', tile_weights[0, 0, 0], picked, preferred_eleme...  8.83 us
    unnamed x16, local copies, waits for them, and re-layouts  7.18 us
    pallas_call x1, Pallas kernels, masked_edges(): pl.pallas_call(edges_kernel, grid=(lev // EB,), in_specs=[full2((rows, co...  4.97 us
    pallas_call x1, Pallas kernels, local(): pl.pallas_call(bucket_kernel, in_specs=[pl.BlockSpec(memory_space=pltpu.S...  4.66 us
    dot_general x1, matrix products, local(): jnp.einsum('scr,sckj->krj', select, arrived[:, :CAP], precision=lax.Preci...  2.16 us
  transfers between devices with their start and end apart: 1, of which 1 were waited for; matrix products, arithmetic and copies ran while one was open for 0% of the time, Pallas kernels for 0%

profile of v16, /device:TPU:16, one launch (start us, length us, event | category | flops | bytes accessed | tf_op | source)
XLA Modules:
  0.0 99.8 jit_solution(5558758658197421928)
XLA Ops:
  0.7 0.7 compare_select_fusion
  1.4 0.7 compare_and_fusion
  2.1 1.5 %convert_select_fusion.wet_ref = f32[128,128]{1,0:T(8,128)} fusion(s32[128,128]{1,0:T(8,128)} %param.9, pred[]{:T(512)S(6)} %eq.8), kind=kLoop, calls=%fused_computation.17 | loop fusion | flops 32768 | bytes 131073 | tf_op jit(solution)/shard_map/jit(_where)/select_n | solution.py:749
  3.6 5.0 %shard_map.87 = (f32[64,128]{1,0:T(8,128)}, f32[64,128]{1,0:T(8,128)}, f32[64,128]{1,0:T(8,128)}, f32[64,128]{1,0:T(8,128)}) custom-call(f32[128,128]{1,0:T(8,128)} %convert_select_fusion.wet_ref, f32[64,128,128]{2,1,0:T(8,128)} %bitcast.31), custom_call_target="tpu_custom_call" | custom-call | flops 2097152 | bytes 4194304 | tf_op jit(solution)/shard_map/pallas_call | solution.py:571
  8.6 0.3 fusion.8
  8.9 0.1 pad_maximum_fusion.coef_ref
  9.0 0.8 gather_fusion
  9.8 0.0 copy-start.2
  9.8 0.0 copy-start.3
  9.8 0.0 copy-start.4
  9.8 8.8 %fusion.contrib_ref = f32[256,8,128]{2,1,0:T(8,128)} fusion(bf16[1,1,1,256,128,128]{5,4,3,2,1,0:T(8,128)(2,1)} %param.10, bf16[256,8,128]{2,1,0:T(8,128)(2,1)S(1)} %gather_fusion, pred[256]{0:T(512)(128)(4,1)S(1)} %compare_and_fusion), kind=kOutput, calls=%fused_computation.1 | convolution fusion | flops 67371008 | bytes 9961728 | tf_op jit(solution)/shard_map/tji,kti->tkj/dot_general | solution.py:762
  18.7 4.7 %shard_map.86.buckets_ref = f32[64,9,8,128]{3,2,1,0:T(8,128)} custom-call(s32[256]{0:T(256)} %bitcast.39, s32[256]{0:T(256)} %bitcast.40, f32[256,8,128]{2,1,0:T(8,128)} %fusion.contrib_ref), custom_call_target="tpu_custom_call" | custom-call | tf_op jit(solution)/shard_map/pallas_call | solution.py:765
  23.4 0.0 copy-start
  23.4 1.7 %copy-done = f32[64,9,8,128]{3,2,1,0:T(8,128)S(1)} copy-done((f32[64,9,8,128]{3,2,1,0:T(8,128)S(1)}, f32[64,9,8,128]{3,2,1,0:T(8,128)}, u32[]{:S(2)}) %copy-start) | copy-done | bytes 2359320
  25.0 62.5 %shard_map.88 = (f32[64,128,128]{2,1,0:T(8,128)}, f32[64,9,8,128]{3,2,1,0:T(8,128)S(1)}) custom-call(f32[2]{0:T(128)S(1)} %pad_maximum_fusion.coef_ref, f32[128,128]{1,0:T(8,128)S(1)} %copy-done.1, f32[64,128,128]{2,1,0:T(8,128)} %bitcast.32, f32[64,128,128]{2,1,0:T(8,128)} %bitcast.33, f32[64,128,128]{2,1,0:T(8,128)} %bitcast.34, ...), custom_call_target="tpu_custom_call" | custom-call | flops 62914560 | bytes 12582912 | tf_op jit(solution)/shard_map/pallas_call | solution.py:305
  87.5 0.3 slice.9
  87.8 0.1 copy.19
  88.0 2.2 %fusion.4 = f32[8,128,128]{2,1,0:T(8,128)S(1)} fusion(f32[64,8,8,128]{3,2,1,0:T(8,128)S(1)} %slice.9, s32[64,8]{0,1:T(8,128)S(1)} %bitcast.37), kind=kOutput, calls=%fused_computation.5 | convolution fusion | flops 805371904 | bytes 2623488 | tf_op jit(solution)/shard_map/scr,sckj->krj/dot_general | solution.py:781
  90.1 0.1 collective-permute-start
  90.2 1.9 %collective-permute-done = f32[8,128,128]{2,1,0:T(8,128)S(1)} collective-permute-done((f32[8,128,128]{2,1,0:T(8,128)S(1)}, f32[8,128,128]{2,1,0:T(8,128)S(1)}, u32[]{:S(2)}, u32[]{:S(2)}) %collective-permute-start) | collective-permute-done | bytes 524320 | tf_op jit(solution)/shard_map/ppermute | solution.py:784
  92.1 0.6 slice_bitcast_fusion.f_ref
  92.8 1.5 %shard_map.89 = f32[64,128,128]{2,1,0:T(8,128)} custom-call(f32[64,128,128]{2,1,0:T(8,128)} %get-tuple-element.12.x_ref, f32[128,128]{1,0:T(8,128)} %convert_select_fusion.wet_ref, f32[128,128]{1,0:T(8,128)} %slice_bitcast_fusion.f_ref), custom_call_target="tpu_custom_call", output_to_operand_aliasing={{}: (0, {})} | custom-call | tf_op jit(solution)/shard_map/pallas_call | solution.py:592
  94.3 4.7 %copy.32 = f32[1,64,128,128]{3,2,1,0:T(8,128)} copy(f32[1,64,128,128]{3,2,1,0:T(8,128)} %bitcast.35) | data formatting | bytes 8388608
  99.0 0.8 copy.33
  (11 shorter events, 0.0 us)
Async XLA Ops:
  0.6 7.9 %copy-start.6 = (f32[1,8,128,128]{3,2,1,0:T(8,128)S(1)}, f32[1,8,128,128]{3,2,1,0:T(8,128)}, u32[]{:S(2)}) copy-start(f32[1,8,128,128]{3,2,1,0:T(8,128)} %param.8) | copy-start | bytes 1572868
  3.6 5.0 %copy-start.1 = (f32[128,128]{1,0:T(8,128)S(1)}, f32[128,128]{1,0:T(8,128)}, u32[]{:S(2)}) copy-start(f32[128,128]{1,0:T(8,128)} %convert_select_fusion.wet_ref) | copy-start | bytes 196612
  9.8 13.5 %copy-start.2 = (f32[64,128]{1,0:T(8,128)S(1)}, f32[64,128]{1,0:T(8,128)}, u32[]{:S(2)}) copy-start(f32[64,128]{1,0:T(8,128)} %get-tuple-element.8.e0n) | copy-start | bytes 98308
  9.8 13.5 %copy-start.3 = (f32[64,128]{1,0:T(8,128)S(1)}, f32[64,128]{1,0:T(8,128)}, u32[]{:S(2)}) copy-start(f32[64,128]{1,0:T(8,128)} %get-tuple-element.9.e0s) | copy-start | bytes 98308
  9.8 13.5 %copy-start.4 = (f32[64,128]{1,0:T(8,128)S(1)}, f32[64,128]{1,0:T(8,128)}, u32[]{:S(2)}) copy-start(f32[64,128]{1,0:T(8,128)} %get-tuple-element.10.e0w) | copy-start | bytes 98308
  9.8 13.5 %copy-start.5 = (f32[64,128]{1,0:T(8,128)S(1)}, f32[64,128]{1,0:T(8,128)}, u32[]{:S(2)}) copy-start(f32[64,128]{1,0:T(8,128)} %get-tuple-element.11.e0e) | copy-start | bytes 98308
  23.4 1.7 %copy-start = (f32[64,9,8,128]{3,2,1,0:T(8,128)S(1)}, f32[64,9,8,128]{3,2,1,0:T(8,128)}, u32[]{:S(2)}) copy-start(f32[64,9,8,128]{3,2,1,0:T(8,128)} %shard_map.86.buckets_ref) | copy-start | bytes 7077892
  90.1 2.0 %collective-permute-start = (f32[8,128,128]{2,1,0:T(8,128)S(1)}, f32[8,128,128]{2,1,0:T(8,128)S(1)}, u32[]{:S(2)}, u32[]{:S(2)}) collective-permute-start(f32[8,128,128]{2,1,0:T(8,128)S(1)} %fusion.4), channel_id=1, source_target_pairs={{0,64},{64,0},{1,65},{65,1},{2,66},{66,2},{3,67},{67,3},{4,68},{68... | collective-permute-start | bytes 1572872 | tf_op jit(solution)/shard_map/ppermute | solution.py:784

commit v17 on v16

--- a/solution.py
+++ b/solution.py
@@ -196,7 +196,7 @@
 
     @pl.when(p == 0)
     def _():
-        issue(1 + 3 * i, 3)
+        issue(1 + 4 * i, 4)
         blk = pl.ds(pl.multiple_of(i * LB, LB), LB)
         hn = halo0[0, blk]
         hs = halo0[1, blk]
@@ -233,7 +233,7 @@
             bucket_copy((me + k) % ndev).start()
             return carry
 
-        lax.fori_loop(min(1 + 3 * nblk, ndev), ndev, late, 0)
+        lax.fori_loop(min(1 + 4 * nblk, ndev), ndev, late, 0)
 
     @pl.when(p == 1)
     def _():

time: 100 us -> 103 us (1.030)
  the two profiles are of different devices: /device:TPU:16 before, /device:TPU:31 now
where the time goes in v17:
time: 103 us; the launch traced here: 102 us
  Pallas kernels  74.5 us (72%)
  matrix products  11 us (11%)
  local copies, waits for them, and re-layouts  9.03 us (9%)
  other arithmetic  3.35 us (3%)
  starting transfers between devices  2.1 us (2%)
  waiting for transfers between devices  1.54 us (1%)
    pallas_call x1, Pallas kernels, interval(): pl.pallas_call(interval_kernel, grid=(2, nblk), in_specs=in_specs, out_sp...  63.4 us
    dot_general x1, matrix products, local(): jnp.einsum('tji,kti->tkj', tile_weights[0, 0, 0], picked, preferred_eleme...  8.83 us
    unnamed x16, local copies, waits for them, and re-layouts  7.18 us
    pallas_call x1, Pallas kernels, masked_edges(): pl.pallas_call(edges_kernel, grid=(lev // EB,), in_specs=[full2((rows, co...  4.97 us
    pallas_call x1, Pallas kernels, local(): pl.pallas_call(bucket_kernel, in_specs=[pl.BlockSpec(memory_space=pltpu.S...  4.66 us
    dot_general x1, matrix products, local(): jnp.einsum('scr,sckj->krj', select, arrived[:, :CAP], precision=lax.Preci...  2.16 us
    ppermute x1, starting transfers between devices, local(): received = lax.ppermute(sent, 'mp', [(0, 1), (1, 0)])  2.1 us
  transfers between devices with their start and end apart: 1, of which 1 were waited for; matrix products, arithmetic and copies ran while one was open for 0% of the time, Pallas kernels for 0%

profile of v17, /device:TPU:31, one launch (start us, length us, event | category | flops | bytes accessed | tf_op | source)
XLA Modules:
  0.0 102.3 jit_solution(141659218907543560)
XLA Ops:
  0.6 0.0 copy-start.6
  0.7 0.7 compare_select_fusion
  1.4 0.7 compare_and_fusion
  2.1 1.5 %convert_select_fusion.wet_ref = f32[128,128]{1,0:T(8,128)} fusion(s32[128,128]{1,0:T(8,128)} %param.9, pred[]{:T(512)S(6)} %eq.8), kind=kLoop, calls=%fused_computation.17 | loop fusion | flops 32768 | bytes 131073 | tf_op jit(solution)/shard_map/jit(_where)/select_n | solution.py:749
  3.6 5.0 %shard_map.87 = (f32[64,128]{1,0:T(8,128)}, f32[64,128]{1,0:T(8,128)}, f32[64,128]{1,0:T(8,128)}, f32[64,128]{1,0:T(8,128)}) custom-call(f32[128,128]{1,0:T(8,128)} %convert_select_fusion.wet_ref, f32[64,128,128]{2,1,0:T(8,128)} %bitcast.31), custom_call_target="tpu_custom_call" | custom-call | flops 2097152 | bytes 4194304 | tf_op jit(solution)/shard_map/pallas_call | solution.py:571
  8.5 0.0 copy-done.6
  8.6 0.3 fusion.8
  8.9 0.1 pad_maximum_fusion.coef_ref
  9.0 0.8 gather_fusion
  9.8 8.8 %fusion.contrib_ref = f32[256,8,128]{2,1,0:T(8,128)} fusion(bf16[1,1,1,256,128,128]{5,4,3,2,1,0:T(8,128)(2,1)} %param.10, bf16[256,8,128]{2,1,0:T(8,128)(2,1)S(1)} %gather_fusion, pred[256]{0:T(512)(128)(4,1)S(1)} %compare_and_fusion), kind=kOutput, calls=%fused_computation.1 | convolution fusion | flops 67371008 | bytes 9961728 | tf_op jit(solution)/shard_map/tji,kti->tkj/dot_general | solution.py:762
  18.7 4.7 %shard_map.86.buckets_ref = f32[64,9,8,128]{3,2,1,0:T(8,128)} custom-call(s32[256]{0:T(256)} %bitcast.39, s32[256]{0:T(256)} %bitcast.40, f32[256,8,128]{2,1,0:T(8,128)} %fusion.contrib_ref), custom_call_target="tpu_custom_call" | custom-call | tf_op jit(solution)/shard_map/pallas_call | solution.py:765
  23.3 0.0 copy-done.5
  23.4 0.0 copy-start
  23.4 1.7 %copy-done = f32[64,9,8,128]{3,2,1,0:T(8,128)S(1)} copy-done((f32[64,9,8,128]{3,2,1,0:T(8,128)S(1)}, f32[64,9,8,128]{3,2,1,0:T(8,128)}, u32[]{:S(2)}) %copy-start) | copy-done | bytes 2359320
  25.0 63.4 %shard_map.88 = (f32[64,128,128]{2,1,0:T(8,128)}, f32[64,9,8,128]{3,2,1,0:T(8,128)S(1)}) custom-call(f32[2]{0:T(128)S(1)} %pad_maximum_fusion.coef_ref, f32[128,128]{1,0:T(8,128)S(1)} %copy-done.1, f32[64,128,128]{2,1,0:T(8,128)} %bitcast.32, f32[64,128,128]{2,1,0:T(8,128)} %bitcast.33, f32[64,128,128]{2,1,0:T(8,128)} %bitcast.34, ...), custom_call_target="tpu_custom_call" | custom-call | flops 62914560 | bytes 12582912 | tf_op jit(solution)/shard_map/pallas_call | solution.py:305
  88.5 0.3 slice.9
  88.7 0.1 copy.19
  88.9 2.2 %fusion.4 = f32[8,128,128]{2,1,0:T(8,128)S(1)} fusion(f32[64,8,8,128]{3,2,1,0:T(8,128)S(1)} %slice.9, s32[64,8]{0,1:T(8,128)S(1)} %bitcast.37), kind=kOutput, calls=%fused_computation.5 | convolution fusion | flops 805371904 | bytes 2623488 | tf_op jit(solution)/shard_map/scr,sckj->krj/dot_general | solution.py:781
  91.0 2.1 %collective-permute-start = (f32[8,128,128]{2,1,0:T(8,128)S(1)}, f32[8,128,128]{2,1,0:T(8,128)S(1)}, u32[]{:S(2)}, u32[]{:S(2)}) collective-permute-start(f32[8,128,128]{2,1,0:T(8,128)S(1)} %fusion.4), channel_id=1, source_target_pairs={{0,64},{64,0},{1,65},{65,1},{2,66},{66,2},{3,67},{67,3},{4,68},{68... | collective-permute-start | bytes 1572872 | tf_op jit(solution)/shard_map/ppermute | solution.py:784
  93.1 1.5 %collective-permute-done = f32[8,128,128]{2,1,0:T(8,128)S(1)} collective-permute-done((f32[8,128,128]{2,1,0:T(8,128)S(1)}, f32[8,128,128]{2,1,0:T(8,128)S(1)}, u32[]{:S(2)}, u32[]{:S(2)}) %collective-permute-start) | collective-permute-done | bytes 524320 | tf_op jit(solution)/shard_map/ppermute | solution.py:784
  94.7 0.6 slice_bitcast_fusion.f_ref
  95.3 1.5 %shard_map.89 = f32[64,128,128]{2,1,0:T(8,128)} custom-call(f32[64,128,128]{2,1,0:T(8,128)} %get-tuple-element.12.x_ref, f32[128,128]{1,0:T(8,128)} %convert_select_fusion.wet_ref, f32[128,128]{1,0:T(8,128)} %slice_bitcast_fusion.f_ref), custom_call_target="tpu_custom_call", output_to_operand_aliasing={{}: (0, {})} | custom-call | tf_op jit(solution)/shard_map/pallas_call | solution.py:592
  96.8 4.7 %copy.32 = f32[1,64,128,128]{3,2,1,0:T(8,128)} copy(f32[1,64,128,128]{3,2,1,0:T(8,128)} %bitcast.35) | data formatting | bytes 8388608
  101.5 0.8 copy.33
  (11 shorter events, 0.0 us)
Async XLA Ops:
  0.6 7.9 %copy-start.6 = (f32[1,8,128,128]{3,2,1,0:T(8,128)S(1)}, f32[1,8,128,128]{3,2,1,0:T(8,128)}, u32[]{:S(2)}) copy-start(f32[1,8,128,128]{3,2,1,0:T(8,128)} %param.8) | copy-start | bytes 1572868
  3.6 5.0 %copy-start.1 = (f32[128,128]{1,0:T(8,128)S(1)}, f32[128,128]{1,0:T(8,128)}, u32[]{:S(2)}) copy-start(f32[128,128]{1,0:T(8,128)} %convert_select_fusion.wet_ref) | copy-start | bytes 196612
  9.8 13.5 %copy-start.2 = (f32[64,128]{1,0:T(8,128)S(1)}, f32[64,128]{1,0:T(8,128)}, u32[]{:S(2)}) copy-start(f32[64,128]{1,0:T(8,128)} %get-tuple-element.8.e0n) | copy-start | bytes 98308
  9.8 13.5 %copy-start.3 = (f32[64,128]{1,0:T(8,128)S(1)}, f32[64,128]{1,0:T(8,128)}, u32[]{:S(2)}) copy-start(f32[64,128]{1,0:T(8,128)} %get-tuple-element.9.e0s) | copy-start | bytes 98308
  9.8 13.5 %copy-start.4 = (f32[64,128]{1,0:T(8,128)S(1)}, f32[64,128]{1,0:T(8,128)}, u32[]{:S(2)}) copy-start(f32[64,128]{1,0:T(8,128)} %get-tuple-element.10.e0w) | copy-start | bytes 98308
  9.8 13.5 %copy-start.5 = (f32[64,128]{1,0:T(8,128)S(1)}, f32[64,128]{1,0:T(8,128)}, u32[]{:S(2)}) copy-start(f32[64,128]{1,0:T(8,128)} %get-tuple-element.11.e0e) | copy-start | bytes 98308
  23.4 1.7 %copy-start = (f32[64,9,8,128]{3,2,1,0:T(8,128)S(1)}, f32[64,9,8,128]{3,2,1,0:T(8,128)}, u32[]{:S(2)}) copy-start(f32[64,9,8,128]{3,2,1,0:T(8,128)} %shard_map.86.buckets_ref) | copy-start | bytes 7077892
  91.0 3.6 %collective-permute-start = (f32[8,128,128]{2,1,0:T(8,128)S(1)}, f32[8,128,128]{2,1,0:T(8,128)S(1)}, u32[]{:S(2)}, u32[]{:S(2)}) collective-permute-start(f32[8,128,128]{2,1,0:T(8,128)S(1)} %fusion.4), channel_id=1, source_target_pairs={{0,64},{64,0},{1,65},{65,1},{2,66},{66,2},{3,67},{67,3},{4,68},{68... | collective-permute-start | bytes 1572872 | tf_op jit(solution)/shard_map/ppermute | solution.py:784

commit v18 on v17

--- a/solution.py
+++ b/solution.py
@@ -10,7 +10,7 @@
 CY = 128
 KF = 8
 CAP = 8
-LB = 8
+LB = 16
 EB = 32
 
 force_gain = 0.5
@@ -196,7 +196,7 @@
 
     @pl.when(p == 0)
     def _():
-        issue(1 + 4 * i, 4)
+        issue(1 + (3 * LB // 8) * i, 3 * LB // 8)
         blk = pl.ds(pl.multiple_of(i * LB, LB), LB)
         hn = halo0[0, blk]
         hs = halo0[1, blk]
@@ -233,7 +233,7 @@
             bucket_copy((me + k) % ndev).start()
             return carry
 
-        lax.fori_loop(min(1 + 4 * nblk, ndev), ndev, late, 0)
+        lax.fori_loop(min(1 + (3 * LB // 8) * nblk, ndev), ndev, late, 0)
 
     @pl.when(p == 1)
     def _():

time: 103 us -> 99.9 us (0.970)
  the two profiles are of different devices: /device:TPU:31 before, /device:TPU:16 now
where the time goes in v18:
time: 99.9 us; the launch traced here: 99.3 us
  Pallas kernels  73.1 us (73%)
  matrix products  11 us (11%)
  local copies, waits for them, and re-layouts  9.04 us (9%)
  other arithmetic  3.35 us (3%)
  waiting for transfers between devices  1.89 us (2%)
    pallas_call x1, Pallas kernels, interval(): pl.pallas_call(interval_kernel, grid=(2, nblk), in_specs=in_specs, out_sp...  62 us
    dot_general x1, matrix products, local(): jnp.einsum('tji,kti->tkj', tile_weights[0, 0, 0], picked, preferred_eleme...  8.83 us
    unnamed x16, local copies, waits for them, and re-layouts  7.18 us
    pallas_call x1, Pallas kernels, masked_edges(): pl.pallas_call(edges_kernel, grid=(lev // EB,), in_specs=[full2((rows, co...  4.97 us
    pallas_call x1, Pallas kernels, local(): pl.pallas_call(bucket_kernel, in_specs=[pl.BlockSpec(memory_space=pltpu.S...  4.66 us
    dot_general x1, matrix products, local(): jnp.einsum('scr,sckj->krj', select, arrived[:, :CAP], precision=lax.Preci...  2.15 us
  transfers between devices with their start and end apart: 1, of which 1 were waited for; matrix products, arithmetic and copies ran while one was open for 0% of the time, Pallas kernels for 0%

profile of v18, /device:TPU:16, one launch (start us, length us, event | category | flops | bytes accessed | tf_op | source)
XLA Modules:
  0.0 99.3 jit_solution(12875023830729888033)
XLA Ops:
  0.6 0.0 copy-start.6
  0.7 0.7 compare_select_fusion
  1.4 0.7 compare_and_fusion
  2.1 1.5 %convert_select_fusion.wet_ref = f32[128,128]{1,0:T(8,128)} fusion(s32[128,128]{1,0:T(8,128)} %param.9, pred[]{:T(512)S(6)} %eq.8), kind=kLoop, calls=%fused_computation.17 | loop fusion | flops 32768 | bytes 131073 | tf_op jit(solution)/shard_map/jit(_where)/select_n | solution.py:749
  3.6 5.0 %shard_map.87 = (f32[64,128]{1,0:T(8,128)}, f32[64,128]{1,0:T(8,128)}, f32[64,128]{1,0:T(8,128)}, f32[64,128]{1,0:T(8,128)}) custom-call(f32[128,128]{1,0:T(8,128)} %convert_select_fusion.wet_ref, f32[64,128,128]{2,1,0:T(8,128)} %bitcast.31), custom_call_target="tpu_custom_call" | custom-call | flops 2097152 | bytes 4194304 | tf_op jit(solution)/shard_map/pallas_call | solution.py:571
  8.5 0.0 copy-done.6
  8.6 0.3 fusion.8
  8.9 0.1 pad_maximum_fusion.coef_ref
  9.0 0.8 gather_fusion
  9.8 8.8 %fusion.contrib_ref = f32[256,8,128]{2,1,0:T(8,128)} fusion(bf16[1,1,1,256,128,128]{5,4,3,2,1,0:T(8,128)(2,1)} %param.10, bf16[256,8,128]{2,1,0:T(8,128)(2,1)S(1)} %gather_fusion, pred[256]{0:T(512)(128)(4,1)S(1)} %compare_and_fusion), kind=kOutput, calls=%fused_computation.1 | convolution fusion | flops 67371008 | bytes 9961728 | tf_op jit(solution)/shard_map/tji,kti->tkj/dot_general | solution.py:762
  18.7 4.7 %shard_map.86.buckets_ref = f32[64,9,8,128]{3,2,1,0:T(8,128)} custom-call(s32[256]{0:T(256)} %bitcast.39, s32[256]{0:T(256)} %bitcast.40, f32[256,8,128]{2,1,0:T(8,128)} %fusion.contrib_ref), custom_call_target="tpu_custom_call" | custom-call | tf_op jit(solution)/shard_map/pallas_call | solution.py:765
  23.3 0.0 copy-done.2
  23.4 0.0 copy-start
  23.4 1.7 %copy-done = f32[64,9,8,128]{3,2,1,0:T(8,128)S(1)} copy-done((f32[64,9,8,128]{3,2,1,0:T(8,128)S(1)}, f32[64,9,8,128]{3,2,1,0:T(8,128)}, u32[]{:S(2)}) %copy-start) | copy-done | bytes 2359320
  25.0 62.0 %shard_map.88 = (f32[64,128,128]{2,1,0:T(8,128)}, f32[64,9,8,128]{3,2,1,0:T(8,128)S(1)}) custom-call(f32[2]{0:T(128)S(1)} %pad_maximum_fusion.coef_ref, f32[128,128]{1,0:T(8,128)S(1)} %copy-done.1, f32[64,128,128]{2,1,0:T(8,128)} %bitcast.32, f32[64,128,128]{2,1,0:T(8,128)} %bitcast.33, f32[64,128,128]{2,1,0:T(8,128)} %bitcast.34, ...), custom_call_target="tpu_custom_call" | custom-call | flops 62914560 | bytes 12582912 | tf_op jit(solution)/shard_map/pallas_call | solution.py:305
  87.0 0.3 slice.9
  87.3 0.1 copy.19
  87.5 2.2 %fusion.4 = f32[8,128,128]{2,1,0:T(8,128)S(1)} fusion(f32[64,8,8,128]{3,2,1,0:T(8,128)S(1)} %slice.9, s32[64,8]{0,1:T(8,128)S(1)} %bitcast.37), kind=kOutput, calls=%fused_computation.5 | convolution fusion | flops 805371904 | bytes 2623488 | tf_op jit(solution)/shard_map/scr,sckj->krj/dot_general | solution.py:781
  89.6 0.1 collective-permute-start
  89.7 1.9 %collective-permute-done = f32[8,128,128]{2,1,0:T(8,128)S(1)} collective-permute-done((f32[8,128,128]{2,1,0:T(8,128)S(1)}, f32[8,128,128]{2,1,0:T(8,128)S(1)}, u32[]{:S(2)}, u32[]{:S(2)}) %collective-permute-start) | collective-permute-done | bytes 524320 | tf_op jit(solution)/shard_map/ppermute | solution.py:784
  91.6 0.6 slice_bitcast_fusion.f_ref
  92.2 1.5 %shard_map.89 = f32[64,128,128]{2,1,0:T(8,128)} custom-call(f32[64,128,128]{2,1,0:T(8,128)} %get-tuple-element.12.x_ref, f32[128,128]{1,0:T(8,128)} %convert_select_fusion.wet_ref, f32[128,128]{1,0:T(8,128)} %slice_bitcast_fusion.f_ref), custom_call_target="tpu_custom_call", output_to_operand_aliasing={{}: (0, {})} | custom-call | tf_op jit(solution)/shard_map/pallas_call | solution.py:592
  93.8 4.7 %copy.32 = f32[1,64,128,128]{3,2,1,0:T(8,128)} copy(f32[1,64,128,128]{3,2,1,0:T(8,128)} %bitcast.35) | data formatting | bytes 8388608
  98.5 0.8 copy.33
  (11 shorter events, 0.0 us)
Async XLA Ops:
  0.6 7.9 %copy-start.6 = (f32[1,8,128,128]{3,2,1,0:T(8,128)S(1)}, f32[1,8,128,128]{3,2,1,0:T(8,128)}, u32[]{:S(2)}) copy-start(f32[1,8,128,128]{3,2,1,0:T(8,128)} %param.8) | copy-start | bytes 1572868
  3.6 5.0 %copy-start.1 = (f32[128,128]{1,0:T(8,128)S(1)}, f32[128,128]{1,0:T(8,128)}, u32[]{:S(2)}) copy-start(f32[128,128]{1,0:T(8,128)} %convert_select_fusion.wet_ref) | copy-start | bytes 196612
  9.8 13.5 %copy-start.2 = (f32[64,128]{1,0:T(8,128)S(1)}, f32[64,128]{1,0:T(8,128)}, u32[]{:S(2)}) copy-start(f32[64,128]{1,0:T(8,128)} %get-tuple-element.8.e0n) | copy-start | bytes 98308
  9.8 13.5 %copy-start.3 = (f32[64,128]{1,0:T(8,128)S(1)}, f32[64,128]{1,0:T(8,128)}, u32[]{:S(2)}) copy-start(f32[64,128]{1,0:T(8,128)} %get-tuple-element.9.e0s) | copy-start | bytes 98308
  9.8 13.5 %copy-start.4 = (f32[64,128]{1,0:T(8,128)S(1)}, f32[64,128]{1,0:T(8,128)}, u32[]{:S(2)}) copy-start(f32[64,128]{1,0:T(8,128)} %get-tuple-element.10.e0w) | copy-start | bytes 98308
  9.8 13.5 %copy-start.5 = (f32[64,128]{1,0:T(8,128)S(1)}, f32[64,128]{1,0:T(8,128)}, u32[]{:S(2)}) copy-start(f32[64,128]{1,0:T(8,128)} %get-tuple-element.11.e0e) | copy-start | bytes 98308
  23.4 1.7 %copy-start = (f32[64,9,8,128]{3,2,1,0:T(8,128)S(1)}, f32[64,9,8,128]{3,2,1,0:T(8,128)}, u32[]{:S(2)}) copy-start(f32[64,9,8,128]{3,2,1,0:T(8,128)} %shard_map.86.buckets_ref) | copy-start | bytes 7077892
  89.6 2.0 %collective-permute-start = (f32[8,128,128]{2,1,0:T(8,128)S(1)}, f32[8,128,128]{2,1,0:T(8,128)S(1)}, u32[]{:S(2)}, u32[]{:S(2)}) collective-permute-start(f32[8,128,128]{2,1,0:T(8,128)S(1)} %fusion.4), channel_id=1, source_target_pairs={{0,64},{64,0},{1,65},{65,1},{2,66},{66,2},{3,67},{67,3},{4,68},{68... | collective-permute-start | bytes 1572872 | tf_op jit(solution)/shard_map/ppermute | solution.py:784

commit v19 on v18

--- a/solution.py
+++ b/solution.py
@@ -10,7 +10,7 @@
 CY = 128
 KF = 8
 CAP = 8
-LB = 16
+LB = 32
 EB = 32
 
 force_gain = 0.5

time: 99.9 us -> 99.9 us (level)
  no operation moved by 1% of the time
where the time goes in v19:
time: 99.9 us; the launch traced here: 99.2 us
  Pallas kernels  73.1 us (73%)
  matrix products  11 us (11%)
  local copies, waits for them, and re-layouts  9.03 us (9%)
  other arithmetic  3.35 us (3%)
  waiting for transfers between devices  1.9 us (2%)
    pallas_call x1, Pallas kernels, interval(): pl.pallas_call(interval_kernel, grid=(2, nblk), in_specs=in_specs, out_sp...  61.9 us
    dot_general x1, matrix products, local(): jnp.einsum('tji,kti->tkj', tile_weights[0, 0, 0], picked, preferred_eleme...  8.83 us
    unnamed x16, local copies, waits for them, and re-layouts  7.18 us
    pallas_call x1, Pallas kernels, masked_edges(): pl.pallas_call(edges_kernel, grid=(lev // EB,), in_specs=[full2((rows, co...  4.97 us
    pallas_call x1, Pallas kernels, local(): pl.pallas_call(bucket_kernel, in_specs=[pl.BlockSpec(memory_space=pltpu.S...  4.66 us
    dot_general x1, matrix products, local(): jnp.einsum('scr,sckj->krj', select, arrived[:, :CAP], precision=lax.Preci...  2.16 us
  transfers between devices with their start and end apart: 1, of which 1 were waited for; matrix products, arithmetic and copies ran while one was open for 0% of the time, Pallas kernels for 0%

profile of v19, /device:TPU:16, one launch (start us, length us, event | category | flops | bytes accessed | tf_op | source)
XLA Modules:
  0.0 99.2 jit_solution(1587128486457213763)
XLA Ops:
  0.6 0.0 copy-start.6
  0.7 0.7 compare_select_fusion
  1.4 0.7 compare_and_fusion
  2.1 1.5 %convert_select_fusion.wet_ref = f32[128,128]{1,0:T(8,128)} fusion(s32[128,128]{1,0:T(8,128)} %param.9, pred[]{:T(512)S(6)} %eq.8), kind=kLoop, calls=%fused_computation.17 | loop fusion | flops 32768 | bytes 131073 | tf_op jit(solution)/shard_map/jit(_where)/select_n | solution.py:749
  3.6 5.0 %shard_map.87 = (f32[64,128]{1,0:T(8,128)}, f32[64,128]{1,0:T(8,128)}, f32[64,128]{1,0:T(8,128)}, f32[64,128]{1,0:T(8,128)}) custom-call(f32[128,128]{1,0:T(8,128)} %convert_select_fusion.wet_ref, f32[64,128,128]{2,1,0:T(8,128)} %bitcast.31), custom_call_target="tpu_custom_call" | custom-call | flops 2097152 | bytes 4194304 | tf_op jit(solution)/shard_map/pallas_call | solution.py:571
  8.5 0.0 copy-done.6
  8.5 0.0 copy-done.1
  8.6 0.3 fusion.8
  8.9 0.1 pad_maximum_fusion.coef_ref
  9.0 0.8 gather_fusion
  9.8 8.8 %fusion.contrib_ref = f32[256,8,128]{2,1,0:T(8,128)} fusion(bf16[1,1,1,256,128,128]{5,4,3,2,1,0:T(8,128)(2,1)} %param.10, bf16[256,8,128]{2,1,0:T(8,128)(2,1)S(1)} %gather_fusion, pred[256]{0:T(512)(128)(4,1)S(1)} %compare_and_fusion), kind=kOutput, calls=%fused_computation.1 | convolution fusion | flops 67371008 | bytes 9961728 | tf_op jit(solution)/shard_map/tji,kti->tkj/dot_general | solution.py:762
  18.7 4.7 %shard_map.86.buckets_ref = f32[64,9,8,128]{3,2,1,0:T(8,128)} custom-call(s32[256]{0:T(256)} %bitcast.39, s32[256]{0:T(256)} %bitcast.40, f32[256,8,128]{2,1,0:T(8,128)} %fusion.contrib_ref), custom_call_target="tpu_custom_call" | custom-call | tf_op jit(solution)/shard_map/pallas_call | solution.py:765
  23.4 0.0 copy-start
  23.4 1.7 %copy-done = f32[64,9,8,128]{3,2,1,0:T(8,128)S(1)} copy-done((f32[64,9,8,128]{3,2,1,0:T(8,128)S(1)}, f32[64,9,8,128]{3,2,1,0:T(8,128)}, u32[]{:S(2)}) %copy-start) | copy-done | bytes 2359320
  25.0 61.9 %shard_map.88 = (f32[64,128,128]{2,1,0:T(8,128)}, f32[64,9,8,128]{3,2,1,0:T(8,128)S(1)}) custom-call(f32[2]{0:T(128)S(1)} %pad_maximum_fusion.coef_ref, f32[128,128]{1,0:T(8,128)S(1)} %copy-done.1, f32[64,128,128]{2,1,0:T(8,128)} %bitcast.32, f32[64,128,128]{2,1,0:T(8,128)} %bitcast.33, f32[64,128,128]{2,1,0:T(8,128)} %bitcast.34, ...), custom_call_target="tpu_custom_call" | custom-call | flops 62914560 | bytes 12582912 | tf_op jit(solution)/shard_map/pallas_call | solution.py:305
  87.0 0.3 slice.9
  87.3 0.1 copy.19
  87.4 2.2 %fusion.4 = f32[8,128,128]{2,1,0:T(8,128)S(1)} fusion(f32[64,8,8,128]{3,2,1,0:T(8,128)S(1)} %slice.9, s32[64,8]{0,1:T(8,128)S(1)} %bitcast.37), kind=kOutput, calls=%fused_computation.5 | convolution fusion | flops 805371904 | bytes 2623488 | tf_op jit(solution)/shard_map/scr,sckj->krj/dot_general | solution.py:781
  89.6 0.1 collective-permute-start
  89.7 1.9 %collective-permute-done = f32[8,128,128]{2,1,0:T(8,128)S(1)} collective-permute-done((f32[8,128,128]{2,1,0:T(8,128)S(1)}, f32[8,128,128]{2,1,0:T(8,128)S(1)}, u32[]{:S(2)}, u32[]{:S(2)}) %collective-permute-start) | collective-permute-done | bytes 524320 | tf_op jit(solution)/shard_map/ppermute | solution.py:784
  91.6 0.6 slice_bitcast_fusion.f_ref
  92.2 1.5 %shard_map.89 = f32[64,128,128]{2,1,0:T(8,128)} custom-call(f32[64,128,128]{2,1,0:T(8,128)} %get-tuple-element.12.x_ref, f32[128,128]{1,0:T(8,128)} %convert_select_fusion.wet_ref, f32[128,128]{1,0:T(8,128)} %slice_bitcast_fusion.f_ref), custom_call_target="tpu_custom_call", output_to_operand_aliasing={{}: (0, {})} | custom-call | tf_op jit(solution)/shard_map/pallas_call | solution.py:592
  93.7 4.7 %copy.32 = f32[1,64,128,128]{3,2,1,0:T(8,128)} copy(f32[1,64,128,128]{3,2,1,0:T(8,128)} %bitcast.35) | data formatting | bytes 8388608
  98.4 0.8 copy.33
  (11 shorter events, 0.0 us)
Async XLA Ops:
  0.6 7.9 %copy-start.6 = (f32[1,8,128,128]{3,2,1,0:T(8,128)S(1)}, f32[1,8,128,128]{3,2,1,0:T(8,128)}, u32[]{:S(2)}) copy-start(f32[1,8,128,128]{3,2,1,0:T(8,128)} %param.8) | copy-start | bytes 1572868
  3.6 5.0 %copy-start.1 = (f32[128,128]{1,0:T(8,128)S(1)}, f32[128,128]{1,0:T(8,128)}, u32[]{:S(2)}) copy-start(f32[128,128]{1,0:T(8,128)} %convert_select_fusion.wet_ref) | copy-start | bytes 196612
  9.8 13.5 %copy-start.2 = (f32[64,128]{1,0:T(8,128)S(1)}, f32[64,128]{1,0:T(8,128)}, u32[]{:S(2)}) copy-start(f32[64,128]{1,0:T(8,128)} %get-tuple-element.8.e0n) | copy-start | bytes 98308
  9.8 13.5 %copy-start.3 = (f32[64,128]{1,0:T(8,128)S(1)}, f32[64,128]{1,0:T(8,128)}, u32[]{:S(2)}) copy-start(f32[64,128]{1,0:T(8,128)} %get-tuple-element.9.e0s) | copy-start | bytes 98308
  9.8 13.5 %copy-start.4 = (f32[64,128]{1,0:T(8,128)S(1)}, f32[64,128]{1,0:T(8,128)}, u32[]{:S(2)}) copy-start(f32[64,128]{1,0:T(8,128)} %get-tuple-element.10.e0w) | copy-start | bytes 98308
  9.8 13.5 %copy-start.5 = (f32[64,128]{1,0:T(8,128)S(1)}, f32[64,128]{1,0:T(8,128)}, u32[]{:S(2)}) copy-start(f32[64,128]{1,0:T(8,128)} %get-tuple-element.11.e0e) | copy-start | bytes 98308
  23.4 1.7 %copy-start = (f32[64,9,8,128]{3,2,1,0:T(8,128)S(1)}, f32[64,9,8,128]{3,2,1,0:T(8,128)}, u32[]{:S(2)}) copy-start(f32[64,9,8,128]{3,2,1,0:T(8,128)} %shard_map.86.buckets_ref) | copy-start | bytes 7077892
  89.6 2.0 %collective-permute-start = (f32[8,128,128]{2,1,0:T(8,128)S(1)}, f32[8,128,128]{2,1,0:T(8,128)S(1)}, u32[]{:S(2)}, u32[]{:S(2)}) collective-permute-start(f32[8,128,128]{2,1,0:T(8,128)S(1)} %fusion.4), channel_id=1, source_target_pairs={{0,64},{64,0},{1,65},{65,1},{2,66},{66,2},{3,67},{67,3},{4,68},{68... | collective-permute-start | bytes 1572872 | tf_op jit(solution)/shard_map/ppermute | solution.py:784

commit v20 on v18

--- a/solution.py
+++ b/solution.py
@@ -738,7 +738,7 @@
         out_ref[d, CAP] = jnp.where(sub == c, row_ref[t].astype(jnp.float32), out_ref[d, CAP])
         return carry
 
-    lax.fori_loop(0, ntiles, body, 0, unroll=8)
+    lax.fori_loop(0, ntiles, body, 0, unroll=16)
 
 
 def local(states, surface, land_mask, tile_weights, tile_source, tile_target, tile_row):

time: 99.9 us -> 99.7 us (level)
  no operation moved by 1% of the time
where the time goes in v20:
time: 99.7 us; the launch traced here: 99 us
  Pallas kernels  72.9 us (73%)
  matrix products  11 us (11%)
  local copies, waits for them, and re-layouts  9.03 us (9%)
  other arithmetic  3.35 us (3%)
  waiting for transfers between devices  1.89 us (2%)
    pallas_call x1, Pallas kernels, interval(): pl.pallas_call(interval_kernel, grid=(2, nblk), in_specs=in_specs, out_sp...  61.9 us
    dot_general x1, matrix products, local(): jnp.einsum('tji,kti->tkj', tile_weights[0, 0, 0], picked, preferred_eleme...  8.83 us
    unnamed x16, local copies, waits for them, and re-layouts  7.18 us
    pallas_call x1, Pallas kernels, masked_edges(): pl.pallas_call(edges_kernel, grid=(lev // EB,), in_specs=[full2((rows, co...  4.97 us
    pallas_call x1, Pallas kernels, local(): pl.pallas_call(bucket_kernel, in_specs=[pl.BlockSpec(memory_space=pltpu.S...  4.51 us
    dot_general x1, matrix products, local(): jnp.einsum('scr,sckj->krj', select, arrived[:, :CAP], precision=lax.Preci...  2.15 us
  transfers between devices with their start and end apart: 1, of which 1 were waited for; matrix products, arithmetic and copies ran while one was open for 0% of the time, Pallas kernels for 0%

profile of v20, /device:TPU:16, one launch (start us, length us, event | category | flops | bytes accessed | tf_op | source)
XLA Modules:
  0.0 99.0 jit_solution(9652006037382718999)
XLA Ops:
  0.6 0.0 copy-start.6
  0.7 0.7 compare_select_fusion
  1.4 0.7 compare_and_fusion
  2.1 1.5 %convert_select_fusion.wet_ref = f32[128,128]{1,0:T(8,128)} fusion(s32[128,128]{1,0:T(8,128)} %param.9, pred[]{:T(512)S(6)} %eq.8), kind=kLoop, calls=%fused_computation.17 | loop fusion | flops 32768 | bytes 131073 | tf_op jit(solution)/shard_map/jit(_where)/select_n | solution.py:749
  3.6 5.0 %shard_map.87 = (f32[64,128]{1,0:T(8,128)}, f32[64,128]{1,0:T(8,128)}, f32[64,128]{1,0:T(8,128)}, f32[64,128]{1,0:T(8,128)}) custom-call(f32[128,128]{1,0:T(8,128)} %convert_select_fusion.wet_ref, f32[64,128,128]{2,1,0:T(8,128)} %bitcast.31), custom_call_target="tpu_custom_call" | custom-call | flops 2097152 | bytes 4194304 | tf_op jit(solution)/shard_map/pallas_call | solution.py:571
  8.6 0.3 fusion.8
  8.9 0.1 pad_maximum_fusion.coef_ref
  9.0 0.8 gather_fusion
  9.8 8.8 %fusion.contrib_ref = f32[256,8,128]{2,1,0:T(8,128)} fusion(bf16[1,1,1,256,128,128]{5,4,3,2,1,0:T(8,128)(2,1)} %param.10, bf16[256,8,128]{2,1,0:T(8,128)(2,1)S(1)} %gather_fusion, pred[256]{0:T(512)(128)(4,1)S(1)} %compare_and_fusion), kind=kOutput, calls=%fused_computation.1 | convolution fusion | flops 67371008 | bytes 9961728 | tf_op jit(solution)/shard_map/tji,kti->tkj/dot_general | solution.py:762
  18.7 4.5 %shard_map.86.buckets_ref = f32[64,9,8,128]{3,2,1,0:T(8,128)} custom-call(s32[256]{0:T(256)} %bitcast.39, s32[256]{0:T(256)} %bitcast.40, f32[256,8,128]{2,1,0:T(8,128)} %fusion.contrib_ref), custom_call_target="tpu_custom_call" | custom-call | tf_op jit(solution)/shard_map/pallas_call | solution.py:765
  23.2 0.0 copy-done.4
  23.2 0.0 copy-done.5
  23.2 0.0 copy-start
  23.2 1.7 %copy-done = f32[64,9,8,128]{3,2,1,0:T(8,128)S(1)} copy-done((f32[64,9,8,128]{3,2,1,0:T(8,128)S(1)}, f32[64,9,8,128]{3,2,1,0:T(8,128)}, u32[]{:S(2)}) %copy-start) | copy-done | bytes 2359320
  24.9 61.9 %shard_map.88 = (f32[64,128,128]{2,1,0:T(8,128)}, f32[64,9,8,128]{3,2,1,0:T(8,128)S(1)}) custom-call(f32[2]{0:T(128)S(1)} %pad_maximum_fusion.coef_ref, f32[128,128]{1,0:T(8,128)S(1)} %copy-done.1, f32[64,128,128]{2,1,0:T(8,128)} %bitcast.32, f32[64,128,128]{2,1,0:T(8,128)} %bitcast.33, f32[64,128,128]{2,1,0:T(8,128)} %bitcast.34, ...), custom_call_target="tpu_custom_call" | custom-call | flops 62914560 | bytes 12582912 | tf_op jit(solution)/shard_map/pallas_call | solution.py:305
  86.8 0.3 slice.9
  87.1 0.1 copy.19
  87.2 2.2 %fusion.4 = f32[8,128,128]{2,1,0:T(8,128)S(1)} fusion(f32[64,8,8,128]{3,2,1,0:T(8,128)S(1)} %slice.9, s32[64,8]{0,1:T(8,128)S(1)} %bitcast.37), kind=kOutput, calls=%fused_computation.5 | convolution fusion | flops 805371904 | bytes 2623488 | tf_op jit(solution)/shard_map/scr,sckj->krj/dot_general | solution.py:781
  89.4 0.1 collective-permute-start
  89.5 1.9 %collective-permute-done = f32[8,128,128]{2,1,0:T(8,128)S(1)} collective-permute-done((f32[8,128,128]{2,1,0:T(8,128)S(1)}, f32[8,128,128]{2,1,0:T(8,128)S(1)}, u32[]{:S(2)}, u32[]{:S(2)}) %collective-permute-start) | collective-permute-done | bytes 524320 | tf_op jit(solution)/shard_map/ppermute | solution.py:784
  91.4 0.6 slice_bitcast_fusion.f_ref
  92.0 1.5 %shard_map.89 = f32[64,128,128]{2,1,0:T(8,128)} custom-call(f32[64,128,128]{2,1,0:T(8,128)} %get-tuple-element.12.x_ref, f32[128,128]{1,0:T(8,128)} %convert_select_fusion.wet_ref, f32[128,128]{1,0:T(8,128)} %slice_bitcast_fusion.f_ref), custom_call_target="tpu_custom_call", output_to_operand_aliasing={{}: (0, {})} | custom-call | tf_op jit(solution)/shard_map/pallas_call | solution.py:592
  93.5 4.7 %copy.32 = f32[1,64,128,128]{3,2,1,0:T(8,128)} copy(f32[1,64,128,128]{3,2,1,0:T(8,128)} %bitcast.35) | data formatting | bytes 8388608
  98.2 0.8 copy.33
  (11 shorter events, 0.0 us)
Async XLA Ops:
  0.6 7.9 %copy-start.6 = (f32[1,8,128,128]{3,2,1,0:T(8,128)S(1)}, f32[1,8,128,128]{3,2,1,0:T(8,128)}, u32[]{:S(2)}) copy-start(f32[1,8,128,128]{3,2,1,0:T(8,128)} %param.8) | copy-start | bytes 1572868
  3.6 5.0 %copy-start.1 = (f32[128,128]{1,0:T(8,128)S(1)}, f32[128,128]{1,0:T(8,128)}, u32[]{:S(2)}) copy-start(f32[128,128]{1,0:T(8,128)} %convert_select_fusion.wet_ref) | copy-start | bytes 196612
  9.8 13.4 %copy-start.2 = (f32[64,128]{1,0:T(8,128)S(1)}, f32[64,128]{1,0:T(8,128)}, u32[]{:S(2)}) copy-start(f32[64,128]{1,0:T(8,128)} %get-tuple-element.8.e0n) | copy-start | bytes 98308
  9.8 13.4 %copy-start.3 = (f32[64,128]{1,0:T(8,128)S(1)}, f32[64,128]{1,0:T(8,128)}, u32[]{:S(2)}) copy-start(f32[64,128]{1,0:T(8,128)} %get-tuple-element.9.e0s) | copy-start | bytes 98308
  9.8 13.4 %copy-start.4 = (f32[64,128]{1,0:T(8,128)S(1)}, f32[64,128]{1,0:T(8,128)}, u32[]{:S(2)}) copy-start(f32[64,128]{1,0:T(8,128)} %get-tuple-element.10.e0w) | copy-start | bytes 98308
  9.8 13.4 %copy-start.5 = (f32[64,128]{1,0:T(8,128)S(1)}, f32[64,128]{1,0:T(8,128)}, u32[]{:S(2)}) copy-start(f32[64,128]{1,0:T(8,128)} %get-tuple-element.11.e0e) | copy-start | bytes 98308
  23.2 1.7 %copy-start = (f32[64,9,8,128]{3,2,1,0:T(8,128)S(1)}, f32[64,9,8,128]{3,2,1,0:T(8,128)}, u32[]{:S(2)}) copy-start(f32[64,9,8,128]{3,2,1,0:T(8,128)} %shard_map.86.buckets_ref) | copy-start | bytes 7077892
  89.4 2.0 %collective-permute-start = (f32[8,128,128]{2,1,0:T(8,128)S(1)}, f32[8,128,128]{2,1,0:T(8,128)S(1)}, u32[]{:S(2)}, u32[]{:S(2)}) collective-permute-start(f32[8,128,128]{2,1,0:T(8,128)S(1)} %fusion.4), channel_id=1, source_target_pairs={{0,64},{64,0},{1,65},{65,1},{2,66},{66,2},{3,67},{67,3},{4,68},{68... | collective-permute-start | bytes 1572872 | tf_op jit(solution)/shard_map/ppermute | solution.py:784
